TPU v7x, 256 devices: a whole 4x4x8 slice. The times are simulated.
256 devices in a mesh: ctx: 32 (over x_hi, z, core), tp: 8 (over x_lo, y).
Axes of the slice: x: 4 (x_hi: 2, x_lo: 2; x = x_hi * 2 + x_lo), y: 4, z: 8, core: 2. Of those that a mesh axis runs over, the one named last changes fastest.
Arguments:
- queries: bfloat16 [64, 3, 128, 128], P('ctx', None, 'tp'), may hold values from -480 to 480
- prefix_keys: bfloat16 [65536, 8, 128], P('ctx', 'tp'), may hold values from -6 to 6
- prefix_values: bfloat16 [65536, 8, 128], P('ctx', 'tp'), may hold values from -6 to 6
- suffix_keys: bfloat16 [64, 512, 8, 128], P('ctx', None, 'tp'), may hold values from -6 to 6
- suffix_values: bfloat16 [64, 512, 8, 128], P('ctx', None, 'tp'), may hold values from -6 to 6
- fork_lengths: int32 [64], P('ctx'), may hold values from 1 to 509, 16384 in all
- out_weight: bfloat16 [16384, 16384], P('tp', 'ctx'), may hold values from -0.046875 to 0.046875
Outputs:
- projected: bfloat16 [64, 3, 16384], P('tp', None, 'ctx')
Inputs may be any that keep to these rules, and one draw needn't show every extreme that they name: `fork_lengths`: A fork's earlier tokens fill the first slots of its suffix, followed by the keys and values of its 3 new tokens.
All inputs are finite; a program needn't handle non-finite values. No bound on the sum of `fork_lengths` on one device may be relied on, other than what follows from the above.
Results may differ from a plain program's by a relative error of at most 0.014.
Values may be sent and summed in bfloat16 or wider, within the bound.
No kernel may reach another device: no remote copies, remote signals or barrier semaphores. Data moves between devices by JAX's collectives and lax.ppermute only.
A program may use at most 64 MiB of HBM per device.

v0:
```python
import math

import jax
import jax.numpy as jnp
from jax import lax
from jax.sharding import PartitionSpec as P


def copy_for_each(value, axis):
    size = lax.axis_size(axis)
    return lax.all_to_all(
        jnp.broadcast_to(value[None], (size, *value.shape)), axis, 0, 0, tiled=True
    )


def in_order(blocks, dim):
    blocks = jnp.moveaxis(blocks, 0, dim)
    lengths = blocks.shape
    return blocks.reshape(*lengths[:dim], lengths[dim] * lengths[dim + 1], *lengths[dim + 2 :])


def gather_directly(value, axis, dim):
    blocks = copy_for_each(value, axis)
    return in_order(blocks, dim)


def split_up(value, dim, size):
    before, after = (value.shape[:dim], value.shape[dim + 1 :])
    return jnp.moveaxis(value.reshape(*before, size, -1, *after), dim, 0)


def sent_and_summed(value, axis, dim):
    blocks = split_up(value, dim, lax.axis_size(axis))
    arrived = lax.all_to_all(blocks, axis, split_axis=0, concat_axis=0, tiled=True)
    return arrived.astype(jnp.float32).sum(axis=0)


def combine(first, second):
    mixed_a, highest_a, totals_a = first
    mixed_b, highest_b, totals_b = second
    summit = jnp.maximum(highest_a, highest_b)
    factor_a = jnp.exp(highest_a - summit)
    factor_b = jnp.exp(highest_b - summit)
    mixed = mixed_a * factor_a[..., None] + mixed_b * factor_b[..., None]
    return (mixed, summit, totals_a * factor_a + totals_b * factor_b)


def softmax_state(scores, values, form, shape):
    highest = jnp.max(scores, axis=-1)
    weights = jnp.exp(scores - highest[..., None])
    totals = jnp.sum(weights, axis=-1)
    mixed = jnp.einsum(
        form, weights.astype(jnp.bfloat16), values, preferred_element_type=jnp.float32
    )
    return (mixed.reshape(shape), highest.reshape(shape[:3]), totals.reshape(shape[:3]))


def shards(
    queries, prefix_keys, prefix_values, suffix_keys, suffix_values, fork_lengths, out_weight
):
    own_forks, steps, heads_local, head_size = queries.shape
    kv_local = prefix_keys.shape[1]
    group = heads_local // kv_local
    slots = suffix_keys.shape[1]
    scale = head_size ** (-0.5)
    every_query = gather_directly(queries, "ctx", 0)
    all_forks = every_query.shape[0]
    width = math.gcd(all_forks, 16)
    blocks = all_forks // width

    def prefix_block(block_queries):
        grouped = block_queries.reshape(width, steps, kv_local, group, head_size)
        scores = (
            jnp.einsum("bskgd,pkd->bskgp", grouped, prefix_keys, preferred_element_type=jnp.float32)
            * scale
        )
        return softmax_state(scores, prefix_values, "bskgp,pkd->bskgd", block_queries.shape)

    stacked = lax.map(
        prefix_block, every_query.reshape(blocks, width, steps, heads_local, head_size)
    )
    prefix_state = (
        stacked[0].reshape(all_forks, steps, heads_local, head_size),
        stacked[1].reshape(all_forks, steps, heads_local),
        stacked[2].reshape(all_forks, steps, heads_local),
    )
    grouped = queries.reshape(own_forks, steps, kv_local, group, head_size)
    scores = (
        jnp.einsum("bskgd,bpkd->bskgp", grouped, suffix_keys, preferred_element_type=jnp.float32)
        * scale
    )
    limit = fork_lengths[:, None] + jnp.arange(steps, dtype=jnp.int32)[None, :] + 1
    visible = jnp.arange(slots, dtype=jnp.int32)[None, None, :] < limit[:, :, None]
    scores = jnp.where(visible[:, :, None, None, :], scores, jnp.float32(-1e30))
    own_state = softmax_state(scores, suffix_values, "bskgp,bpkd->bskgd", queries.shape)
    received = lax.all_to_all(
        tuple((piece[None] for piece in prefix_state)),
        "ctx",
        split_axis=1,
        concat_axis=0,
        tiled=True,
    )
    summit = jnp.max(received[1], axis=0)
    factors = jnp.exp(received[1] - summit[None])
    gathered_mixed = jnp.sum(received[0] * factors[..., None], axis=0)
    gathered_totals = jnp.sum(received[2] * factors, axis=0)
    mixed, highest, totals = combine((gathered_mixed, summit, gathered_totals), own_state)
    own_attention = (
        (mixed / totals[..., None])
        .astype(jnp.bfloat16)
        .reshape(own_forks, steps, heads_local * head_size)
    )
    attention = gather_directly(own_attention, "ctx", 0)
    product = jnp.dot(
        attention.reshape(
            all_forks // lax.axis_size("tp") * lax.axis_size("tp") * steps, heads_local * head_size
        ),
        out_weight,
        preferred_element_type=jnp.float32,
    )
    projected = sent_and_summed(
        product.reshape(
            all_forks // lax.axis_size("tp") * lax.axis_size("tp"), steps, out_weight.shape[1]
        ).astype(jnp.bfloat16),
        "tp",
        0,
    )
    return projected.astype(jnp.bfloat16)


def solution(mesh):
    return jax.shard_map(
        shards,
        mesh=mesh,
        in_specs=(
            P("ctx", None, "tp", None),
            P("ctx", "tp", None),
            P("ctx", "tp", None),
            P("ctx", None, "tp", None),
            P("ctx", None, "tp", None),
            P("ctx"),
            P("tp", "ctx"),
        ),
        out_specs=P("tp", None, "ctx"),
        check_vma=False,
    )
```

profile of v0, /device:TPU:1, one launch (start us, length us, event | category | flops | bytes accessed | tf_op | source)
XLA Modules:
  0.0 181.6 jit_solution(7770636676601895800)
XLA Ops:
  0.0 1.9 %broadcast_in_dim.31 = bf16[32,2,3,16,128]{4,3,2,1,0:T(8,128)(2,1)} broadcast(bf16[2,3,16,128]{3,2,1,0:T(8,128)(2,1)} %param.9), dimensions={1,2,3,4} | broadcast | bytes 811008 | tf_op jit(solution)/shard_map/broadcast_in_dim | solution.py:12
  1.9 12.6 %all-to-all-start = ((bf16[32,2,3,16,128]{4,3,2,1,0:T(8,128)(2,1)}), bf16[32,2,3,16,128]{4,3,2,1,0:T(8,128)(2,1)S(1)}, u32[]{:S(2)}, u32[]{:S(2)}) async-start(bf16[32,2,3,16,128]{4,3,2,1,0:T(8,128)(2,1)} %broadcast_in_dim.31), calls=%async_computation | async-start | bytes 1572864 | tf_op jit(solution)/shard_map/all_to_all | solution.py:11
  14.5 22.8 %all-to-all-done = bf16[32,2,3,16,128]{4,3,2,1,0:T(8,128)(2,1)S(1)} async-done(((bf16[32,2,3,16,128]{4,3,2,1,0:T(8,128)(2,1)}), bf16[32,2,3,16,128]{4,3,2,1,0:T(8,128)(2,1)S(1)}, u32[]{:S(2)}, u32[]{:S(2)}) %all-to-all-start) | async-done | bytes 786464 | tf_op jit(solution)/shard_map/all_to_all | solution.py:11
  37.2 23.5 %while.14 = (s32[]{:T(128)}, f32[4,16,3,16,128]{4,3,2,1,0:T(8,128)}, f32[4,16,3,16]{3,2,1,0:T(4,128)S(1)}, f32[4,16,3,16]{3,2,1,0:T(4,128)}, bf16[4,16,3,16,128]...) while((s32[]{:T(128)}, ...), condition=%wide.region_3.4_spmd, body=%wide.region_0.3_spmd.sunk | while | flops 817887744 | bytes 22754420 | solution.py:79
  37.3 2.2 %bitcast_reduce_fusion.2 = (f32[16,3,16]{2,1,0:T(4,128)S(1)}, f32[16,3,16,2048]{3,2,1,0:T(8,128)S(1)}) fusion(bf16[2048,1,128]{2,0,1:T(8,128)(2,1)} %get-tuple-element.165, bf16[4,16,3,16,128]{4,3,2,1,0:T(8,128)(2,1)S(1)} %get-tuple-element.164, s32[]{:T(128)} %get-tuple-element.152), kind=kOutput, calls=%fused_computation.1.clone.1 | convolution fusion | flops 405798144 | bytes 7015428 | tf_op jit(solution)/shard_map/while/body/eval_jaxpr/bskgd,pkd->bskgp/dot_general | solution.py:74
  39.5 1.2 fusion.52
  40.6 0.6 bitcast_dynamic-update-slice_fusion.3
  41.3 0.0 copy-done.1
  41.3 1.9 %fusion.51 = f32[4,16,3,16,128]{4,3,2,1,0:T(8,128)} fusion(f32[4,16,3,16,128]{4,3,2,1,0:T(8,128)} %get-tuple-element.153, s32[]{:T(128)} %get-tuple-element.152, f32[16,3,16,2048]{3,2,1,0:T(8,128)S(1)} %get-tuple-element.140, f32[16,3,16]{2,1,0:T(4,128)S(1)} %get-tuple-element.141, bf16[2048,1,128]{2,0,1:T(8,128)(2,1)S(1)} %copy-done.1), kind=kOutput, calls=%fused_computation.8.clone.1 | convolution fusion | flops 407371776 | bytes 7212544 | tf_op jit(solution)/shard_map/while/body/eval_jaxpr/bskgp,pkd->bskgd/dot_general | solution.py:52
  43.1 2.2 %bitcast_reduce_fusion.2 = (f32[16,3,16]{2,1,0:T(4,128)S(1)}, f32[16,3,16,2048]{3,2,1,0:T(8,128)S(1)}) fusion(bf16[2048,1,128]{2,0,1:T(8,128)(2,1)} %get-tuple-element.165, bf16[4,16,3,16,128]{4,3,2,1,0:T(8,128)(2,1)S(1)} %get-tuple-element.164, s32[]{:T(128)} %get-tuple-element.152), kind=kOutput, calls=%fused_computation.1.clone.1 | convolution fusion | flops 405798144 | bytes 7015428 | tf_op jit(solution)/shard_map/while/body/eval_jaxpr/bskgd,pkd->bskgp/dot_general | solution.py:74
  45.3 1.2 fusion.52
  46.5 0.6 bitcast_dynamic-update-slice_fusion.3
  47.1 1.9 %fusion.51 = f32[4,16,3,16,128]{4,3,2,1,0:T(8,128)} fusion(f32[4,16,3,16,128]{4,3,2,1,0:T(8,128)} %get-tuple-element.153, s32[]{:T(128)} %get-tuple-element.152, f32[16,3,16,2048]{3,2,1,0:T(8,128)S(1)} %get-tuple-element.140, f32[16,3,16]{2,1,0:T(4,128)S(1)} %get-tuple-element.141, bf16[2048,1,128]{2,0,1:T(8,128)(2,1)S(1)} %copy-done.1), kind=kOutput, calls=%fused_computation.8.clone.1 | convolution fusion | flops 407371776 | bytes 7212544 | tf_op jit(solution)/shard_map/while/body/eval_jaxpr/bskgp,pkd->bskgd/dot_general | solution.py:52
  49.0 2.2 %bitcast_reduce_fusion.2 = (f32[16,3,16]{2,1,0:T(4,128)S(1)}, f32[16,3,16,2048]{3,2,1,0:T(8,128)S(1)}) fusion(bf16[2048,1,128]{2,0,1:T(8,128)(2,1)} %get-tuple-element.165, bf16[4,16,3,16,128]{4,3,2,1,0:T(8,128)(2,1)S(1)} %get-tuple-element.164, s32[]{:T(128)} %get-tuple-element.152), kind=kOutput, calls=%fused_computation.1.clone.1 | convolution fusion | flops 405798144 | bytes 7015428 | tf_op jit(solution)/shard_map/while/body/eval_jaxpr/bskgd,pkd->bskgp/dot_general | solution.py:74
  51.2 1.2 fusion.52
  52.4 0.6 bitcast_dynamic-update-slice_fusion.3
  53.0 1.9 %fusion.51 = f32[4,16,3,16,128]{4,3,2,1,0:T(8,128)} fusion(f32[4,16,3,16,128]{4,3,2,1,0:T(8,128)} %get-tuple-element.153, s32[]{:T(128)} %get-tuple-element.152, f32[16,3,16,2048]{3,2,1,0:T(8,128)S(1)} %get-tuple-element.140, f32[16,3,16]{2,1,0:T(4,128)S(1)} %get-tuple-element.141, bf16[2048,1,128]{2,0,1:T(8,128)(2,1)S(1)} %copy-done.1), kind=kOutput, calls=%fused_computation.8.clone.1 | convolution fusion | flops 407371776 | bytes 7212544 | tf_op jit(solution)/shard_map/while/body/eval_jaxpr/bskgp,pkd->bskgd/dot_general | solution.py:52
  54.9 2.2 %bitcast_reduce_fusion.2 = (f32[16,3,16]{2,1,0:T(4,128)S(1)}, f32[16,3,16,2048]{3,2,1,0:T(8,128)S(1)}) fusion(bf16[2048,1,128]{2,0,1:T(8,128)(2,1)} %get-tuple-element.165, bf16[4,16,3,16,128]{4,3,2,1,0:T(8,128)(2,1)S(1)} %get-tuple-element.164, s32[]{:T(128)} %get-tuple-element.152), kind=kOutput, calls=%fused_computation.1.clone.1 | convolution fusion | flops 405798144 | bytes 7015428 | tf_op jit(solution)/shard_map/while/body/eval_jaxpr/bskgd,pkd->bskgp/dot_general | solution.py:74
  57.0 1.2 fusion.52
  58.2 0.6 bitcast_dynamic-update-slice_fusion.3
  58.9 1.9 %fusion.51 = f32[4,16,3,16,128]{4,3,2,1,0:T(8,128)} fusion(f32[4,16,3,16,128]{4,3,2,1,0:T(8,128)} %get-tuple-element.153, s32[]{:T(128)} %get-tuple-element.152, f32[16,3,16,2048]{3,2,1,0:T(8,128)S(1)} %get-tuple-element.140, f32[16,3,16]{2,1,0:T(4,128)S(1)} %get-tuple-element.141, bf16[2048,1,128]{2,0,1:T(8,128)(2,1)S(1)} %copy-done.1), kind=kOutput, calls=%fused_computation.8.clone.1 | convolution fusion | flops 407371776 | bytes 7212544 | tf_op jit(solution)/shard_map/while/body/eval_jaxpr/bskgp,pkd->bskgd/dot_general | solution.py:52
  60.8 0.7 copy.54
  61.5 5.7 %all-to-all-start.2 = ((f32[1,64,3,16]{3,0,2,1:T(1,128)}), f32[1,64,3,16]{3,0,2,1:T(1,128)S(1)}, u32[]{:S(2)}, u32[]{:S(2)}) async-start(f32[1,64,3,16]{3,0,2,1:T(1,128)} %copy.54), calls=%async_computation.2 | async-start | bytes 196608 | tf_op jit(solution)/shard_map/all_to_all | solution.py:96
  67.2 1.0 copy.63
  68.3 9.0 %all-to-all-done.2 = f32[1,64,3,16]{3,0,2,1:T(1,128)S(1)} async-done(((f32[1,64,3,16]{3,0,2,1:T(1,128)}), f32[1,64,3,16]{3,0,2,1:T(1,128)S(1)}, u32[]{:S(2)}, u32[]{:S(2)}) %all-to-all-start.2) | async-done | bytes 12320 | tf_op jit(solution)/shard_map/all_to_all | solution.py:96
  77.2 14.2 %all_to_all.51 = f32[1,64,3,16]{3,0,2,1:T(1,128)S(1)} all-to-all(f32[1,64,3,16]{3,0,2,1:T(1,128)S(1)} %copy.63), channel_id=1, replica_groups=mesh['ctx'=32,'tp'=8] {'ctx'}, dimensions={1} | all-to-all | bytes 24576 | tf_op jit(solution)/shard_map/all_to_all | solution.py:96
  91.4 5.9 %all-to-all-start.1 = ((f32[1,64,3,16,128]{4,3,2,0,1:T(8,128)}), f32[1,64,3,16,128]{4,3,2,0,1:T(8,128)}, u32[]{:S(2)}, u32[]{:S(2)}) async-start(f32[1,64,3,16,128]{4,3,2,0,1:T(8,128)} %bitcast.20), calls=%async_computation.1 | async-start | bytes 3145728 | tf_op jit(solution)/shard_map/all_to_all | solution.py:96
  97.3 0.1 add_add_fusion
  97.4 0.1 iota_compare_fusion
  97.5 1.0 fusion.42
  98.5 0.2 convolution_bitcast_fusion
  98.8 0.2 fusion.31
  99.0 0.1 reduce_max.27
  99.1 0.1 multiply_reduce_fusion.1
  99.2 0.1 copy.56
  99.3 0.1 div.14
  99.4 0.1 mul.93
  99.5 37.7 %all-to-all-done.1 = f32[1,64,3,16,128]{4,3,2,0,1:T(8,128)} async-done(((f32[1,64,3,16,128]{4,3,2,0,1:T(8,128)}), f32[1,64,3,16,128]{4,3,2,0,1:T(8,128)}, u32[]{:S(2)}, u32[]{:S(2)}) %all-to-all-start.1) | async-done | bytes 1572896 | tf_op jit(solution)/shard_map/all_to_all | solution.py:96
  137.2 1.9 %multiply_reduce_fusion = f32[2,3,16,128]{3,2,1,0:T(8,128)S(1)} fusion(f32[32,2,3,16,128]{4,3,2,1,0:T(8,128)} %bitcast.21, f32[32,2,3,16]{3,2,1,0:T(4,128)S(1)} %copy.56), kind=kLoop, calls=%fused_computation.20 | loop fusion | flops 774144 | bytes 1634304 | tf_op jit(solution)/shard_map/reduce_sum | solution.py:105
  139.1 0.1 broadcast_multiply_fusion
  139.2 0.1 fusion.36
  139.3 0.4 broadcast_in_dim.53
  139.7 28.0 %all_to_all.52 = bf16[32,2,3,2048]{3,1,2,0:T(2,128)(2,1)S(1)} all-to-all(bf16[32,2,3,2048]{3,1,2,0:T(2,128)(2,1)S(1)} %broadcast_in_dim.53), channel_id=1, replica_groups=mesh['ctx'=32,'tp'=8] {'ctx'}, dimensions={0} | all-to-all | bytes 1572864 | tf_op jit(solution)/shard_map/all_to_all | solution.py:11
  167.7 0.5 copy.66
  168.3 1.2 dot_general.29
  169.4 1.7 fusion.24
  171.2 9.8 %all_to_all.53 = bf16[8,8,3,512]{3,1,2,0:T(8,128)(2,1)S(1)} all-to-all(bf16[8,8,3,512]{3,1,2,0:T(8,128)(2,1)S(1)} %copy.67), channel_id=1, replica_groups=mesh['ctx'=32,'tp'=8] {'tp'}, dimensions={0} | all-to-all | bytes 393216 | tf_op jit(solution)/shard_map/all_to_all | solution.py:34
  181.0 0.6 reduce_sum.51
  (29 shorter events, 0.2 us)
Async XLA Ops:
  0.0 169.4 %copy-start = (bf16[2048,512]{1,0:T(8,128)(2,1)S(1)}, bf16[2048,512]{1,0:T(8,128)(2,1)}, u32[]{:S(2)}) copy-start(bf16[2048,512]{1,0:T(8,128)(2,1)} %param.15) | copy-start | bytes 6291460
  1.9 35.4 %all-to-all-start = ((bf16[32,2,3,16,128]{4,3,2,1,0:T(8,128)(2,1)}), bf16[32,2,3,16,128]{4,3,2,1,0:T(8,128)(2,1)S(1)}, u32[]{:S(2)}, u32[]{:S(2)}) async-start(bf16[32,2,3,16,128]{4,3,2,1,0:T(8,128)(2,1)} %broadcast_in_dim.31), calls=%async_computation | async-start | bytes 1572864 | tf_op jit(solution)/shard_map/all_to_all | solution.py:11
  37.2 60.1 %copy-start.4 = (s32[2]{0:T(128)S(1)}, s32[2]{0:T(128)}, u32[]{:S(2)}) copy-start(s32[2]{0:T(128)} %param.14) | copy-start | bytes 28
  37.2 60.2 %copy-start.3 = (bf16[2,512,1,128]{3,1,2,0:T(8,128)(2,1)S(1)}, bf16[2,512,1,128]{3,1,2,0:T(8,128)(2,1)}, u32[]{:S(2)}) copy-start(bf16[2,512,1,128]{3,1,2,0:T(8,128)(2,1)} %param.12) | copy-start | bytes 786436
  37.2 61.3 %copy-start.2 = (bf16[2,512,1,128]{3,1,2,0:T(8,128)(2,1)S(1)}, bf16[2,512,1,128]{3,1,2,0:T(8,128)(2,1)}, u32[]{:S(2)}) copy-start(bf16[2,512,1,128]{3,1,2,0:T(8,128)(2,1)} %param.13) | copy-start | bytes 786436
  37.2 4.0 %copy-start.1 = (bf16[2048,1,128]{2,0,1:T(8,128)(2,1)S(1)}, bf16[2048,1,128]{2,0,1:T(8,128)(2,1)}, u32[]{:S(2)}) copy-start(bf16[2048,1,128]{2,0,1:T(8,128)(2,1)} %get-tuple-element.166) | copy-start | bytes 1572868 | tf_op jit(solution)/shard_map/while
  43.1 4.0 %copy-start.1 = (bf16[2048,1,128]{2,0,1:T(8,128)(2,1)S(1)}, bf16[2048,1,128]{2,0,1:T(8,128)(2,1)}, u32[]{:S(2)}) copy-start(bf16[2048,1,128]{2,0,1:T(8,128)(2,1)} %get-tuple-element.166) | copy-start | bytes 1572868 | tf_op jit(solution)/shard_map/while
  49.0 4.0 %copy-start.1 = (bf16[2048,1,128]{2,0,1:T(8,128)(2,1)S(1)}, bf16[2048,1,128]{2,0,1:T(8,128)(2,1)}, u32[]{:S(2)}) copy-start(bf16[2048,1,128]{2,0,1:T(8,128)(2,1)} %get-tuple-element.166) | copy-start | bytes 1572868 | tf_op jit(solution)/shard_map/while
  54.9 4.0 %copy-start.1 = (bf16[2048,1,128]{2,0,1:T(8,128)(2,1)S(1)}, bf16[2048,1,128]{2,0,1:T(8,128)(2,1)}, u32[]{:S(2)}) copy-start(bf16[2048,1,128]{2,0,1:T(8,128)(2,1)} %get-tuple-element.166) | copy-start | bytes 1572868 | tf_op jit(solution)/shard_map/while
  61.5 15.7 %all-to-all-start.2 = ((f32[1,64,3,16]{3,0,2,1:T(1,128)}), f32[1,64,3,16]{3,0,2,1:T(1,128)S(1)}, u32[]{:S(2)}, u32[]{:S(2)}) async-start(f32[1,64,3,16]{3,0,2,1:T(1,128)} %copy.54), calls=%async_computation.2 | async-start | bytes 196608 | tf_op jit(solution)/shard_map/all_to_all | solution.py:96
  91.4 45.8 %all-to-all-start.1 = ((f32[1,64,3,16,128]{4,3,2,0,1:T(8,128)}), f32[1,64,3,16,128]{4,3,2,0,1:T(8,128)}, u32[]{:S(2)}, u32[]{:S(2)}) async-start(f32[1,64,3,16,128]{4,3,2,0,1:T(8,128)} %bitcast.20), calls=%async_computation.1 | async-start | bytes 3145728 | tf_op jit(solution)/shard_map/all_to_all | solution.py:96
where the time goes:
time: 184 us; the launch traced here: 182 us
  waiting for transfers between devices  69.4 us (38%)
  blocking collectives  52 us (28%)
  starting transfers between devices  24.2 us (13%)
  matrix products  19.2 us (10%)
  local copies, waits for them, and re-layouts  8.62 us (5%)
  other arithmetic  7.9 us (4%)
    all_to_all x2, waiting for transfers between devices, shards(): lax.all_to_all(tuple((piece[None] for piece in prefix_state)), 'ctx', spl...  46.6 us
    all_to_all x1, blocking collectives, copy_for_each(): lax.all_to_all(jnp.broadcast_to(value[None], (size, *value.shape)), axis,...  28 us
    all_to_all x1, waiting for transfers between devices, copy_for_each(): lax.all_to_all(jnp.broadcast_to(value[None], (size, *value.shape)), axis,...  22.8 us
    all_to_all x1, blocking collectives, shards(): lax.all_to_all(tuple((piece[None] for piece in prefix_state)), 'ctx', spl...  14.2 us
    all_to_all x1, starting transfers between devices, copy_for_each(): lax.all_to_all(jnp.broadcast_to(value[None], (size, *value.shape)), axis,...  12.6 us
    all_to_all x2, starting transfers between devices, shards(): lax.all_to_all(tuple((piece[None] for piece in prefix_state)), 'ctx', spl...  11.7 us
    all_to_all x1, blocking collectives, sent_and_summed(): lax.all_to_all(blocks, axis, split_axis=0, concat_axis=0, tiled=True)  9.8 us
    dot_general x4, matrix products, prefix_block(): jnp.einsum('bskgd,pkd->bskgp', grouped, prefix_keys, preferred_element_ty...  8.68 us
  transfers between devices with their start and end apart: 3, of which 3 were waited for; matrix products, arithmetic and copies ran while one was open for 2% of the time, Pallas kernels for 0%

commit v1 on v0

v1 whole, which is shorter than its diff:
```python
import functools

import jax
import jax.numpy as jnp
from jax import lax
from jax.experimental import pallas as pl
from jax.experimental.pallas import tpu as pltpu
from jax.sharding import Mesh
from jax.sharding import PartitionSpec as P

CTX = ("xh", "z", "core")
CHIPS = ("xh", "z")
TP = ("xl", "y")
STATS = 8
NEG = -1e30
LOG2E = 1.4426950408889634
VMEM = pltpu.VMEM


def dot(a, b, ca, cb):
    return lax.dot_general(
        a, b, (((ca,), (cb,)), ((), ())), preferred_element_type=jnp.float32
    )


def shift_of(scores_max):
    hi = scores_max.astype(jnp.bfloat16)
    lo = (scores_max - hi.astype(jnp.float32)).astype(jnp.bfloat16)
    return hi, lo, hi.astype(jnp.float32) + lo.astype(jnp.float32)


def stat_rows(hi, lo, totals):
    rows = hi.shape[0]
    t_hi = totals.astype(jnp.bfloat16)
    t_lo = (totals - t_hi.astype(jnp.float32)).astype(jnp.bfloat16)
    lane = lax.broadcasted_iota(jnp.int32, (rows, 128), 1)
    f = jnp.float32
    table = jnp.where(
        lane == 0,
        hi.astype(f),
        jnp.where(
            lane == 1,
            lo.astype(f),
            jnp.where(lane == 2, t_hi.astype(f), jnp.where(lane == 3, t_lo.astype(f), 0.0)),
        ),
    ).astype(jnp.bfloat16)
    if rows < 128:
        table = jnp.concatenate([table, jnp.zeros((128 - rows, 128), jnp.bfloat16)], axis=0)
    pick = (
        lax.broadcasted_iota(jnp.int32, (STATS, 128), 0)
        == lax.broadcasted_iota(jnp.int32, (STATS, 128), 1)
    ).astype(jnp.bfloat16)
    return dot(pick, table, 1, 1).astype(jnp.bfloat16)


def prefix_kernel(c, q_ref, ko_ref, kp_ref, vo_ref, vp_ref, out_ref, v_ref):
    n_seg, rows, hd = q_ref.shape
    keys = ko_ref.shape[0]

    @pl.when(pl.program_id(0) == 0)
    def _():
        v_ref[:keys, :hd] = vo_ref[...]
        v_ref[keys:, :hd] = vp_ref[...]
        v_ref[:, hd:] = jnp.ones((2 * keys, hd), jnp.bfloat16)

    q = q_ref[...].reshape(n_seg * rows, hd)
    s1 = dot(q, ko_ref[...], 1, 1)
    s2 = dot(q, kp_ref[...], 1, 1)
    top = jnp.maximum(
        jnp.max(s1, axis=1, keepdims=True), jnp.max(s2, axis=1, keepdims=True)
    )
    hi, lo, shift = shift_of(top)
    p1 = jnp.exp2((s1 - shift) * c).astype(jnp.bfloat16)
    p2 = jnp.exp2((s2 - shift) * c).astype(jnp.bfloat16)
    o = dot(p1, v_ref[:keys], 1, 0) + dot(p2, v_ref[keys:], 1, 0)
    mixed = o[:, :hd].astype(jnp.bfloat16)
    totals = o[:, hd : hd + 1]
    for i in range(n_seg):
        r = slice(i * rows, (i + 1) * rows)
        out_ref[i, :rows, :] = mixed[r]
        out_ref[i, rows:, :] = stat_rows(hi[r], lo[r], totals[r])


def suffix_kernel(c, heads, len_ref, q_ref, k_ref, v_ref, out_ref):
    forks, slots, hd = k_ref.shape
    rows = q_ref.shape[0] // forks
    his, los, tots = [], [], []
    for f in range(forks):
        q = q_ref[f * rows : (f + 1) * rows, :]
        s = dot(q, k_ref[f], 1, 1)
        step = lax.broadcasted_iota(jnp.int32, (rows, slots), 0) // heads
        slot = lax.broadcasted_iota(jnp.int32, (rows, slots), 1)
        s = jnp.where(slot < len_ref[f] + step + 1, s, NEG)
        hi, lo, shift = shift_of(jnp.max(s, axis=1, keepdims=True))
        p = jnp.exp2((s - shift) * c)
        out_ref[f * rows : (f + 1) * rows, :] = dot(
            p.astype(jnp.bfloat16), v_ref[f], 1, 0
        ).astype(jnp.bfloat16)
        his.append(hi)
        los.append(lo)
        tots.append(jnp.sum(p, axis=1, keepdims=True))
    cat = functools.partial(jnp.concatenate, axis=0)
    out_ref[forks * rows :, :] = stat_rows(cat(his), cat(los), cat(tots))


def combine_kernel(c, got_ref, own_ref, out_ref):
    n = got_ref.shape[0]
    rows = own_ref.shape[0] - STATS
    f = jnp.float32
    m = got_ref[:, rows, :].astype(f) + got_ref[:, rows + 1, :].astype(f)
    t = got_ref[:, rows + 2, :].astype(f) + got_ref[:, rows + 3, :].astype(f)
    own = own_ref[rows:, :].astype(f)
    m_own = own[0:1] + own[1:2]
    t_own = own[2:3] + own[3:4]
    top = jnp.maximum(jnp.max(m, axis=0, keepdims=True), m_own)
    a = jnp.exp2((m - top) * c)
    a_own = jnp.exp2((m_own - top) * c)
    whole = jnp.sum(a * t, axis=0, keepdims=True) + a_own * t_own
    inv = 1.0 / whole
    table = jnp.concatenate(
        [a * inv, a_own * inv, jnp.zeros((128 - n - 1, 128), f)], axis=0
    )
    coef = jnp.transpose(table)
    acc = own_ref[:rows, :].astype(f) * coef[:rows, n : n + 1]
    for i in range(n):
        acc = acc + got_ref[i, :rows, :].astype(f) * coef[:rows, i : i + 1]
    att = acc.astype(jnp.bfloat16)
    for i in range(out_ref.shape[0]):
        out_ref[i] = att


def project_kernel(heads, core_ref, own_ref, other_ref, w_ref, out_ref, x_ref):
    n, rows, hd = own_ref.shape
    core = core_ref[0]
    x4 = x_ref.reshape(n, 2, rows, hd)
    x4[:, core] = own_ref[...].astype(jnp.float32)
    x4[:, 1 - core] = other_ref[...].astype(jnp.float32)
    total = n * 2 * rows // heads
    acc = jnp.zeros((total, w_ref.shape[1]), jnp.float32)
    for h in range(0, heads, 2):
        pair = [
            x_ref[pl.ds(h + j, total, stride=heads), :].astype(jnp.bfloat16) for j in range(2)
        ]
        lhs = jnp.concatenate(pair, axis=1)
        acc = acc + dot(lhs, w_ref[h * hd : (h + 2) * hd, :], 1, 0)
    out_ref[...] = acc.astype(jnp.bfloat16).reshape(out_ref.shape)


def whole(n):
    return [pl.BlockSpec(memory_space=VMEM)] * n


def shards(q, pk, pv, sk, sv, lengths, w):
    forks, steps, heads, hd = q.shape
    rows = forks * steps * heads
    keys = pk.shape[0]
    slots = sk.shape[1]
    c = hd**-0.5 * LOG2E
    chips = lax.axis_size(CHIPS)
    n_tp = lax.axis_size(TP)
    cols = w.shape[1]
    bf = jnp.bfloat16
    swap = [(0, 1), (1, 0)]

    q = q.reshape(rows, hd)
    every = lax.all_to_all(
        jnp.broadcast_to(q[None], (chips, rows, hd)), CHIPS, 0, 0, tiled=True
    )
    k_own, v_own = pk.reshape(keys, hd), pv.reshape(keys, hd)
    k_pair = lax.ppermute(k_own, "core", swap)
    v_pair = lax.ppermute(v_own, "core", swap)

    own = pl.pallas_call(
        functools.partial(suffix_kernel, c, heads),
        out_shape=jax.ShapeDtypeStruct((rows + STATS, hd), bf),
        in_specs=[pl.BlockSpec(memory_space=pltpu.SMEM)] + whole(3),
        out_specs=pl.BlockSpec(memory_space=VMEM),
        cost_estimate=pl.CostEstimate(
            flops=4 * rows * slots * hd, bytes_accessed=4 * forks * slots * hd, transcendentals=rows * slots
        ),
        name="suffix",
    )(lengths, q, sk.reshape(forks, slots, hd), sv.reshape(forks, slots, hd))

    seg = 2
    states = pl.pallas_call(
        functools.partial(prefix_kernel, c),
        grid=(chips // seg,),
        out_shape=jax.ShapeDtypeStruct((chips, rows + STATS, hd), bf),
        in_specs=[pl.BlockSpec((seg, rows, hd), lambda i: (i, 0, 0))] + whole(4),
        out_specs=pl.BlockSpec((seg, rows + STATS, hd), lambda i: (i, 0, 0)),
        scratch_shapes=[VMEM((2 * keys, 2 * hd), bf)],
        name="prefix",
    )(every, k_own, k_pair, v_own, v_pair)

    got = lax.all_to_all(states, CHIPS, 0, 0, tiled=True)
    att = pl.pallas_call(
        functools.partial(combine_kernel, c),
        out_shape=jax.ShapeDtypeStruct((chips, rows, hd), bf),
        in_specs=whole(2),
        out_specs=pl.BlockSpec(memory_space=VMEM),
        name="combine",
    )(got, own)

    att = lax.all_to_all(att, CHIPS, 0, 0, tiled=True)
    other = lax.ppermute(att, "core", swap)
    core = lax.axis_index("core").astype(jnp.int32).reshape(1)
    all_rows = chips * 2 * forks * steps
    product = pl.pallas_call(
        functools.partial(project_kernel, heads),
        out_shape=jax.ShapeDtypeStruct((n_tp, all_rows // n_tp, cols), bf),
        in_specs=[pl.BlockSpec(memory_space=pltpu.SMEM)] + whole(3),
        out_specs=pl.BlockSpec(memory_space=VMEM),
        scratch_shapes=[VMEM((chips * 2 * rows, hd), jnp.float32)],
        name="project",
    )(core, att, other, w)
    parts = lax.all_to_all(product, TP, 0, 0, tiled=True)
    out = parts.astype(jnp.float32).sum(axis=0).astype(bf)
    return out.reshape(all_rows // n_tp // steps, steps, cols)


def solution(mesh):
    fine = Mesh(
        mesh.devices.reshape(2, mesh.shape["ctx"] // 4, 2, 2, mesh.shape["tp"] // 2),
        CTX + TP,
    )
    return jax.shard_map(
        shards,
        mesh=fine,
        in_specs=(
            P(CTX, None, TP, None),
            P(CTX, TP, None),
            P(CTX, TP, None),
            P(CTX, None, TP, None),
            P(CTX, None, TP, None),
            P(CTX),
            P(TP, CTX),
        ),
        out_specs=P(TP, None, CTX),
        check_vma=False,
    )
```

time: 184 us -> 109 us (0.59)
  waiting for transfers between devices: 69.4 us -> 22.7 us
  Pallas kernels: 0 us -> 30.6 us
  blocking collectives: 52 us -> 28.4 us
  matrix products: 19.2 us -> 0 us
  other arithmetic: 7.9 us -> 0.03 us
  local copies, waits for them, and re-layouts: 8.62 us -> 4.43 us
  starting transfers between devices: 24.2 us -> 21.9 us
    all_to_all x3 -> x2, waiting for transfers between devices: 69.4 us -> 19 us  [the longest x1 10.3 us: shards(): got = lax.all_to_all(states, CHIPS, 0, 0, tiled=True)]
    pallas_call x0 -> x4, Pallas kernels: none -> 30.6 us  [the longest x1 22.6 us: shards(): pl.pallas_call(functools.partial(prefix_kernel, c), grid=(chips // seg,),...]
    all_to_all x3 -> x2, blocking collectives: 52 us -> 28.4 us  [the longest x1 18.3 us: shards(): att = lax.all_to_all(att, CHIPS, 0, 0, tiled=True)]
    dot_general x11 -> x0, matrix products: 19.2 us -> none  [the longest x4 8.68 us: prefix_block(): jnp.einsum('bskgd,pkd->bskgp', grouped, prefix_keys, preferred_element_ty...]
    reduce_sum x8 -> x1, other arithmetic: 7.55 us -> 0.03 us  [shards(): out = parts.astype(jnp.float32).sum(axis=0).astype(bf)]
    all_to_all x3 -> x2, starting transfers between devices: 24.2 us -> 18 us  [the longest x1 11.6 us: shards(): lax.all_to_all(jnp.broadcast_to(q[None], (chips, rows, hd)), CHIPS, 0, 0,...]
    ppermute x0 -> x3, starting transfers between devices: none -> 3.99 us  [the longest x1 2.84 us: shards(): other = lax.ppermute(att, 'core', swap)]
    ppermute x0 -> x3, waiting for transfers between devices: none -> 3.74 us  [the longest x1 1.64 us: shards(): k_pair = lax.ppermute(k_own, 'core', swap)]
  transfers between devices with their start and end apart: 3 -> 5, of which waited for: 3 -> 5; matrix products, arithmetic and copies ran while one was open for 2% -> 0% of each run, Pallas kernels for 0% -> 2%
where the time goes in v1:
time: 109 us; the launch traced here: 108 us
  Pallas kernels  30.6 us (28%)
  blocking collectives  28.4 us (26%)
  waiting for transfers between devices  22.7 us (21%)
  starting transfers between devices  21.9 us (20%)
  local copies, waits for them, and re-layouts  4.43 us (4%)
    pallas_call x1, Pallas kernels, shards(): pl.pallas_call(functools.partial(prefix_kernel, c), grid=(chips // seg,),...  22.6 us
    all_to_all x1, blocking collectives, shards(): att = lax.all_to_all(att, CHIPS, 0, 0, tiled=True)  18.3 us
    all_to_all x1, starting transfers between devices, shards(): lax.all_to_all(jnp.broadcast_to(q[None], (chips, rows, hd)), CHIPS, 0, 0,...  11.6 us
    all_to_all x1, waiting for transfers between devices, shards(): got = lax.all_to_all(states, CHIPS, 0, 0, tiled=True)  10.3 us
    all_to_all x1, blocking collectives, shards(): parts = lax.all_to_all(product, TP, 0, 0, tiled=True)  10.1 us
    all_to_all x1, waiting for transfers between devices, shards(): lax.all_to_all(jnp.broadcast_to(q[None], (chips, rows, hd)), CHIPS, 0, 0,...  8.7 us
    all_to_all x1, starting transfers between devices, shards(): got = lax.all_to_all(states, CHIPS, 0, 0, tiled=True)  6.39 us
    pallas_call x1, Pallas kernels, shards(): pl.pallas_call(functools.partial(project_kernel, heads), out_shape=jax.Sh...  3.29 us
  transfers between devices with their start and end apart: 5, of which 5 were waited for; matrix products, arithmetic and copies ran while one was open for 0% of the time, Pallas kernels for 2%

profile of v1, /device:TPU:1, one launch (start us, length us, event | category | flops | bytes accessed | tf_op | source)
XLA Modules:
  0.0 108.2 jit_solution(491625734361528902)
XLA Ops:
  0.0 1.5 %broadcast_in_dim.8 = bf16[16,96,128]{2,1,0:T(8,128)(2,1)} broadcast(bf16[96,128]{1,0:T(8,128)(2,1)} %bitcast.12), dimensions={1,2} | broadcast | bytes 417792 | tf_op jit(solution)/shard_map/broadcast_in_dim | solution.py:167
  1.6 11.6 %all-to-all-start = ((bf16[16,96,128]{2,1,0:T(8,128)(2,1)}), bf16[16,96,128]{2,1,0:T(8,128)(2,1)S(1)}, u32[]{:S(2)}, u32[]{:S(2)}) async-start(bf16[16,96,128]{2,1,0:T(8,128)(2,1)} %broadcast_in_dim.8), calls=%async_computation | async-start | bytes 786432 | tf_op jit(solution)/shard_map/all_to_all | solution.py:166
  13.1 1.0 collective-permute-start
  14.2 0.1 collective-permute-start.1
  14.3 1.6 %collective-permute-done.kp_ref = bf16[2048,128]{1,0:T(8,128)(2,1)S(1)} collective-permute-done((bf16[2048,128]{1,0:T(8,128)(2,1)}, bf16[2048,128]{1,0:T(8,128)(2,1)S(1)}, u32[]{:S(2)}, u32[]{:S(2)}) %collective-permute-start) | collective-permute-done | bytes 524320 | tf_op jit(solution)/shard_map/ppermute | solution.py:170
  15.9 0.0 copy-start.3
  15.9 0.7 collective-permute-done.1.vp_ref
  16.7 0.0 copy-start.4
  16.7 8.7 %all-to-all-done.q_ref = bf16[16,96,128]{2,1,0:T(8,128)(2,1)S(1)} async-done(((bf16[16,96,128]{2,1,0:T(8,128)(2,1)}), bf16[16,96,128]{2,1,0:T(8,128)(2,1)S(1)}, u32[]{:S(2)}, u32[]{:S(2)}) %all-to-all-start) | async-done | bytes 393248 | tf_op jit(solution)/shard_map/all_to_all | solution.py:166
  25.4 0.0 copy-done.3
  25.4 0.0 copy-done.4
  25.4 0.0 copy-start.2
  25.4 0.7 copy-done.2
  26.1 22.6 %prefix.1 = bf16[16,104,128]{2,1,0:T(8,128)(2,1)} custom-call(bf16[16,96,128]{2,1,0:T(8,128)(2,1)} %copy-done.2, bf16[2048,128]{1,0:T(8,128)(2,1)} %bitcast.7, bf16[2048,128]{1,0:T(8,128)(2,1)} %copy-done.3, bf16[2048,128]{1,0:T(8,128)(2,1)} %bitcast.9, bf16[2048,128]{1,0:T(8,128)(2,1)} %copy-done.4), custom_call_target="tpu_custom_call" | custom-call | tf_op jit(solution)/shard_map/prefix/pallas_call | solution.py:185
  48.7 6.4 %all-to-all-start.1 = ((bf16[16,104,128]{2,1,0:T(8,128)(2,1)}), bf16[16,104,128]{2,1,0:T(8,128)(2,1)S(1)}, u32[]{:S(2)}, u32[]{:S(2)}) async-start(bf16[16,104,128]{2,1,0:T(8,128)(2,1)} %prefix.1), calls=%async_computation.1 | async-start | bytes 851968 | tf_op jit(solution)/shard_map/all_to_all | solution.py:195
  55.1 2.5 %suffix.1.own_ref = bf16[104,128]{1,0:T(8,128)(2,1)} custom-call(s32[2]{0:T(128)} %len_ref.1, bf16[96,128]{1,0:T(8,128)(2,1)} %bitcast.13, bf16[2,512,128]{2,1,0:T(8,128)(2,1)} %bitcast.10, bf16[2,512,128]{2,1,0:T(8,128)(2,1)} %bitcast.11), custom_call_target="tpu_custom_call" | custom-call | flops 25165824 | bytes 524288 | tf_op jit(solution)/shard_map/suffix/pallas_call | solution.py:173
  57.6 10.3 %all-to-all-done.1.got_ref = bf16[16,104,128]{2,1,0:T(8,128)(2,1)S(1)} async-done(((bf16[16,104,128]{2,1,0:T(8,128)(2,1)}), bf16[16,104,128]{2,1,0:T(8,128)(2,1)S(1)}, u32[]{:S(2)}, u32[]{:S(2)}) %all-to-all-start.1) | async-done | bytes 426016 | tf_op jit(solution)/shard_map/all_to_all | solution.py:195
  67.9 0.0 copy-start
  67.9 0.7 copy-done
  68.6 2.2 %combine.1 = bf16[16,96,128]{2,1,0:T(8,128)(2,1)} custom-call(bf16[16,104,128]{2,1,0:T(8,128)(2,1)} %copy-done, bf16[104,128]{1,0:T(8,128)(2,1)} %suffix.1.own_ref), custom_call_target="tpu_custom_call" | custom-call | tf_op jit(solution)/shard_map/combine/pallas_call | solution.py:196
  70.9 18.3 %all_to_all.20.own_ref = bf16[16,96,128]{2,1,0:T(8,128)(2,1)S(1)} all-to-all(bf16[16,96,128]{2,1,0:T(8,128)(2,1)} %combine.1), channel_id=1, replica_groups=mesh['xh'=2,'z'=8,'core'=2,'xl'=2,'y'=4] {'xh','z'}, dimensions={0} | all-to-all | bytes 786432 | tf_op jit(solution)/shard_map/all_to_all | solution.py:204
  89.1 0.0 copy-start.1
  89.1 2.8 %collective-permute-start.2 = (bf16[16,96,128]{2,1,0:T(8,128)(2,1)S(1)}, bf16[16,96,128]{2,1,0:T(8,128)(2,1)S(1)}, u32[]{:S(2)}, u32[]{:S(2)}) collective-permute-start(bf16[16,96,128]{2,1,0:T(8,128)(2,1)S(1)} %all_to_all.20.own_ref), channel_id=1, source_target_pairs={{0,8},{8,0},{1,9},{9,1},{2,10},{10,2},{3,11},{11,3},{4,12},{12,4},... | collective-permute-start | bytes 1179656 | tf_op jit(solution)/shard_map/ppermute | solution.py:205
  92.0 1.3 %collective-permute-done.2.other_ref = bf16[16,96,128]{2,1,0:T(8,128)(2,1)S(1)} collective-permute-done((bf16[16,96,128]{2,1,0:T(8,128)(2,1)S(1)}, bf16[16,96,128]{2,1,0:T(8,128)(2,1)S(1)}, u32[]{:S(2)}, u32[]{:S(2)}) %collective-permute-start.2) | collective-permute-done | bytes 393248 | tf_op jit(solution)/shard_map/ppermute | solution.py:205
  93.3 0.0 copy-start.5
  93.3 0.0 copy-done.1
  93.3 0.7 copy-done.5
  94.1 3.3 %project.1 = bf16[8,24,512]{2,1,0:T(8,128)(2,1)} custom-call(s32[1]{0:T(128)} %bitcast.core_ref, bf16[16,96,128]{2,1,0:T(8,128)(2,1)} %copy-done.1, bf16[16,96,128]{2,1,0:T(8,128)(2,1)} %copy-done.5, bf16[2048,512]{1,0:T(8,128)(2,1)} %w_ref.1), custom_call_target="tpu_custom_call" | custom-call | tf_op jit(solution)/shard_map/project/pallas_call | solution.py:208
  97.4 10.1 %all_to_all.21 = bf16[8,24,512]{2,1,0:T(8,128)(2,1)S(1)} all-to-all(bf16[8,24,512]{2,1,0:T(8,128)(2,1)} %project.1), channel_id=1, replica_groups=mesh['xh'=2,'z'=8,'core'=2,'xl'=2,'y'=4] {'xl','y'}, dimensions={0} | all-to-all | bytes 393216 | tf_op jit(solution)/shard_map/all_to_all | solution.py:216
  107.6 0.6 copy.8
  (2 shorter events, 0.1 us)
Async XLA Ops:
  1.6 23.8 %all-to-all-start = ((bf16[16,96,128]{2,1,0:T(8,128)(2,1)}), bf16[16,96,128]{2,1,0:T(8,128)(2,1)S(1)}, u32[]{:S(2)}, u32[]{:S(2)}) async-start(bf16[16,96,128]{2,1,0:T(8,128)(2,1)} %broadcast_in_dim.8), calls=%async_computation | async-start | bytes 786432 | tf_op jit(solution)/shard_map/all_to_all | solution.py:166
  13.1 2.8 %collective-permute-start = (bf16[2048,128]{1,0:T(8,128)(2,1)}, bf16[2048,128]{1,0:T(8,128)(2,1)S(1)}, u32[]{:S(2)}, u32[]{:S(2)}) collective-permute-start(bf16[2048,128]{1,0:T(8,128)(2,1)} %bitcast.6), channel_id=1, source_target_pairs={{0,8},{8,0},{1,9},{9,1},{2,10},{10,2},{3,11},{11,3},{4,12},{12,4},... | collective-permute-start | bytes 1572872 | tf_op jit(solution)/shard_map/ppermute | solution.py:170
  14.2 2.5 %collective-permute-start.1 = (bf16[2048,128]{1,0:T(8,128)(2,1)}, bf16[2048,128]{1,0:T(8,128)(2,1)S(1)}, u32[]{:S(2)}, u32[]{:S(2)}) collective-permute-start(bf16[2048,128]{1,0:T(8,128)(2,1)} %bitcast.8), channel_id=1, source_target_pairs={{0,8},{8,0},{1,9},{9,1},{2,10},{10,2},{3,11},{11,3},{4,12},{12,4},... | collective-permute-start | bytes 1572872 | tf_op jit(solution)/shard_map/ppermute | solution.py:171
  15.9 9.5 %copy-start.3 = (bf16[2048,128]{1,0:T(8,128)(2,1)}, bf16[2048,128]{1,0:T(8,128)(2,1)S(1)}, u32[]{:S(2)}) copy-start(bf16[2048,128]{1,0:T(8,128)(2,1)S(1)} %collective-permute-done.kp_ref) | copy-start | bytes 1572868
  16.7 8.7 %copy-start.4 = (bf16[2048,128]{1,0:T(8,128)(2,1)}, bf16[2048,128]{1,0:T(8,128)(2,1)S(1)}, u32[]{:S(2)}) copy-start(bf16[2048,128]{1,0:T(8,128)(2,1)S(1)} %collective-permute-done.1.vp_ref) | copy-start | bytes 1572868
  25.4 0.7 copy-start.2
  48.7 19.2 %all-to-all-start.1 = ((bf16[16,104,128]{2,1,0:T(8,128)(2,1)}), bf16[16,104,128]{2,1,0:T(8,128)(2,1)S(1)}, u32[]{:S(2)}, u32[]{:S(2)}) async-start(bf16[16,104,128]{2,1,0:T(8,128)(2,1)} %prefix.1), calls=%async_computation.1 | async-start | bytes 851968 | tf_op jit(solution)/shard_map/all_to_all | solution.py:195
  67.9 0.8 copy-start
  89.1 4.2 %copy-start.1 = (bf16[16,96,128]{2,1,0:T(8,128)(2,1)}, bf16[16,96,128]{2,1,0:T(8,128)(2,1)S(1)}, u32[]{:S(2)}) copy-start(bf16[16,96,128]{2,1,0:T(8,128)(2,1)S(1)} %all_to_all.20.own_ref) | copy-start | bytes 1179652
  89.1 4.2 %collective-permute-start.2 = (bf16[16,96,128]{2,1,0:T(8,128)(2,1)S(1)}, bf16[16,96,128]{2,1,0:T(8,128)(2,1)S(1)}, u32[]{:S(2)}, u32[]{:S(2)}) collective-permute-start(bf16[16,96,128]{2,1,0:T(8,128)(2,1)S(1)} %all_to_all.20.own_ref), channel_id=1, source_target_pairs={{0,8},{8,0},{1,9},{9,1},{2,10},{10,2},{3,11},{11,3},{4,12},{12,4},... | collective-permute-start | bytes 1179656 | tf_op jit(solution)/shard_map/ppermute | solution.py:205
  93.3 0.7 copy-start.5

commit v2 on v1

--- a/solution.py
+++ b/solution.py
@@ -5,6 +5,7 @@
 from jax import lax
 from jax.experimental import pallas as pl
 from jax.experimental.pallas import tpu as pltpu
+from jax._src.pallas.mosaic import core as pltpu_core
 from jax.sharding import Mesh
 from jax.sharding import PartitionSpec as P
 
@@ -13,6 +14,9 @@
 TP = ("xl", "y")
 STATS = 8
 NEG = -1e30
+TILE = 256
+PART = 768
+UNROLL = 4
 LOG2E = 1.4426950408889634
 VMEM = pltpu.VMEM
 
@@ -53,32 +57,93 @@
     return dot(pick, table, 1, 1).astype(jnp.bfloat16)
 
 
-def prefix_kernel(c, q_ref, ko_ref, kp_ref, vo_ref, vp_ref, out_ref, v_ref):
-    n_seg, rows, hd = q_ref.shape
+def accumulator(mxu, rows):
+    return pltpu_core.AccMemorySpace(mxu)((rows, TILE), jnp.float32)
+
+
+def prefix_kernel(c, q_ref, ko_ref, kp_ref, vo_ref, vp_ref, out_ref, q2, s_o, s_p, m_ref, o_ref):
+    n, rows, hd = q_ref.shape
+    total = n * rows
     keys = ko_ref.shape[0]
-
-    @pl.when(pl.program_id(0) == 0)
-    def _():
-        v_ref[:keys, :hd] = vo_ref[...]
-        v_ref[keys:, :hd] = vp_ref[...]
-        v_ref[:, hd:] = jnp.ones((2 * keys, hd), jnp.bfloat16)
-
-    q = q_ref[...].reshape(n_seg * rows, hd)
-    s1 = dot(q, ko_ref[...], 1, 1)
-    s2 = dot(q, kp_ref[...], 1, 1)
-    top = jnp.maximum(
-        jnp.max(s1, axis=1, keepdims=True), jnp.max(s2, axis=1, keepdims=True)
-    )
-    hi, lo, shift = shift_of(top)
-    p1 = jnp.exp2((s1 - shift) * c).astype(jnp.bfloat16)
-    p2 = jnp.exp2((s2 - shift) * c).astype(jnp.bfloat16)
-    o = dot(p1, v_ref[:keys], 1, 0) + dot(p2, v_ref[keys:], 1, 0)
-    mixed = o[:, :hd].astype(jnp.bfloat16)
-    totals = o[:, hd : hd + 1]
-    for i in range(n_seg):
-        r = slice(i * rows, (i + 1) * rows)
-        out_ref[i, :rows, :] = mixed[r]
-        out_ref[i, rows:, :] = stat_rows(hi[r], lo[r], totals[r])
+    f, bf = jnp.float32, jnp.bfloat16
+    scores, ks, vs = (s_o, s_p), (ko_ref, kp_ref), (vo_ref, vp_ref)
+
+    scaled = q_ref[...].reshape(total, hd).astype(f) * c
+    high = scaled.astype(bf)
+    q2[:, :hd] = high
+    q2[:, hd:] = (scaled - high.astype(f)).astype(bf)
+    m_ref[...] = jnp.full(m_ref.shape, -jnp.inf, f)
+
+    def pass_a(*accs):
+        @pl.loop(0, keys // TILE // UNROLL)
+        def _(outer):
+            for w in range(UNROLL):
+                at = pl.ds(pl.multiple_of((outer * UNROLL + w) * TILE, TILE), TILE)
+                for x in range(2):
+                    k = ks[x][at, :]
+                    pltpu.matmul_push_rhs(
+                        jnp.concatenate([k, k], axis=1), w % 2, x, transpose=True
+                    )
+                for r in range(total // TILE):
+                    rs = slice(r * TILE, (r + 1) * TILE)
+                    for x in range(2):
+                        pltpu.matmul_acc_lhs(
+                            accs[2 * (r % 2) + x],
+                            q2[rs, :],
+                            load_staged_rhs=w % 2 if r == 0 else None,
+                        )
+                    tops = []
+                    for x in range(2):
+                        s = pltpu.matmul_pop(accs[2 * (r % 2) + x])
+                        scores[x][rs, at] = s
+                        tops.append(jnp.maximum(s[:, :128], s[:, 128:]))
+                    m_ref[rs, :] = jnp.maximum(jnp.maximum(tops[0], tops[1]), m_ref[rs, :])
+
+    pl.run_scoped(pass_a, *[accumulator(i % 2, TILE) for i in range(4)])
+    shift = shift_of(jnp.max(m_ref[...], axis=1, keepdims=True))[2]
+    m_ref[...] = jnp.broadcast_to(shift, m_ref.shape)
+    ones = jnp.ones((TILE, TILE - hd), bf)
+    parts = PART // TILE
+
+    def pass_b(*accs):
+        for b in range(total // PART):
+
+            @pl.loop(0, keys // TILE // UNROLL)
+            def _(outer):
+                for w in range(UNROLL):
+                    at = pl.ds(pl.multiple_of((outer * UNROLL + w) * TILE, TILE), TILE)
+                    for x in range(2):
+                        pltpu.matmul_push_rhs(
+                            jnp.concatenate([vs[x][at, :], ones], axis=1), w % 2, x
+                        )
+                    for u in range(parts):
+                        rs = slice(b * PART + u * TILE, b * PART + (u + 1) * TILE)
+                        m = m_ref[rs, :]
+                        m = jnp.concatenate([m, m], axis=1)
+                        for x in range(2):
+                            p = jnp.exp2(scores[x][rs, at] - m).astype(bf)
+                            pltpu.matmul_acc_lhs(
+                                accs[x * parts + u], p, load_staged_rhs=w % 2 if u == 0 else None
+                            )
+
+            for u in range(parts):
+                rs = slice(b * PART + u * TILE, b * PART + (u + 1) * TILE)
+                o_ref[rs, :] = pltpu.matmul_pop(accs[u]) + pltpu.matmul_pop(accs[parts + u])
+
+    pl.run_scoped(pass_b, *[accumulator(i // parts, TILE) for i in range(2 * parts)])
+
+    lane = lax.broadcasted_iota(jnp.int32, (rows, 128), 1)
+    table = jnp.zeros((rows, 128), f)
+    for i in range(n):
+        rs = slice(i * rows, (i + 1) * rows)
+        out_ref[i, :rows, :] = o_ref[rs, :hd].astype(bf)
+        t, m = o_ref[rs, hd:], m_ref[rs, :]
+        hi, t_hi = m.astype(bf).astype(f), t.astype(bf).astype(f)
+        for l, v in enumerate((hi, m - hi, t_hi, t - t_hi)):
+            table = jnp.where(lane == STATS * i + l, v, table)
+    turned = jnp.transpose(jnp.concatenate([table, jnp.zeros((128 - rows, 128), f)], axis=0))
+    for i in range(n):
+        out_ref[i, rows:, :] = turned[STATS * i : STATS * (i + 1)].astype(bf)
 
 
 def suffix_kernel(c, heads, len_ref, q_ref, k_ref, v_ref, out_ref):
@@ -87,12 +152,12 @@
     his, los, tots = [], [], []
     for f in range(forks):
         q = q_ref[f * rows : (f + 1) * rows, :]
-        s = dot(q, k_ref[f], 1, 1)
+        s = dot(q, k_ref[f], 1, 1) * c
         step = lax.broadcasted_iota(jnp.int32, (rows, slots), 0) // heads
         slot = lax.broadcasted_iota(jnp.int32, (rows, slots), 1)
         s = jnp.where(slot < len_ref[f] + step + 1, s, NEG)
         hi, lo, shift = shift_of(jnp.max(s, axis=1, keepdims=True))
-        p = jnp.exp2((s - shift) * c)
+        p = jnp.exp2(s - shift)
         out_ref[f * rows : (f + 1) * rows, :] = dot(
             p.astype(jnp.bfloat16), v_ref[f], 1, 0
         ).astype(jnp.bfloat16)
@@ -103,7 +168,7 @@
     out_ref[forks * rows :, :] = stat_rows(cat(his), cat(los), cat(tots))
 
 
-def combine_kernel(c, got_ref, own_ref, out_ref):
+def combine_kernel(got_ref, own_ref, out_ref):
     n = got_ref.shape[0]
     rows = own_ref.shape[0] - STATS
     f = jnp.float32
@@ -113,8 +178,8 @@
     m_own = own[0:1] + own[1:2]
     t_own = own[2:3] + own[3:4]
     top = jnp.maximum(jnp.max(m, axis=0, keepdims=True), m_own)
-    a = jnp.exp2((m - top) * c)
-    a_own = jnp.exp2((m_own - top) * c)
+    a = jnp.exp2(m - top)
+    a_own = jnp.exp2(m_own - top)
     whole = jnp.sum(a * t, axis=0, keepdims=True) + a_own * t_own
     inv = 1.0 / whole
     table = jnp.concatenate(
@@ -129,21 +194,36 @@
         out_ref[i] = att
 
 
-def project_kernel(heads, core_ref, own_ref, other_ref, w_ref, out_ref, x_ref):
+def project_kernel(heads, steps, core_ref, own_ref, other_ref, w_ref, out_ref, x_ref):
     n, rows, hd = own_ref.shape
     core = core_ref[0]
     x4 = x_ref.reshape(n, 2, rows, hd)
     x4[:, core] = own_ref[...].astype(jnp.float32)
     x4[:, 1 - core] = other_ref[...].astype(jnp.float32)
-    total = n * 2 * rows // heads
-    acc = jnp.zeros((total, w_ref.shape[1]), jnp.float32)
+    forks = n * 2 * rows // heads // steps
+    acc = jnp.zeros((steps * forks, w_ref.shape[1]), jnp.float32)
     for h in range(0, heads, 2):
         pair = [
-            x_ref[pl.ds(h + j, total, stride=heads), :].astype(jnp.bfloat16) for j in range(2)
+            jnp.concatenate(
+                [
+                    x_ref[pl.ds(s * heads + h + j, forks, stride=steps * heads), :]
+                    for s in range(steps)
+                ],
+                axis=0,
+            ).astype(jnp.bfloat16)
+            for j in range(2)
         ]
         lhs = jnp.concatenate(pair, axis=1)
         acc = acc + dot(lhs, w_ref[h * hd : (h + 2) * hd, :], 1, 0)
-    out_ref[...] = acc.astype(jnp.bfloat16).reshape(out_ref.shape)
+    tps = out_ref.shape[0]
+    mine = forks // tps
+    for s in range(steps):
+        block = acc[s * forks : (s + 1) * forks].astype(jnp.bfloat16)
+        out_ref[:, s] = block.reshape(tps, mine, -1)
+
+
+def sum_kernel(parts_ref, out_ref):
+    out_ref[...] = jnp.sum(parts_ref[...].astype(jnp.float32), axis=0).astype(jnp.bfloat16)
 
 
 def whole(n):
@@ -178,44 +258,61 @@
         cost_estimate=pl.CostEstimate(
             flops=4 * rows * slots * hd, bytes_accessed=4 * forks * slots * hd, transcendentals=rows * slots
         ),
+        compiler_params=pltpu.CompilerParams(vmem_limit_bytes=4 * 2**20),
         name="suffix",
     )(lengths, q, sk.reshape(forks, slots, hd), sv.reshape(forks, slots, hd))
 
-    seg = 2
+    total = chips * rows
+    f = jnp.float32
     states = pl.pallas_call(
         functools.partial(prefix_kernel, c),
-        grid=(chips // seg,),
         out_shape=jax.ShapeDtypeStruct((chips, rows + STATS, hd), bf),
-        in_specs=[pl.BlockSpec((seg, rows, hd), lambda i: (i, 0, 0))] + whole(4),
-        out_specs=pl.BlockSpec((seg, rows + STATS, hd), lambda i: (i, 0, 0)),
-        scratch_shapes=[VMEM((2 * keys, 2 * hd), bf)],
+        in_specs=whole(5),
+        out_specs=pl.BlockSpec(memory_space=VMEM),
+        scratch_shapes=[
+            VMEM((total, TILE), bf),
+            VMEM((total, keys), f),
+            VMEM((total, keys), f),
+            VMEM((total, 128), f),
+            VMEM((total, TILE), f),
+        ],
+        compiler_params=pltpu.CompilerParams(vmem_limit_bytes=36 * 2**20),
         name="prefix",
     )(every, k_own, k_pair, v_own, v_pair)
 
     got = lax.all_to_all(states, CHIPS, 0, 0, tiled=True)
     att = pl.pallas_call(
-        functools.partial(combine_kernel, c),
+        combine_kernel,
         out_shape=jax.ShapeDtypeStruct((chips, rows, hd), bf),
         in_specs=whole(2),
         out_specs=pl.BlockSpec(memory_space=VMEM),
+        compiler_params=pltpu.CompilerParams(vmem_limit_bytes=4 * 2**20),
         name="combine",
     )(got, own)
 
     att = lax.all_to_all(att, CHIPS, 0, 0, tiled=True)
     other = lax.ppermute(att, "core", swap)
     core = lax.axis_index("core").astype(jnp.int32).reshape(1)
-    all_rows = chips * 2 * forks * steps
+    mine = chips * 2 * forks // n_tp
     product = pl.pallas_call(
-        functools.partial(project_kernel, heads),
-        out_shape=jax.ShapeDtypeStruct((n_tp, all_rows // n_tp, cols), bf),
+        functools.partial(project_kernel, heads, steps),
+        out_shape=jax.ShapeDtypeStruct((n_tp, steps, mine, cols), bf),
         in_specs=[pl.BlockSpec(memory_space=pltpu.SMEM)] + whole(3),
         out_specs=pl.BlockSpec(memory_space=VMEM),
         scratch_shapes=[VMEM((chips * 2 * rows, hd), jnp.float32)],
+        compiler_params=pltpu.CompilerParams(vmem_limit_bytes=10 * 2**20),
         name="project",
     )(core, att, other, w)
     parts = lax.all_to_all(product, TP, 0, 0, tiled=True)
-    out = parts.astype(jnp.float32).sum(axis=0).astype(bf)
-    return out.reshape(all_rows // n_tp // steps, steps, cols)
+    out = pl.pallas_call(
+        sum_kernel,
+        out_shape=jax.ShapeDtypeStruct((steps, mine, cols), bf),
+        in_specs=whole(1),
+        out_specs=pl.BlockSpec(memory_space=VMEM),
+        compiler_params=pltpu.CompilerParams(vmem_limit_bytes=2 * 2**20),
+        name="total",
+    )(parts)
+    return jnp.swapaxes(out, 0, 1)
 
 
 def solution(mesh):

time: 109 us -> 90.5 us (0.83)
  Pallas kernels: 30.6 us -> 12.3 us
  waiting for transfers between devices: 22.7 us -> 23.8 us
    pallas_call x3 -> x4, Pallas kernels: 28.1 us -> 10.9 us  [the longest x1 9.04 us: shards(): pl.pallas_call(functools.partial(prefix_kernel, c), out_shape=jax.ShapeDt...]
    pallas_call x1, Pallas kernels: 2.51 us -> 1.37 us  [shards(): pl.pallas_call(functools.partial(suffix_kernel, c, heads), out_shape=jax....]
    all_to_all x1, waiting for transfers between devices: 10.3 us -> 11.4 us  [shards(): got = lax.all_to_all(states, CHIPS, 0, 0, tiled=True)]
    unnamed x12 -> x14, local copies, waits for them, and re-layouts: 2.25 us -> 2.1 us
where the time goes in v2:
time: 90.5 us; the launch traced here: 90 us
  blocking collectives  28 us (31%)
  waiting for transfers between devices  23.8 us (26%)
  starting transfers between devices  22.2 us (25%)
  Pallas kernels  12.3 us (14%)
  local copies, waits for them, and re-layouts  3.63 us (4%)
    all_to_all x1, blocking collectives, shards(): att = lax.all_to_all(att, CHIPS, 0, 0, tiled=True)  18.1 us
    all_to_all x1, starting transfers between devices, shards(): lax.all_to_all(jnp.broadcast_to(q[None], (chips, rows, hd)), CHIPS, 0, 0,...  11.7 us
    all_to_all x1, waiting for transfers between devices, shards(): got = lax.all_to_all(states, CHIPS, 0, 0, tiled=True)  11.4 us
    all_to_all x1, blocking collectives, shards(): parts = lax.all_to_all(product, TP, 0, 0, tiled=True)  9.94 us
    pallas_call x1, Pallas kernels, shards(): pl.pallas_call(functools.partial(prefix_kernel, c), out_shape=jax.ShapeDt...  9.04 us
    all_to_all x1, waiting for transfers between devices, shards(): lax.all_to_all(jnp.broadcast_to(q[None], (chips, rows, hd)), CHIPS, 0, 0,...  8.7 us
    all_to_all x1, starting transfers between devices, shards(): got = lax.all_to_all(states, CHIPS, 0, 0, tiled=True)  6.52 us
    ppermute x1, starting transfers between devices, shards(): other = lax.ppermute(att, 'core', swap)  2.84 us
  transfers between devices with their start and end apart: 5, of which 5 were waited for; matrix products, arithmetic and copies ran while one was open for 0% of the time, Pallas kernels for 2%

profile of v2, /device:TPU:1, one launch (start us, length us, event | category | flops | bytes accessed | tf_op | source)
XLA Modules:
  0.0 90.0 jit_solution(5651289606179408492)
XLA Ops:
  0.0 1.5 %broadcast_in_dim.8 = bf16[16,96,128]{2,1,0:T(8,128)(2,1)} broadcast(bf16[96,128]{1,0:T(8,128)(2,1)} %bitcast.13), dimensions={1,2} | broadcast | bytes 417792 | tf_op jit(solution)/shard_map/broadcast_in_dim | solution.py:247
  1.5 0.0 copy-start.3
  1.5 0.0 copy-start.4
  1.5 0.0 copy-start.5
  1.5 0.0 copy-start.6
  1.5 11.7 %all-to-all-start = ((bf16[16,96,128]{2,1,0:T(8,128)(2,1)}), bf16[16,96,128]{2,1,0:T(8,128)(2,1)S(1)}, u32[]{:S(2)}, u32[]{:S(2)}) async-start(bf16[16,96,128]{2,1,0:T(8,128)(2,1)} %broadcast_in_dim.8), calls=%async_computation | async-start | bytes 786432 | tf_op jit(solution)/shard_map/all_to_all | solution.py:246
  13.3 1.0 %collective-permute-start = (bf16[2048,128]{1,0:T(8,128)(2,1)}, bf16[2048,128]{1,0:T(8,128)(2,1)S(1)}, u32[]{:S(2)}, u32[]{:S(2)}) collective-permute-start(bf16[2048,128]{1,0:T(8,128)(2,1)} %bitcast.7), channel_id=1, source_target_pairs={{0,8},{8,0},{1,9},{9,1},{2,10},{10,2},{3,11},{11,3},{4,12},{12,4},... | collective-permute-start | bytes 1572872 | tf_op jit(solution)/shard_map/ppermute | solution.py:250
  14.3 0.1 collective-permute-start.1
  14.4 1.6 %collective-permute-done.kp_ref = bf16[2048,128]{1,0:T(8,128)(2,1)S(1)} collective-permute-done((bf16[2048,128]{1,0:T(8,128)(2,1)}, bf16[2048,128]{1,0:T(8,128)(2,1)S(1)}, u32[]{:S(2)}, u32[]{:S(2)}) %collective-permute-start) | collective-permute-done | bytes 524320 | tf_op jit(solution)/shard_map/ppermute | solution.py:250
  16.1 0.7 collective-permute-done.1.vp_ref
  16.8 8.7 %all-to-all-done.q_ref = bf16[16,96,128]{2,1,0:T(8,128)(2,1)S(1)} async-done(((bf16[16,96,128]{2,1,0:T(8,128)(2,1)}), bf16[16,96,128]{2,1,0:T(8,128)(2,1)S(1)}, u32[]{:S(2)}, u32[]{:S(2)}) %all-to-all-start) | async-done | bytes 393248 | tf_op jit(solution)/shard_map/all_to_all | solution.py:246
  25.5 0.0 copy-start.1
  25.5 1.0 %copy-done.1 = bf16[2048,1,128]{2,0,1:T(8,128)(2,1)S(1)} copy-done((bf16[2048,1,128]{2,0,1:T(8,128)(2,1)S(1)}, bf16[2048,1,128]{2,0,1:T(8,128)(2,1)}, u32[]{:S(2)}) %copy-start.1) | copy-done | bytes 524312
  26.5 0.0 copy-start.2
  26.5 1.0 %copy-done.2 = bf16[2048,1,128]{2,0,1:T(8,128)(2,1)S(1)} copy-done((bf16[2048,1,128]{2,0,1:T(8,128)(2,1)S(1)}, bf16[2048,1,128]{2,0,1:T(8,128)(2,1)}, u32[]{:S(2)}) %copy-start.2) | copy-done | bytes 524312
  27.6 9.0 %prefix.1 = bf16[16,104,128]{2,1,0:T(8,128)(2,1)} custom-call(bf16[16,96,128]{2,1,0:T(8,128)(2,1)S(1)} %all-to-all-done.q_ref, bf16[2048,128]{1,0:T(8,128)(2,1)S(1)} %bitcast.8, bf16[2048,128]{1,0:T(8,128)(2,1)S(1)} %collective-permute-done.kp_ref, bf16[2048,128]{1,0:T(8,128)(2,1)S(1)} %bitcast.10, bf16[2048,128]{1,0:T(8,128)(2,1)S(1)} %collective-permute-done.1.vp_ref), custom_call_target="tpu_custom_call" | custom-call | tf_op jit(solution)/shard_map/prefix/pallas_call | solution.py:267
  36.6 0.0 copy-start
  36.6 6.5 %all-to-all-start.1 = ((bf16[16,104,128]{2,1,0:T(8,128)(2,1)}), bf16[16,104,128]{2,1,0:T(8,128)(2,1)S(1)}, u32[]{:S(2)}, u32[]{:S(2)}) async-start(bf16[16,104,128]{2,1,0:T(8,128)(2,1)} %prefix.1), calls=%async_computation.1 | async-start | bytes 851968 | tf_op jit(solution)/shard_map/all_to_all | solution.py:283
  43.2 0.0 copy-done.3
  43.2 0.0 copy-done.4
  43.2 0.0 copy-done.5
  43.2 0.0 copy-done.6
  43.2 1.4 %suffix.1.own_ref = bf16[104,128]{1,0:T(8,128)(2,1)S(1)} custom-call(s32[2]{0:T(128)S(1)} %copy-done.6, bf16[96,128]{1,0:T(8,128)(2,1)S(1)} %bitcast.14, bf16[2,512,128]{2,1,0:T(8,128)(2,1)S(1)} %bitcast.11, bf16[2,512,128]{2,1,0:T(8,128)(2,1)S(1)} %bitcast.12), custom_call_target="tpu_custom_call" | custom-call | flops 25165824 | bytes 524288 | tf_op jit(solution)/shard_map/suffix/pallas_call | solution.py:253
  44.6 11.4 %all-to-all-done.1.got_ref = bf16[16,104,128]{2,1,0:T(8,128)(2,1)S(1)} async-done(((bf16[16,104,128]{2,1,0:T(8,128)(2,1)}), bf16[16,104,128]{2,1,0:T(8,128)(2,1)S(1)}, u32[]{:S(2)}, u32[]{:S(2)}) %all-to-all-start.1) | async-done | bytes 426016 | tf_op jit(solution)/shard_map/all_to_all | solution.py:283
  55.9 0.5 combine.1
  56.4 18.1 %all_to_all.20.own_ref = bf16[16,96,128]{2,1,0:T(8,128)(2,1)S(1)} all-to-all(bf16[16,96,128]{2,1,0:T(8,128)(2,1)S(1)} %combine.1), channel_id=1, replica_groups=mesh['xh'=2,'z'=8,'core'=2,'xl'=2,'y'=4] {'xh','z'}, dimensions={0} | all-to-all | bytes 786432 | tf_op jit(solution)/shard_map/all_to_all | solution.py:293
  74.5 2.8 %collective-permute-start.2 = (bf16[16,96,128]{2,1,0:T(8,128)(2,1)S(1)}, bf16[16,96,128]{2,1,0:T(8,128)(2,1)S(1)}, u32[]{:S(2)}, u32[]{:S(2)}) collective-permute-start(bf16[16,96,128]{2,1,0:T(8,128)(2,1)S(1)} %all_to_all.20.own_ref), channel_id=1, source_target_pairs={{0,8},{8,0},{1,9},{9,1},{2,10},{10,2},{3,11},{11,3},{4,12},{12,4},... | collective-permute-start | bytes 1179656 | tf_op jit(solution)/shard_map/ppermute | solution.py:294
  77.3 1.3 %collective-permute-done.2.other_ref = bf16[16,96,128]{2,1,0:T(8,128)(2,1)S(1)} collective-permute-done((bf16[16,96,128]{2,1,0:T(8,128)(2,1)S(1)}, bf16[16,96,128]{2,1,0:T(8,128)(2,1)S(1)}, u32[]{:S(2)}, u32[]{:S(2)}) %collective-permute-start.2) | collective-permute-done | bytes 393248 | tf_op jit(solution)/shard_map/ppermute | solution.py:294
  78.7 0.0 copy-done
  78.7 0.8 project.1
  79.4 9.9 %all_to_all.21.parts_ref = bf16[8,3,8,512]{3,2,1,0:T(8,128)(2,1)S(1)} all-to-all(bf16[8,3,8,512]{3,2,1,0:T(8,128)(2,1)S(1)} %project.1), channel_id=1, replica_groups=mesh['xh'=2,'z'=8,'core'=2,'xl'=2,'y'=4] {'xl','y'}, dimensions={0} | all-to-all | bytes 393216 | tf_op jit(solution)/shard_map/all_to_all | solution.py:306
  89.4 0.6 total.1
Async XLA Ops:
  1.5 41.6 %copy-start.3 = (bf16[2,512,1,128]{3,1,2,0:T(8,128)(2,1)S(1)}, bf16[2,512,1,128]{3,1,2,0:T(8,128)(2,1)}, u32[]{:S(2)}) copy-start(bf16[2,512,1,128]{3,1,2,0:T(8,128)(2,1)} %param.10) | copy-start | bytes 786436
  1.5 41.6 %copy-start.4 = (bf16[2,512,1,128]{3,1,2,0:T(8,128)(2,1)S(1)}, bf16[2,512,1,128]{3,1,2,0:T(8,128)(2,1)}, u32[]{:S(2)}) copy-start(bf16[2,512,1,128]{3,1,2,0:T(8,128)(2,1)} %param.11) | copy-start | bytes 786436
  1.5 41.6 %copy-start.5 = (bf16[2,3,16,128]{3,2,1,0:T(8,128)(2,1)S(1)}, bf16[2,3,16,128]{3,2,1,0:T(8,128)(2,1)}, u32[]{:S(2)}) copy-start(bf16[2,3,16,128]{3,2,1,0:T(8,128)(2,1)} %param.7) | copy-start | bytes 73732
  1.5 41.7 %copy-start.6 = (s32[2]{0:T(128)S(1)}, s32[2]{0:T(128)}, u32[]{:S(2)}) copy-start(s32[2]{0:T(128)} %len_ref.1) | copy-start | bytes 28
  1.5 24.0 %all-to-all-start = ((bf16[16,96,128]{2,1,0:T(8,128)(2,1)}), bf16[16,96,128]{2,1,0:T(8,128)(2,1)S(1)}, u32[]{:S(2)}, u32[]{:S(2)}) async-start(bf16[16,96,128]{2,1,0:T(8,128)(2,1)} %broadcast_in_dim.8), calls=%async_computation | async-start | bytes 786432 | tf_op jit(solution)/shard_map/all_to_all | solution.py:246
  13.3 2.8 %collective-permute-start = (bf16[2048,128]{1,0:T(8,128)(2,1)}, bf16[2048,128]{1,0:T(8,128)(2,1)S(1)}, u32[]{:S(2)}, u32[]{:S(2)}) collective-permute-start(bf16[2048,128]{1,0:T(8,128)(2,1)} %bitcast.7), channel_id=1, source_target_pairs={{0,8},{8,0},{1,9},{9,1},{2,10},{10,2},{3,11},{11,3},{4,12},{12,4},... | collective-permute-start | bytes 1572872 | tf_op jit(solution)/shard_map/ppermute | solution.py:250
  14.3 2.5 %collective-permute-start.1 = (bf16[2048,128]{1,0:T(8,128)(2,1)}, bf16[2048,128]{1,0:T(8,128)(2,1)S(1)}, u32[]{:S(2)}, u32[]{:S(2)}) collective-permute-start(bf16[2048,128]{1,0:T(8,128)(2,1)} %bitcast.9), channel_id=1, source_target_pairs={{0,8},{8,0},{1,9},{9,1},{2,10},{10,2},{3,11},{11,3},{4,12},{12,4},... | collective-permute-start | bytes 1572872 | tf_op jit(solution)/shard_map/ppermute | solution.py:251
  25.5 1.0 %copy-start.1 = (bf16[2048,1,128]{2,0,1:T(8,128)(2,1)S(1)}, bf16[2048,1,128]{2,0,1:T(8,128)(2,1)}, u32[]{:S(2)}) copy-start(bf16[2048,1,128]{2,0,1:T(8,128)(2,1)} %param.8) | copy-start | bytes 1572868
  26.5 1.0 %copy-start.2 = (bf16[2048,1,128]{2,0,1:T(8,128)(2,1)S(1)}, bf16[2048,1,128]{2,0,1:T(8,128)(2,1)}, u32[]{:S(2)}) copy-start(bf16[2048,1,128]{2,0,1:T(8,128)(2,1)} %param.9) | copy-start | bytes 1572868
  36.6 42.1 %copy-start = (bf16[2048,512]{1,0:T(8,128)(2,1)S(1)}, bf16[2048,512]{1,0:T(8,128)(2,1)}, u32[]{:S(2)}) copy-start(bf16[2048,512]{1,0:T(8,128)(2,1)} %w_ref.1) | copy-start | bytes 6291460
  36.6 19.3 %all-to-all-start.1 = ((bf16[16,104,128]{2,1,0:T(8,128)(2,1)}), bf16[16,104,128]{2,1,0:T(8,128)(2,1)S(1)}, u32[]{:S(2)}, u32[]{:S(2)}) async-start(bf16[16,104,128]{2,1,0:T(8,128)(2,1)} %prefix.1), calls=%async_computation.1 | async-start | bytes 851968 | tf_op jit(solution)/shard_map/all_to_all | solution.py:283
  74.5 4.2 %collective-permute-start.2 = (bf16[16,96,128]{2,1,0:T(8,128)(2,1)S(1)}, bf16[16,96,128]{2,1,0:T(8,128)(2,1)S(1)}, u32[]{:S(2)}, u32[]{:S(2)}) collective-permute-start(bf16[16,96,128]{2,1,0:T(8,128)(2,1)S(1)} %all_to_all.20.own_ref), channel_id=1, source_target_pairs={{0,8},{8,0},{1,9},{9,1},{2,10},{10,2},{3,11},{11,3},{4,12},{12,4},... | collective-permute-start | bytes 1179656 | tf_op jit(solution)/shard_map/ppermute | solution.py:294

commit v3 on v2

--- a/solution.py
+++ b/solution.py
@@ -9,13 +9,13 @@
 from jax.sharding import Mesh
 from jax.sharding import PartitionSpec as P
 
+
 CTX = ("xh", "z", "core")
 CHIPS = ("xh", "z")
 TP = ("xl", "y")
 STATS = 8
 NEG = -1e30
 TILE = 256
-PART = 768
 UNROLL = 4
 LOG2E = 1.4426950408889634
 VMEM = pltpu.VMEM
@@ -61,20 +61,20 @@
     return pltpu_core.AccMemorySpace(mxu)((rows, TILE), jnp.float32)
 
 
-def prefix_kernel(c, q_ref, ko_ref, kp_ref, vo_ref, vp_ref, out_ref, q2, s_o, s_p, m_ref, o_ref):
+def scaled_queries(c, q_ref, q2):
     n, rows, hd = q_ref.shape
-    total = n * rows
-    keys = ko_ref.shape[0]
     f, bf = jnp.float32, jnp.bfloat16
-    scores, ks, vs = (s_o, s_p), (ko_ref, kp_ref), (vo_ref, vp_ref)
-
-    scaled = q_ref[...].reshape(total, hd).astype(f) * c
+    scaled = q_ref[...].reshape(n * rows, hd).astype(f) * c
     high = scaled.astype(bf)
     q2[:, :hd] = high
     q2[:, hd:] = (scaled - high.astype(f)).astype(bf)
-    m_ref[...] = jnp.full(m_ref.shape, -jnp.inf, f)
-
-    def pass_a(*accs):
+
+
+def score_pass(q2, ks, scores, m_ref):
+    keys = ks[0].shape[0]
+    total = q2.shape[0]
+
+    def body(*accs):
         @pl.loop(0, keys // TILE // UNROLL)
         def _(outer):
             for w in range(UNROLL):
@@ -99,45 +99,77 @@
                         tops.append(jnp.maximum(s[:, :128], s[:, 128:]))
                     m_ref[rs, :] = jnp.maximum(jnp.maximum(tops[0], tops[1]), m_ref[rs, :])
 
-    pl.run_scoped(pass_a, *[accumulator(i % 2, TILE) for i in range(4)])
+    pl.run_scoped(body, *[accumulator(i % 2, TILE) for i in range(4)])
     shift = shift_of(jnp.max(m_ref[...], axis=1, keepdims=True))[2]
     m_ref[...] = jnp.broadcast_to(shift, m_ref.shape)
+
+
+def mix_pass(vs, scores, m_ref, o_ref):
+    keys, hd = vs[0].shape
+    total = m_ref.shape[0]
+    parts = total // TILE
+    bf = jnp.bfloat16
     ones = jnp.ones((TILE, TILE - hd), bf)
-    parts = PART // TILE
-
-    def pass_b(*accs):
-        for b in range(total // PART):
-
-            @pl.loop(0, keys // TILE // UNROLL)
-            def _(outer):
-                for w in range(UNROLL):
-                    at = pl.ds(pl.multiple_of((outer * UNROLL + w) * TILE, TILE), TILE)
+
+    def body(*accs):
+        @pl.loop(0, keys // TILE // UNROLL)
+        def _(outer):
+            for w in range(UNROLL):
+                at = pl.ds(pl.multiple_of((outer * UNROLL + w) * TILE, TILE), TILE)
+                for x in range(2):
+                    pltpu.matmul_push_rhs(
+                        jnp.concatenate([vs[x][at, :], ones], axis=1), w % 2, x
+                    )
+                for u in range(parts):
+                    rs = slice(u * TILE, (u + 1) * TILE)
+                    m = m_ref[rs, :]
+                    m = jnp.concatenate([m, m], axis=1)
                     for x in range(2):
-                        pltpu.matmul_push_rhs(
-                            jnp.concatenate([vs[x][at, :], ones], axis=1), w % 2, x
+                        p = jnp.exp2(scores[x][rs, at] - m).astype(bf)
+                        pltpu.matmul_acc_lhs(
+                            accs[x * parts + u], p, load_staged_rhs=w % 2 if u == 0 else None
                         )
-                    for u in range(parts):
-                        rs = slice(b * PART + u * TILE, b * PART + (u + 1) * TILE)
-                        m = m_ref[rs, :]
-                        m = jnp.concatenate([m, m], axis=1)
-                        for x in range(2):
-                            p = jnp.exp2(scores[x][rs, at] - m).astype(bf)
-                            pltpu.matmul_acc_lhs(
-                                accs[x * parts + u], p, load_staged_rhs=w % 2 if u == 0 else None
-                            )
-
-            for u in range(parts):
-                rs = slice(b * PART + u * TILE, b * PART + (u + 1) * TILE)
-                o_ref[rs, :] = pltpu.matmul_pop(accs[u]) + pltpu.matmul_pop(accs[parts + u])
-
-    pl.run_scoped(pass_b, *[accumulator(i // parts, TILE) for i in range(2 * parts)])
+
+        for u in range(parts):
+            rs = slice(u * TILE, (u + 1) * TILE)
+            o_ref[rs, :] = pltpu.matmul_pop(accs[u]) + pltpu.matmul_pop(accs[parts + u])
+
+    pl.run_scoped(body, *[accumulator(i // parts, TILE) for i in range(2 * parts)])
+
+
+def near_kernel(
+    c, q_ref, ko_ref, kp_ref, vo_ref, vp_ref, o_ref, m_ref, q2, s_o, s_p, k_buf, v_buf, sems
+):
+    get_k = pltpu.make_async_copy(ko_ref, k_buf, sems.at[0])
+    get_v = pltpu.make_async_copy(vo_ref, v_buf, sems.at[1])
+    get_k.start()
+    get_v.start()
+    scaled_queries(c, q_ref, q2)
+    m_ref[...] = jnp.full(m_ref.shape, -jnp.inf, jnp.float32)
+    get_k.wait()
+    score_pass(q2, (k_buf, kp_ref), (s_o, s_p), m_ref)
+    get_v.wait()
+    mix_pass((v_buf, vp_ref), (s_o, s_p), m_ref, o_ref)
+
+
+def far_kernel(
+    c, q_ref, ko_ref, kp_ref, vo_ref, vp_ref, o1_ref, m1_ref, out_ref, q2, s_o, s_p, m_ref, o_ref
+):
+    n, rows, hd = q_ref.shape
+    f, bf = jnp.float32, jnp.bfloat16
+    scaled_queries(c, q_ref, q2)
+    m_ref[...] = m1_ref[...]
+    score_pass(q2, (ko_ref, kp_ref), (s_o, s_p), m_ref)
+    mix_pass((vo_ref, vp_ref), (s_o, s_p), m_ref, o_ref)
 
     lane = lax.broadcasted_iota(jnp.int32, (rows, 128), 1)
     table = jnp.zeros((rows, 128), f)
     for i in range(n):
         rs = slice(i * rows, (i + 1) * rows)
-        out_ref[i, :rows, :] = o_ref[rs, :hd].astype(bf)
-        t, m = o_ref[rs, hd:], m_ref[rs, :]
+        m = m_ref[rs, :]
+        a = jnp.exp2(m1_ref[rs, :] - m)
+        out_ref[i, :rows, :] = (o_ref[rs, :hd] + a * o1_ref[rs, :hd]).astype(bf)
+        t = o_ref[rs, hd:] + a * o1_ref[rs, hd:]
         hi, t_hi = m.astype(bf).astype(f), t.astype(bf).astype(f)
         for l, v in enumerate((hi, m - hi, t_hi, t - t_hi)):
             table = jnp.where(lane == STATS * i + l, v, table)
@@ -147,7 +179,7 @@
 
 
 def suffix_kernel(c, heads, len_ref, q_ref, k_ref, v_ref, out_ref):
-    forks, slots, hd = k_ref.shape
+    forks, slots, _ = k_ref.shape
     rows = q_ref.shape[0] // forks
     his, los, tots = [], [], []
     for f in range(forks):
@@ -230,7 +262,7 @@
     return [pl.BlockSpec(memory_space=VMEM)] * n
 
 
-def shards(q, pk, pv, sk, sv, lengths, w):
+def body(q, pk, pv, sk, sv, lengths, w):
     forks, steps, heads, hd = q.shape
     rows = forks * steps * heads
     keys = pk.shape[0]
@@ -242,13 +274,19 @@
     bf = jnp.bfloat16
     swap = [(0, 1), (1, 0)]
 
-    q = q.reshape(rows, hd)
-    every = lax.all_to_all(
-        jnp.broadcast_to(q[None], (chips, rows, hd)), CHIPS, 0, 0, tiled=True
-    )
     k_own, v_own = pk.reshape(keys, hd), pv.reshape(keys, hd)
+    k_far = lax.ppermute(k_own, "xh", swap)
+    v_far = lax.ppermute(v_own, "xh", swap)
     k_pair = lax.ppermute(k_own, "core", swap)
     v_pair = lax.ppermute(v_own, "core", swap)
+    q = q.reshape(rows, hd)
+    ring = lax.axis_size("z")
+    every = lax.all_to_all(
+        jnp.broadcast_to(q[None], (ring, rows, hd)), "z", 0, 0, tiled=True
+    )
+    every, k_far = lax.optimization_barrier((every, k_far))
+    k_far_pair = lax.ppermute(k_far, "core", swap)
+    every, k_far_pair = lax.optimization_barrier((every, k_far_pair))
 
     own = pl.pallas_call(
         functools.partial(suffix_kernel, c, heads),
@@ -262,12 +300,42 @@
         name="suffix",
     )(lengths, q, sk.reshape(forks, slots, hd), sv.reshape(forks, slots, hd))
 
-    total = chips * rows
+    total = ring * rows
     f = jnp.float32
+    near = pl.pallas_call(
+        functools.partial(near_kernel, c),
+        out_shape=[
+            jax.ShapeDtypeStruct((total, TILE), f),
+            jax.ShapeDtypeStruct((total, 128), f),
+        ],
+        in_specs=[
+            pl.BlockSpec(memory_space=VMEM),
+            pl.BlockSpec(memory_space=pltpu.HBM),
+            pl.BlockSpec(memory_space=VMEM),
+            pl.BlockSpec(memory_space=pltpu.HBM),
+            pl.BlockSpec(memory_space=VMEM),
+        ],
+        out_specs=whole(2),
+        scratch_shapes=[
+            VMEM((total, TILE), bf),
+            VMEM((total, keys), f),
+            VMEM((total, keys), f),
+            VMEM((keys, hd), bf),
+            VMEM((keys, hd), bf),
+            pltpu.SemaphoreType.DMA((2,)),
+        ],
+        compiler_params=pltpu.CompilerParams(vmem_limit_bytes=20 * 2**20),
+        cost_estimate=pl.CostEstimate(
+            flops=8 * total * keys * hd, bytes_accessed=8 * keys * hd, transcendentals=2 * total * keys
+        ),
+        name="near",
+    )(every, k_own, k_pair, v_own, v_pair)
+    o1, m1, v_far = lax.optimization_barrier((*near, v_far))
+    v_far_pair = lax.ppermute(v_far, "core", swap)
     states = pl.pallas_call(
-        functools.partial(prefix_kernel, c),
-        out_shape=jax.ShapeDtypeStruct((chips, rows + STATS, hd), bf),
-        in_specs=whole(5),
+        functools.partial(far_kernel, c),
+        out_shape=jax.ShapeDtypeStruct((ring, rows + STATS, hd), bf),
+        in_specs=whole(7),
         out_specs=pl.BlockSpec(memory_space=VMEM),
         scratch_shapes=[
             VMEM((total, TILE), bf),
@@ -276,11 +344,14 @@
             VMEM((total, 128), f),
             VMEM((total, TILE), f),
         ],
-        compiler_params=pltpu.CompilerParams(vmem_limit_bytes=36 * 2**20),
-        name="prefix",
-    )(every, k_own, k_pair, v_own, v_pair)
-
-    got = lax.all_to_all(states, CHIPS, 0, 0, tiled=True)
+        compiler_params=pltpu.CompilerParams(vmem_limit_bytes=22 * 2**20),
+        cost_estimate=pl.CostEstimate(
+            flops=8 * total * keys * hd, bytes_accessed=8 * keys * hd, transcendentals=2 * total * keys
+        ),
+        name="far",
+    )(every, k_far, k_far_pair, v_far, v_far_pair, o1, m1)
+
+    got = lax.all_to_all(states, "z", 0, 0, tiled=True)
     att = pl.pallas_call(
         combine_kernel,
         out_shape=jax.ShapeDtypeStruct((chips, rows, hd), bf),
@@ -321,7 +392,7 @@
         CTX + TP,
     )
     return jax.shard_map(
-        shards,
+        body,
         mesh=fine,
         in_specs=(
             P(CTX, None, TP, None),

time: 90.5 us -> 92.9 us (1.027)
  blocking collectives: 28 us -> 41.4 us
  starting transfers between devices: 22.2 us -> 14.4 us
  waiting for transfers between devices: 23.8 us -> 20.4 us
  Pallas kernels: 12.3 us -> 13.4 us
    all_to_all x2 -> x1, starting transfers between devices: 18.2 us -> 3.53 us  [body(): got = lax.all_to_all(states, 'z', 0, 0, tiled=True)]
    all_to_all x2 -> x3, blocking collectives: 28 us -> 41.4 us  [the longest x1 16.6 us: body(): lax.all_to_all(jnp.broadcast_to(q[None], (ring, rows, hd)), 'z', 0, 0, ti...]
    all_to_all x2 -> x1, waiting for transfers between devices: 20.1 us -> 9.33 us  [body(): got = lax.all_to_all(states, 'z', 0, 0, tiled=True)]
    ppermute x3 -> x7, waiting for transfers between devices: 3.74 us -> 11 us  [the longest x1 5.86 us: body(): v_far = lax.ppermute(v_own, 'xh', swap)]
    ppermute x3 -> x7, starting transfers between devices: 3.99 us -> 10.9 us  [the longest x1 3.56 us: body(): k_far = lax.ppermute(k_own, 'xh', swap)]
    pallas_call x5 -> x6, Pallas kernels: 12.3 us -> 13.4 us  [the longest x1 5.54 us: body(): pl.pallas_call(functools.partial(far_kernel, c), out_shape=jax.ShapeDtype...]
  transfers between devices with their start and end apart: 5 -> 8, of which waited for: 5 -> 7; matrix products, arithmetic and copies ran while one was open for 0% -> 1% of each run, Pallas kernels for 2% -> 7%
where the time goes in v3:
time: 92.9 us; the launch traced here: 92.5 us
  blocking collectives  41.4 us (45%)
  waiting for transfers between devices  20.4 us (22%)
  starting transfers between devices  14.4 us (16%)
  Pallas kernels  13.4 us (14%)
  local copies, waits for them, and re-layouts  2.86 us (3%)
    all_to_all x1, blocking collectives, body(): lax.all_to_all(jnp.broadcast_to(q[None], (ring, rows, hd)), 'z', 0, 0, ti...  16.6 us
    all_to_all x1, blocking collectives, body(): att = lax.all_to_all(att, CHIPS, 0, 0, tiled=True)  14.9 us
    all_to_all x1, blocking collectives, body(): parts = lax.all_to_all(product, TP, 0, 0, tiled=True)  9.93 us
    all_to_all x1, waiting for transfers between devices, body(): got = lax.all_to_all(states, 'z', 0, 0, tiled=True)  9.33 us
    ppermute x1, waiting for transfers between devices, body(): v_far = lax.ppermute(v_own, 'xh', swap)  5.86 us
    pallas_call x1, Pallas kernels, body(): pl.pallas_call(functools.partial(far_kernel, c), out_shape=jax.ShapeDtype...  5.54 us
    pallas_call x1, Pallas kernels, body(): pl.pallas_call(functools.partial(near_kernel, c), out_shape=[jax.ShapeDty...  4.72 us
    ppermute x1, starting transfers between devices, body(): k_far = lax.ppermute(k_own, 'xh', swap)  3.56 us
  transfers between devices with their start and end apart: 8, of which 7 were waited for; matrix products, arithmetic and copies ran while one was open for 1% of the time, Pallas kernels for 7%

profile of v3, /device:TPU:1, one launch (start us, length us, event | category | flops | bytes accessed | tf_op | source)
XLA Modules:
  0.0 92.5 jit_solution(9724309569697435154)
XLA Ops:
  0.0 3.6 %collective-permute-start = (bf16[2048,128]{1,0:T(8,128)(2,1)}, bf16[2048,128]{1,0:T(8,128)(2,1)S(1)}, u32[]{:S(2)}, u32[]{:S(2)}) collective-permute-start(bf16[2048,128]{1,0:T(8,128)(2,1)} %bitcast.11), channel_id=1, source_target_pairs={{0,128},{128,0},{1,129},{129,1},{2,130},{130,2},{3,131},{131,3},{4... | collective-permute-start | bytes 1572872 | tf_op jit(solution)/shard_map/ppermute | solution.py:278
  3.6 0.8 broadcast_in_dim.8
  4.3 16.6 %all_to_all.20.q_ref = bf16[8,96,128]{2,1,0:T(8,128)(2,1)S(1)} all-to-all(bf16[8,96,128]{2,1,0:T(8,128)(2,1)S(1)} %broadcast_in_dim.8), channel_id=1, replica_groups=mesh['xh'=2,'z'=8,'core'=2,'xl'=2,'y'=4] {'z'}, dimensions={0} | all-to-all | bytes 393216 | tf_op jit(solution)/shard_map/all_to_all | solution.py:284
  20.9 0.0 collective-permute-done.ko_ref
  20.9 2.8 %collective-permute-start.1 = (bf16[2048,128]{1,0:T(8,128)(2,1)S(1)}, bf16[2048,128]{1,0:T(8,128)(2,1)S(1)}, u32[]{:S(2)}, u32[]{:S(2)}) collective-permute-start(bf16[2048,128]{1,0:T(8,128)(2,1)S(1)} %collective-permute-done.ko_ref), channel_id=1, source_target_pairs={{0,8},{8,0},{1,9},{9,1},{2,10},{10,2},{3,11},{11,3},{4,12},{12,4},... | collective-permute-start | bytes 1572872 | tf_op jit(solution)/shard_map/ppermute | solution.py:288
  23.7 0.0 collective-permute-start.2
  23.7 0.5 collective-permute-start.3
  24.3 0.2 collective-permute-start.4
  24.5 0.8 collective-permute-done.1.kp_ref
  25.3 0.7 collective-permute-done.2.kp_ref
  26.0 0.7 collective-permute-done.3.vp_ref
  26.8 0.0 copy-start.5
  26.8 1.0 %copy-done.5 = bf16[2048,1,128]{2,0,1:T(8,128)(2,1)S(1)} copy-done((bf16[2048,1,128]{2,0,1:T(8,128)(2,1)S(1)}, bf16[2048,1,128]{2,0,1:T(8,128)(2,1)}, u32[]{:S(2)}) %copy-start.5) | copy-done | bytes 524312
  27.8 0.0 copy-start.6
  27.8 1.0 %copy-done.6 = bf16[2048,1,128]{2,0,1:T(8,128)(2,1)S(1)} copy-done((bf16[2048,1,128]{2,0,1:T(8,128)(2,1)S(1)}, bf16[2048,1,128]{2,0,1:T(8,128)(2,1)}, u32[]{:S(2)}) %copy-start.6) | copy-done | bytes 524312
  28.9 4.7 %near.1 = (f32[768,256]{1,0:T(8,128)S(1)}, f32[768,128]{1,0:T(8,128)S(1)}) custom-call(bf16[8,96,128]{2,1,0:T(8,128)(2,1)S(1)} %all_to_all.20.q_ref, bf16[2048,128]{1,0:T(8,128)(2,1)S(1)} %bitcast.13, bf16[2048,128]{1,0:T(8,128)(2,1)S(1)} %collective-permute-done.2.kp_ref, bf16[2048,128]{1,0:T(8,128)(2,1)S(1)} %bitcast.16, ...), custom_call_target="tpu_custom_call" | custom-call | flops 1610612736 | bytes 2097152 | tf_op jit(solution)/shard_map/near/pallas_call | solution.py:305
  33.6 5.9 %collective-permute-done.4.vo_ref = bf16[2048,128]{1,0:T(8,128)(2,1)S(1)} collective-permute-done((bf16[2048,128]{1,0:T(8,128)(2,1)}, bf16[2048,128]{1,0:T(8,128)(2,1)S(1)}, u32[]{:S(2)}, u32[]{:S(2)}) %collective-permute-start.4) | collective-permute-done | bytes 524320 | tf_op jit(solution)/shard_map/ppermute | solution.py:279
  39.4 0.0 copy-start.1
  39.5 0.0 copy-start.2
  39.5 0.0 copy-start.3
  39.5 0.0 copy-start.4
  39.5 0.9 %collective-permute-start.5 = (bf16[2048,128]{1,0:T(8,128)(2,1)S(1)}, bf16[2048,128]{1,0:T(8,128)(2,1)S(1)}, u32[]{:S(2)}, u32[]{:S(2)}) collective-permute-start(bf16[2048,128]{1,0:T(8,128)(2,1)S(1)} %collective-permute-done.4.vo_ref), channel_id=1, source_target_pairs={{0,8},{8,0},{1,9},{9,1},{2,10},{10,2},{3,11},{11,3},{4,12},{12,4},... | collective-permute-start | bytes 1572872 | tf_op jit(solution)/shard_map/ppermute | solution.py:334
  40.4 1.5 %collective-permute-done.5.vp_ref = bf16[2048,128]{1,0:T(8,128)(2,1)S(1)} collective-permute-done((bf16[2048,128]{1,0:T(8,128)(2,1)S(1)}, bf16[2048,128]{1,0:T(8,128)(2,1)S(1)}, u32[]{:S(2)}, u32[]{:S(2)}) %collective-permute-start.5) | collective-permute-done | bytes 524320 | tf_op jit(solution)/shard_map/ppermute | solution.py:334
  41.9 5.5 %far.1 = bf16[8,104,128]{2,1,0:T(8,128)(2,1)} custom-call(bf16[8,96,128]{2,1,0:T(8,128)(2,1)S(1)} %all_to_all.20.q_ref, bf16[2048,128]{1,0:T(8,128)(2,1)S(1)} %collective-permute-done.ko_ref, bf16[2048,128]{1,0:T(8,128)(2,1)S(1)} %collective-permute-done.1.kp_ref, bf16[2048,128]{1,0:T(8,128)(2,1)S(1)} %collective-permute-done.4.vo_ref, ...), custom_call_target="tpu_custom_call" | custom-call | flops 1610612736 | bytes 2097152 | tf_op jit(solution)/shard_map/far/pallas_call | solution.py:335
  47.5 0.0 copy-start
  47.5 3.5 %all-to-all-start.1 = ((bf16[8,104,128]{2,1,0:T(8,128)(2,1)}), bf16[8,104,128]{2,1,0:T(8,128)(2,1)S(1)}, u32[]{:S(2)}, u32[]{:S(2)}) async-start(bf16[8,104,128]{2,1,0:T(8,128)(2,1)} %far.1), calls=%async_computation.1 | async-start | bytes 425984 | tf_op jit(solution)/shard_map/all_to_all | solution.py:354
  51.0 0.0 copy-done.1
  51.0 0.0 copy-done.2
  51.0 0.0 copy-done.3
  51.1 0.0 copy-done.4
  51.1 1.4 %suffix.1.own_ref = bf16[104,128]{1,0:T(8,128)(2,1)S(1)} custom-call(s32[2]{0:T(128)S(1)} %copy-done.4, bf16[96,128]{1,0:T(8,128)(2,1)S(1)} %bitcast.10, bf16[2,512,128]{2,1,0:T(8,128)(2,1)S(1)} %bitcast.7, bf16[2,512,128]{2,1,0:T(8,128)(2,1)S(1)} %bitcast.8), custom_call_target="tpu_custom_call" | custom-call | flops 25165824 | bytes 524288 | tf_op jit(solution)/shard_map/suffix/pallas_call | solution.py:291
  52.4 9.3 %all-to-all-done.1.got_ref = bf16[8,104,128]{2,1,0:T(8,128)(2,1)S(1)} async-done(((bf16[8,104,128]{2,1,0:T(8,128)(2,1)}), bf16[8,104,128]{2,1,0:T(8,128)(2,1)S(1)}, u32[]{:S(2)}, u32[]{:S(2)}) %all-to-all-start.1) | async-done | bytes 213024 | tf_op jit(solution)/shard_map/all_to_all | solution.py:354
  61.8 0.4 combine.1
  62.1 14.9 %all_to_all.21.own_ref = bf16[16,96,128]{2,1,0:T(8,128)(2,1)S(1)} all-to-all(bf16[16,96,128]{2,1,0:T(8,128)(2,1)S(1)} %combine.1), channel_id=1, replica_groups=mesh['xh'=2,'z'=8,'core'=2,'xl'=2,'y'=4] {'xh','z'}, dimensions={0} | all-to-all | bytes 786432 | tf_op jit(solution)/shard_map/all_to_all | solution.py:364
  77.0 2.8 %collective-permute-start.6 = (bf16[16,96,128]{2,1,0:T(8,128)(2,1)S(1)}, bf16[16,96,128]{2,1,0:T(8,128)(2,1)S(1)}, u32[]{:S(2)}, u32[]{:S(2)}) collective-permute-start(bf16[16,96,128]{2,1,0:T(8,128)(2,1)S(1)} %all_to_all.21.own_ref), channel_id=1, source_target_pairs={{0,8},{8,0},{1,9},{9,1},{2,10},{10,2},{3,11},{11,3},{4,12},{12,4},... | collective-permute-start | bytes 1179656 | tf_op jit(solution)/shard_map/ppermute | solution.py:365
  79.8 1.3 %collective-permute-done.6.other_ref = bf16[16,96,128]{2,1,0:T(8,128)(2,1)S(1)} collective-permute-done((bf16[16,96,128]{2,1,0:T(8,128)(2,1)S(1)}, bf16[16,96,128]{2,1,0:T(8,128)(2,1)S(1)}, u32[]{:S(2)}, u32[]{:S(2)}) %collective-permute-start.6) | collective-permute-done | bytes 393248 | tf_op jit(solution)/shard_map/ppermute | solution.py:365
  81.2 0.0 copy-done
  81.2 0.8 project.1
  81.9 9.9 %all_to_all.22.parts_ref = bf16[8,3,8,512]{3,2,1,0:T(8,128)(2,1)S(1)} all-to-all(bf16[8,3,8,512]{3,2,1,0:T(8,128)(2,1)S(1)} %project.1), channel_id=1, replica_groups=mesh['xh'=2,'z'=8,'core'=2,'xl'=2,'y'=4] {'xl','y'}, dimensions={0} | all-to-all | bytes 393216 | tf_op jit(solution)/shard_map/all_to_all | solution.py:377
  91.9 0.6 total.1
Async XLA Ops:
  0.0 20.9 %collective-permute-start = (bf16[2048,128]{1,0:T(8,128)(2,1)}, bf16[2048,128]{1,0:T(8,128)(2,1)S(1)}, u32[]{:S(2)}, u32[]{:S(2)}) collective-permute-start(bf16[2048,128]{1,0:T(8,128)(2,1)} %bitcast.11), channel_id=1, source_target_pairs={{0,128},{128,0},{1,129},{129,1},{2,130},{130,2},{3,131},{131,3},{4... | collective-permute-start | bytes 1572872 | tf_op jit(solution)/shard_map/ppermute | solution.py:278
  20.9 4.4 %collective-permute-start.1 = (bf16[2048,128]{1,0:T(8,128)(2,1)S(1)}, bf16[2048,128]{1,0:T(8,128)(2,1)S(1)}, u32[]{:S(2)}, u32[]{:S(2)}) collective-permute-start(bf16[2048,128]{1,0:T(8,128)(2,1)S(1)} %collective-permute-done.ko_ref), channel_id=1, source_target_pairs={{0,8},{8,0},{1,9},{9,1},{2,10},{10,2},{3,11},{11,3},{4,12},{12,4},... | collective-permute-start | bytes 1572872 | tf_op jit(solution)/shard_map/ppermute | solution.py:288
  23.7 2.3 %collective-permute-start.2 = (bf16[2048,128]{1,0:T(8,128)(2,1)}, bf16[2048,128]{1,0:T(8,128)(2,1)S(1)}, u32[]{:S(2)}, u32[]{:S(2)}) collective-permute-start(bf16[2048,128]{1,0:T(8,128)(2,1)} %bitcast.12), channel_id=1, source_target_pairs={{0,8},{8,0},{1,9},{9,1},{2,10},{10,2},{3,11},{11,3},{4,12},{12,4},... | collective-permute-start | bytes 1572872 | tf_op jit(solution)/shard_map/ppermute | solution.py:280
  23.7 3.0 %collective-permute-start.3 = (bf16[2048,128]{1,0:T(8,128)(2,1)}, bf16[2048,128]{1,0:T(8,128)(2,1)S(1)}, u32[]{:S(2)}, u32[]{:S(2)}) collective-permute-start(bf16[2048,128]{1,0:T(8,128)(2,1)} %bitcast.14), channel_id=1, source_target_pairs={{0,8},{8,0},{1,9},{9,1},{2,10},{10,2},{3,11},{11,3},{4,12},{12,4},... | collective-permute-start | bytes 1572872 | tf_op jit(solution)/shard_map/ppermute | solution.py:281
  24.3 15.2 %collective-permute-start.4 = (bf16[2048,128]{1,0:T(8,128)(2,1)}, bf16[2048,128]{1,0:T(8,128)(2,1)S(1)}, u32[]{:S(2)}, u32[]{:S(2)}) collective-permute-start(bf16[2048,128]{1,0:T(8,128)(2,1)} %bitcast.15), channel_id=1, source_target_pairs={{0,128},{128,0},{1,129},{129,1},{2,130},{130,2},{3,131},{131,3},{4... | collective-permute-start | bytes 1572872 | tf_op jit(solution)/shard_map/ppermute | solution.py:279
  26.8 1.0 %copy-start.5 = (bf16[2048,1,128]{2,0,1:T(8,128)(2,1)S(1)}, bf16[2048,1,128]{2,0,1:T(8,128)(2,1)}, u32[]{:S(2)}) copy-start(bf16[2048,1,128]{2,0,1:T(8,128)(2,1)} %param.8) | copy-start | bytes 1572868
  27.8 1.0 %copy-start.6 = (bf16[2048,1,128]{2,0,1:T(8,128)(2,1)S(1)}, bf16[2048,1,128]{2,0,1:T(8,128)(2,1)}, u32[]{:S(2)}) copy-start(bf16[2048,1,128]{2,0,1:T(8,128)(2,1)} %param.9) | copy-start | bytes 1572868
  39.4 11.6 %copy-start.1 = (bf16[2,512,1,128]{3,1,2,0:T(8,128)(2,1)S(1)}, bf16[2,512,1,128]{3,1,2,0:T(8,128)(2,1)}, u32[]{:S(2)}) copy-start(bf16[2,512,1,128]{3,1,2,0:T(8,128)(2,1)} %param.10) | copy-start | bytes 786436
  39.5 11.6 %copy-start.2 = (bf16[2,512,1,128]{3,1,2,0:T(8,128)(2,1)S(1)}, bf16[2,512,1,128]{3,1,2,0:T(8,128)(2,1)}, u32[]{:S(2)}) copy-start(bf16[2,512,1,128]{3,1,2,0:T(8,128)(2,1)} %param.11) | copy-start | bytes 786436
  39.5 11.6 %copy-start.3 = (bf16[2,3,16,128]{3,2,1,0:T(8,128)(2,1)S(1)}, bf16[2,3,16,128]{3,2,1,0:T(8,128)(2,1)}, u32[]{:S(2)}) copy-start(bf16[2,3,16,128]{3,2,1,0:T(8,128)(2,1)} %param.7) | copy-start | bytes 73732
  39.5 11.6 %copy-start.4 = (s32[2]{0:T(128)S(1)}, s32[2]{0:T(128)}, u32[]{:S(2)}) copy-start(s32[2]{0:T(128)} %len_ref.1) | copy-start | bytes 28
  39.5 2.5 %collective-permute-start.5 = (bf16[2048,128]{1,0:T(8,128)(2,1)S(1)}, bf16[2048,128]{1,0:T(8,128)(2,1)S(1)}, u32[]{:S(2)}, u32[]{:S(2)}) collective-permute-start(bf16[2048,128]{1,0:T(8,128)(2,1)S(1)} %collective-permute-done.4.vo_ref), channel_id=1, source_target_pairs={{0,8},{8,0},{1,9},{9,1},{2,10},{10,2},{3,11},{11,3},{4,12},{12,4},... | collective-permute-start | bytes 1572872 | tf_op jit(solution)/shard_map/ppermute | solution.py:334
  47.5 33.7 %copy-start = (bf16[2048,512]{1,0:T(8,128)(2,1)S(1)}, bf16[2048,512]{1,0:T(8,128)(2,1)}, u32[]{:S(2)}) copy-start(bf16[2048,512]{1,0:T(8,128)(2,1)} %w_ref.1) | copy-start | bytes 6291460
  47.5 14.3 %all-to-all-start.1 = ((bf16[8,104,128]{2,1,0:T(8,128)(2,1)}), bf16[8,104,128]{2,1,0:T(8,128)(2,1)S(1)}, u32[]{:S(2)}, u32[]{:S(2)}) async-start(bf16[8,104,128]{2,1,0:T(8,128)(2,1)} %far.1), calls=%async_computation.1 | async-start | bytes 425984 | tf_op jit(solution)/shard_map/all_to_all | solution.py:354
  77.0 4.2 %collective-permute-start.6 = (bf16[16,96,128]{2,1,0:T(8,128)(2,1)S(1)}, bf16[16,96,128]{2,1,0:T(8,128)(2,1)S(1)}, u32[]{:S(2)}, u32[]{:S(2)}) collective-permute-start(bf16[16,96,128]{2,1,0:T(8,128)(2,1)S(1)} %all_to_all.21.own_ref), channel_id=1, source_target_pairs={{0,8},{8,0},{1,9},{9,1},{2,10},{10,2},{3,11},{11,3},{4,12},{12,4},... | collective-permute-start | bytes 1179656 | tf_op jit(solution)/shard_map/ppermute | solution.py:365

commit v4 on v3

--- a/solution.py
+++ b/solution.py
@@ -137,30 +137,36 @@
     pl.run_scoped(body, *[accumulator(i // parts, TILE) for i in range(2 * parts)])
 
 
-def near_kernel(
-    c, q_ref, ko_ref, kp_ref, vo_ref, vp_ref, o_ref, m_ref, q2, s_o, s_p, k_buf, v_buf, sems
-):
-    get_k = pltpu.make_async_copy(ko_ref, k_buf, sems.at[0])
-    get_v = pltpu.make_async_copy(vo_ref, v_buf, sems.at[1])
-    get_k.start()
-    get_v.start()
+def near_kernel(c, q_ref, ko_ref, kp_ref, vo_ref, vp_ref, o_ref, m_ref, q2, s_o, s_p):
     scaled_queries(c, q_ref, q2)
     m_ref[...] = jnp.full(m_ref.shape, -jnp.inf, jnp.float32)
-    get_k.wait()
-    score_pass(q2, (k_buf, kp_ref), (s_o, s_p), m_ref)
-    get_v.wait()
-    mix_pass((v_buf, vp_ref), (s_o, s_p), m_ref, o_ref)
+    score_pass(q2, (ko_ref, kp_ref), (s_o, s_p), m_ref)
+    mix_pass((vo_ref, vp_ref), (s_o, s_p), m_ref, o_ref)
+
+
+def halves(ref):
+    half = ref.shape[0] // 2
+    return ref.at[:half], ref.at[half:]
+
+
+def next_kernel(c, q_ref, k_ref, v_ref, o1_ref, m1_ref, o_ref, m_ref, q2, s_o, s_p):
+    scaled_queries(c, q_ref, q2)
+    m_ref[...] = m1_ref[...]
+    score_pass(q2, halves(k_ref), (s_o, s_p), m_ref)
+    mix_pass(halves(v_ref), (s_o, s_p), m_ref, o_ref)
+    a = jnp.exp2(m1_ref[...] - m_ref[...])
+    o_ref[...] = o_ref[...] + jnp.concatenate([a, a], axis=1) * o1_ref[...]
 
 
 def far_kernel(
-    c, q_ref, ko_ref, kp_ref, vo_ref, vp_ref, o1_ref, m1_ref, out_ref, q2, s_o, s_p, m_ref, o_ref
+    c, q_ref, k_ref, v_ref, o1_ref, m1_ref, out_ref, q2, s_o, s_p, m_ref, o_ref
 ):
     n, rows, hd = q_ref.shape
     f, bf = jnp.float32, jnp.bfloat16
     scaled_queries(c, q_ref, q2)
     m_ref[...] = m1_ref[...]
-    score_pass(q2, (ko_ref, kp_ref), (s_o, s_p), m_ref)
-    mix_pass((vo_ref, vp_ref), (s_o, s_p), m_ref, o_ref)
+    score_pass(q2, halves(k_ref), (s_o, s_p), m_ref)
+    mix_pass(halves(v_ref), (s_o, s_p), m_ref, o_ref)
 
     lane = lax.broadcasted_iota(jnp.int32, (rows, 128), 1)
     table = jnp.zeros((rows, 128), f)
@@ -178,7 +184,13 @@
         out_ref[i, rows:, :] = turned[STATS * i : STATS * (i + 1)].astype(bf)
 
 
-def suffix_kernel(c, heads, len_ref, q_ref, k_ref, v_ref, out_ref):
+def suffix_kernel(
+    c, heads, len_ref, q_ref, k_ref, v_ref, pk_ref, pv_ref, out_ref, k_out, v_out, sems
+):
+    get_k = pltpu.make_async_copy(pk_ref, k_out, sems.at[0])
+    get_v = pltpu.make_async_copy(pv_ref, v_out, sems.at[1])
+    get_k.start()
+    get_v.start()
     forks, slots, _ = k_ref.shape
     rows = q_ref.shape[0] // forks
     his, los, tots = [], [], []
@@ -198,6 +210,8 @@
         tots.append(jnp.sum(p, axis=1, keepdims=True))
     cat = functools.partial(jnp.concatenate, axis=0)
     out_ref[forks * rows :, :] = stat_rows(cat(his), cat(los), cat(tots))
+    get_k.wait()
+    get_v.wait()
 
 
 def combine_kernel(got_ref, own_ref, out_ref):
@@ -284,72 +298,66 @@
     every = lax.all_to_all(
         jnp.broadcast_to(q[None], (ring, rows, hd)), "z", 0, 0, tiled=True
     )
-    every, k_far = lax.optimization_barrier((every, k_far))
-    k_far_pair = lax.ppermute(k_far, "core", swap)
-    every, k_far_pair = lax.optimization_barrier((every, k_far_pair))
-
-    own = pl.pallas_call(
+    hbm = pl.BlockSpec(memory_space=pltpu.HBM)
+    own, k_held, v_held = pl.pallas_call(
         functools.partial(suffix_kernel, c, heads),
-        out_shape=jax.ShapeDtypeStruct((rows + STATS, hd), bf),
-        in_specs=[pl.BlockSpec(memory_space=pltpu.SMEM)] + whole(3),
-        out_specs=pl.BlockSpec(memory_space=VMEM),
+        out_shape=[
+            jax.ShapeDtypeStruct((rows + STATS, hd), bf),
+            jax.ShapeDtypeStruct((keys, hd), bf),
+            jax.ShapeDtypeStruct((keys, hd), bf),
+        ],
+        in_specs=[pl.BlockSpec(memory_space=pltpu.SMEM)] + whole(3) + [hbm, hbm],
+        out_specs=whole(3),
+        scratch_shapes=[pltpu.SemaphoreType.DMA((2,))],
         cost_estimate=pl.CostEstimate(
-            flops=4 * rows * slots * hd, bytes_accessed=4 * forks * slots * hd, transcendentals=rows * slots
+            flops=4 * rows * slots * hd,
+            bytes_accessed=4 * forks * slots * hd,
+            transcendentals=rows * slots,
         ),
-        compiler_params=pltpu.CompilerParams(vmem_limit_bytes=4 * 2**20),
+        compiler_params=pltpu.CompilerParams(vmem_limit_bytes=6 * 2**20),
         name="suffix",
-    )(lengths, q, sk.reshape(forks, slots, hd), sv.reshape(forks, slots, hd))
+    )(
+        lengths,
+        q,
+        sk.reshape(forks, slots, hd),
+        sv.reshape(forks, slots, hd),
+        k_own,
+        v_own,
+    )
 
     total = ring * rows
     f = jnp.float32
-    near = pl.pallas_call(
-        functools.partial(near_kernel, c),
-        out_shape=[
-            jax.ShapeDtypeStruct((total, TILE), f),
-            jax.ShapeDtypeStruct((total, 128), f),
-        ],
-        in_specs=[
-            pl.BlockSpec(memory_space=VMEM),
-            pl.BlockSpec(memory_space=pltpu.HBM),
-            pl.BlockSpec(memory_space=VMEM),
-            pl.BlockSpec(memory_space=pltpu.HBM),
-            pl.BlockSpec(memory_space=VMEM),
-        ],
-        out_specs=whole(2),
-        scratch_shapes=[
-            VMEM((total, TILE), bf),
-            VMEM((total, keys), f),
-            VMEM((total, keys), f),
-            VMEM((keys, hd), bf),
-            VMEM((keys, hd), bf),
-            pltpu.SemaphoreType.DMA((2,)),
-        ],
-        compiler_params=pltpu.CompilerParams(vmem_limit_bytes=20 * 2**20),
-        cost_estimate=pl.CostEstimate(
-            flops=8 * total * keys * hd, bytes_accessed=8 * keys * hd, transcendentals=2 * total * keys
-        ),
-        name="near",
-    )(every, k_own, k_pair, v_own, v_pair)
-    o1, m1, v_far = lax.optimization_barrier((*near, v_far))
+
+    def attend(kernel, n_in, key_count, packed, limit):
+        state = [((total, TILE), f), ((total, 128), f)]
+        outs = [((ring, rows + STATS, hd), bf)] if packed else state
+        scratch = [((total, TILE), bf)] + [((total, key_count // 2), f)] * 2
+        if packed:
+            scratch += [state[1], state[0]]
+        return pl.pallas_call(
+            functools.partial(kernel, c),
+            out_shape=[jax.ShapeDtypeStruct(*o) for o in outs],
+            in_specs=whole(n_in),
+            out_specs=whole(len(outs)),
+            scratch_shapes=[VMEM(*x) for x in scratch],
+            compiler_params=pltpu.CompilerParams(vmem_limit_bytes=limit * 2**20),
+            cost_estimate=pl.CostEstimate(
+                flops=4 * total * key_count * hd,
+                bytes_accessed=4 * key_count * hd,
+                transcendentals=total * key_count,
+            ),
+        )
+
+    o1, m1 = attend(near_kernel, 5, 2 * keys, False, 20)(
+        every, k_held, k_pair, v_held, v_pair
+    )
+    o1, m1, k_far, v_far = lax.optimization_barrier((o1, m1, k_far, v_far))
+    k_far_pair = lax.ppermute(k_far, "core", swap)
     v_far_pair = lax.ppermute(v_far, "core", swap)
-    states = pl.pallas_call(
-        functools.partial(far_kernel, c),
-        out_shape=jax.ShapeDtypeStruct((ring, rows + STATS, hd), bf),
-        in_specs=whole(7),
-        out_specs=pl.BlockSpec(memory_space=VMEM),
-        scratch_shapes=[
-            VMEM((total, TILE), bf),
-            VMEM((total, keys), f),
-            VMEM((total, keys), f),
-            VMEM((total, 128), f),
-            VMEM((total, TILE), f),
-        ],
-        compiler_params=pltpu.CompilerParams(vmem_limit_bytes=22 * 2**20),
-        cost_estimate=pl.CostEstimate(
-            flops=8 * total * keys * hd, bytes_accessed=8 * keys * hd, transcendentals=2 * total * keys
-        ),
-        name="far",
-    )(every, k_far, k_far_pair, v_far, v_far_pair, o1, m1)
+    o2, m2 = attend(next_kernel, 5, keys, False, 14)(every, k_far, v_far, o1, m1)
+    (states,) = attend(far_kernel, 5, keys, True, 16)(
+        every, k_far_pair, v_far_pair, o2, m2
+    )
 
     got = lax.all_to_all(states, "z", 0, 0, tiled=True)
     att = pl.pallas_call(

time: 92.9 us -> 85.2 us (0.917)
  waiting for transfers between devices: 20.4 us -> 4.9 us
  local copies, waits for them, and re-layouts: 2.86 us -> 6.82 us
  starting transfers between devices: 14.4 us -> 16.8 us
  blocking collectives: 41.4 us -> 43.5 us
    all_to_all x1, waiting for transfers between devices: 9.33 us -> 1.56 us  [body(): lax.all_to_all(jnp.broadcast_to(q[None], (ring, rows, hd)), 'z', 0, 0, ti...]
    ppermute x1, waiting for transfers between devices: 5.86 us -> 1.92 us  [body(): v_far = lax.ppermute(v_own, 'xh', swap)]
    unnamed x14, local copies, waits for them, and re-layouts: 2.1 us -> 5.37 us
    ppermute x1, starting transfers between devices: 0.01 us -> 3.2 us  [body(): k_pair = lax.ppermute(k_own, 'core', swap)]
    all_to_all x1, starting transfers between devices: 3.53 us -> 6.48 us  [body(): lax.all_to_all(jnp.broadcast_to(q[None], (ring, rows, hd)), 'z', 0, 0, ti...]
    all_to_all x1, blocking collectives: 14.9 us -> 17.7 us  [body(): att = lax.all_to_all(att, CHIPS, 0, 0, tiled=True)]
    ppermute x1, starting transfers between devices: 3.56 us -> 1.04 us  [body(): k_far = lax.ppermute(k_own, 'xh', swap)]
    ppermute x1, starting transfers between devices: 0.23 us -> 1.93 us  [body(): v_far = lax.ppermute(v_own, 'xh', swap)]
  transfers between devices with their start and end apart: 8 -> 8, of which waited for: 7 -> 3; matrix products, arithmetic and copies ran while one was open for 1% -> 2% of each run, Pallas kernels for 7% -> 10%
where the time goes in v4:
time: 85.2 us; the launch traced here: 84.6 us
  blocking collectives  43.5 us (51%)
  starting transfers between devices  16.8 us (20%)
  Pallas kernels  12.5 us (15%)
  local copies, waits for them, and re-layouts  6.82 us (8%)
  waiting for transfers between devices  4.9 us (6%)
    all_to_all x1, blocking collectives, body(): att = lax.all_to_all(att, CHIPS, 0, 0, tiled=True)  17.7 us
    all_to_all x1, blocking collectives, body(): got = lax.all_to_all(states, 'z', 0, 0, tiled=True)  15.9 us
    all_to_all x1, blocking collectives, body(): parts = lax.all_to_all(product, TP, 0, 0, tiled=True)  9.91 us
    all_to_all x1, starting transfers between devices, body(): lax.all_to_all(jnp.broadcast_to(q[None], (ring, rows, hd)), 'z', 0, 0, ti...  6.48 us
    unnamed x14, local copies, waits for them, and re-layouts  5.37 us
    pallas_call x1, Pallas kernels, body(): attend(near_kernel, 5, 2 * keys, False, 20)  4.65 us
    ppermute x1, starting transfers between devices, body(): k_pair = lax.ppermute(k_own, 'core', swap)  3.2 us
    ppermute x1, starting transfers between devices, body(): other = lax.ppermute(att, 'core', swap)  2.8 us
  transfers between devices with their start and end apart: 8, of which 3 were waited for; matrix products, arithmetic and copies ran while one was open for 2% of the time, Pallas kernels for 10%

profile of v4, /device:TPU:1, one launch (start us, length us, event | category | flops | bytes accessed | tf_op | source)
XLA Modules:
  0.0 84.6 jit_solution(2332123099970013117)
XLA Ops:
  0.0 3.2 %collective-permute-start = (bf16[2048,128]{1,0:T(8,128)(2,1)}, bf16[2048,128]{1,0:T(8,128)(2,1)S(1)}, u32[]{:S(2)}, u32[]{:S(2)}) collective-permute-start(bf16[2048,128]{1,0:T(8,128)(2,1)} %bitcast.7), channel_id=1, source_target_pairs={{0,8},{8,0},{1,9},{9,1},{2,10},{10,2},{3,11},{11,3},{4,12},{12,4},... | collective-permute-start | bytes 1572872 | tf_op jit(solution)/shard_map/ppermute | solution.py:294
  3.2 0.0 collective-permute-start.1
  3.2 1.0 %collective-permute-start.2 = (bf16[2048,128]{1,0:T(8,128)(2,1)}, bf16[2048,128]{1,0:T(8,128)(2,1)S(1)}, u32[]{:S(2)}, u32[]{:S(2)}) collective-permute-start(bf16[2048,128]{1,0:T(8,128)(2,1)} %bitcast.8), channel_id=1, source_target_pairs={{0,128},{128,0},{1,129},{129,1},{2,130},{130,2},{3,131},{131,3},{4... | collective-permute-start | bytes 1572872 | tf_op jit(solution)/shard_map/ppermute | solution.py:292
  4.2 1.9 %collective-permute-start.3 = (bf16[2048,128]{1,0:T(8,128)(2,1)}, bf16[2048,128]{1,0:T(8,128)(2,1)S(1)}, u32[]{:S(2)}, u32[]{:S(2)}) collective-permute-start(bf16[2048,128]{1,0:T(8,128)(2,1)} %bitcast.11), channel_id=1, source_target_pairs={{0,128},{128,0},{1,129},{129,1},{2,130},{130,2},{3,131},{131,3},{4... | collective-permute-start | bytes 1572872 | tf_op jit(solution)/shard_map/ppermute | solution.py:293
  6.2 1.5 %broadcast_in_dim.8 = bf16[8,96,128]{2,1,0:T(8,128)(2,1)} broadcast(bf16[96,128]{1,0:T(8,128)(2,1)} %bitcast.15), dimensions={1,2} | broadcast | bytes 221184 | tf_op jit(solution)/shard_map/broadcast_in_dim | solution.py:299
  7.6 6.5 %all-to-all-start = ((bf16[8,96,128]{2,1,0:T(8,128)(2,1)}), bf16[8,96,128]{2,1,0:T(8,128)(2,1)S(1)}, u32[]{:S(2)}, u32[]{:S(2)}) async-start(bf16[8,96,128]{2,1,0:T(8,128)(2,1)} %broadcast_in_dim.8), calls=%async_computation | async-start | bytes 393216 | tf_op jit(solution)/shard_map/all_to_all | solution.py:298
  14.1 0.0 copy-start.1
  14.1 1.0 %copy-done.1 = bf16[2048,1,128]{2,0,1:T(8,128)(2,1)S(1)} copy-done((bf16[2048,1,128]{2,0,1:T(8,128)(2,1)S(1)}, bf16[2048,1,128]{2,0,1:T(8,128)(2,1)}, u32[]{:S(2)}) %copy-start.1) | copy-done | bytes 524312
  15.1 0.0 copy-start.2
  15.1 1.0 %copy-done.2 = bf16[2048,1,128]{2,0,1:T(8,128)(2,1)S(1)} copy-done((bf16[2048,1,128]{2,0,1:T(8,128)(2,1)S(1)}, bf16[2048,1,128]{2,0,1:T(8,128)(2,1)}, u32[]{:S(2)}) %copy-start.2) | copy-done | bytes 524312
  16.2 0.0 copy-start.3
  16.2 0.9 %copy-done.3 = bf16[2,512,1,128]{3,1,2,0:T(8,128)(2,1)S(1)} copy-done((bf16[2,512,1,128]{3,1,2,0:T(8,128)(2,1)S(1)}, bf16[2,512,1,128]{3,1,2,0:T(8,128)(2,1)}, u32[]{:S(2)}) %copy-start.3) | copy-done | bytes 262168
  17.1 0.0 copy-start.4
  17.1 0.9 %copy-done.4 = bf16[2,512,1,128]{3,1,2,0:T(8,128)(2,1)S(1)} copy-done((bf16[2,512,1,128]{3,1,2,0:T(8,128)(2,1)S(1)}, bf16[2,512,1,128]{3,1,2,0:T(8,128)(2,1)}, u32[]{:S(2)}) %copy-start.4) | copy-done | bytes 262168
  18.1 0.0 copy-start.5
  18.1 0.7 copy-done.5
  18.8 0.0 copy-start.6
  18.8 0.7 copy-done.6
  19.5 1.5 %suffix.1 = (bf16[104,128]{1,0:T(8,128)(2,1)S(1)}, bf16[2048,128]{1,0:T(8,128)(2,1)S(1)}, bf16[2048,128]{1,0:T(8,128)(2,1)S(1)}) custom-call(s32[2]{0:T(128)S(1)} %copy-done.6, bf16[96,128]{1,0:T(8,128)(2,1)S(1)} %bitcast.16, bf16[2,512,128]{2,1,0:T(8,128)(2,1)S(1)} %bitcast.13, bf16[2,512,128]{2,1,0:T(8,128)(2,1)S(1)} %bitcast.14, ...), custom_call_target="tpu_custom_call" | custom-call | flops 25165824 | bytes 524288 | tf_op jit(solution)/shard_map/suffix/pallas_call | solution.py:302
  21.0 1.6 %all-to-all-done.q_ref = bf16[8,96,128]{2,1,0:T(8,128)(2,1)S(1)} async-done(((bf16[8,96,128]{2,1,0:T(8,128)(2,1)}), bf16[8,96,128]{2,1,0:T(8,128)(2,1)S(1)}, u32[]{:S(2)}, u32[]{:S(2)}) %all-to-all-start) | async-done | bytes 196640 | tf_op jit(solution)/shard_map/all_to_all | solution.py:298
  22.5 0.0 collective-permute-done.kp_ref
  22.5 0.0 collective-permute-done.1.vp_ref
  22.5 4.6 %shard_map.73 = (f32[768,256]{1,0:T(8,128)S(1)}, f32[768,128]{1,0:T(8,128)S(1)}) custom-call(bf16[8,96,128]{2,1,0:T(8,128)(2,1)S(1)} %all-to-all-done.q_ref, bf16[2048,128]{1,0:T(8,128)(2,1)S(1)} %get-tuple-element.16.ko_ref, bf16[2048,128]{1,0:T(8,128)(2,1)S(1)} %collective-permute-done.kp_ref, bf16[2048,128]{1,0:T(8,128)(2,1)S(1)} %get-tuple-element.17.vo_ref, ...), custom_call_target="tpu_custom_call" | custom-call | flops 1610612736 | bytes 2097152 | tf_op jit(solution)/shard_map/pallas_call | solution.py:351
  27.2 0.0 collective-permute-done.2.k_ref
  27.2 1.9 %collective-permute-done.3.v_ref = bf16[2048,128]{1,0:T(8,128)(2,1)S(1)} collective-permute-done((bf16[2048,128]{1,0:T(8,128)(2,1)}, bf16[2048,128]{1,0:T(8,128)(2,1)S(1)}, u32[]{:S(2)}, u32[]{:S(2)}) %collective-permute-start.3) | collective-permute-done | bytes 524320 | tf_op jit(solution)/shard_map/ppermute | solution.py:293
  29.1 1.4 %collective-permute-start.4 = (bf16[2048,128]{1,0:T(8,128)(2,1)S(1)}, bf16[2048,128]{1,0:T(8,128)(2,1)S(1)}, u32[]{:S(2)}, u32[]{:S(2)}) collective-permute-start(bf16[2048,128]{1,0:T(8,128)(2,1)S(1)} %collective-permute-done.2.k_ref), channel_id=1, source_target_pairs={{0,8},{8,0},{1,9},{9,1},{2,10},{10,2},{3,11},{11,3},{4,12},{12,4},... | collective-permute-start | bytes 1572872 | tf_op jit(solution)/shard_map/ppermute | solution.py:355
  30.5 0.0 collective-permute-start.5
  30.5 2.2 %shard_map.74 = (f32[768,256]{1,0:T(8,128)S(1)}, f32[768,128]{1,0:T(8,128)S(1)}) custom-call(bf16[8,96,128]{2,1,0:T(8,128)(2,1)S(1)} %all-to-all-done.q_ref, bf16[2048,128]{1,0:T(8,128)(2,1)S(1)} %collective-permute-done.2.k_ref, bf16[2048,128]{1,0:T(8,128)(2,1)S(1)} %collective-permute-done.3.v_ref, f32[768,256]{1,0:T(8,128)S(1)} %get-tuple-element.22.o1_ref, ...), custom_call_target="tpu_custom_call" | custom-call | flops 805306368 | bytes 1048576 | tf_op jit(solution)/shard_map/pallas_call | solution.py:357
  32.7 0.0 collective-permute-done.4.k_ref
  32.7 0.0 collective-permute-done.5.v_ref
  32.8 0.0 copy-start
  32.8 2.4 %shard_map.75 = bf16[8,104,128]{2,1,0:T(8,128)(2,1)S(1)} custom-call(bf16[8,96,128]{2,1,0:T(8,128)(2,1)S(1)} %all-to-all-done.q_ref, bf16[2048,128]{1,0:T(8,128)(2,1)S(1)} %collective-permute-done.4.k_ref, bf16[2048,128]{1,0:T(8,128)(2,1)S(1)} %collective-permute-done.5.v_ref, f32[768,256]{1,0:T(8,128)S(1)} %get-tuple-element.24.o1_ref, ...), custom_call_target="tpu_custom_call" | custom-call | flops 805306368 | bytes 1048576 | tf_op jit(solution)/shard_map/pallas_call | solution.py:358
  35.1 15.9 %all_to_all.20.got_ref = bf16[8,104,128]{2,1,0:T(8,128)(2,1)S(1)} all-to-all(bf16[8,104,128]{2,1,0:T(8,128)(2,1)S(1)} %shard_map.75), channel_id=1, replica_groups=mesh['xh'=2,'z'=8,'core'=2,'xl'=2,'y'=4] {'z'}, dimensions={0} | all-to-all | bytes 425984 | tf_op jit(solution)/shard_map/all_to_all | solution.py:362
  51.0 0.4 combine.1
  51.4 17.7 %all_to_all.21.own_ref = bf16[16,96,128]{2,1,0:T(8,128)(2,1)S(1)} all-to-all(bf16[16,96,128]{2,1,0:T(8,128)(2,1)S(1)} %combine.1), channel_id=1, replica_groups=mesh['xh'=2,'z'=8,'core'=2,'xl'=2,'y'=4] {'xh','z'}, dimensions={0} | all-to-all | bytes 786432 | tf_op jit(solution)/shard_map/all_to_all | solution.py:372
  69.1 2.8 %collective-permute-start.6 = (bf16[16,96,128]{2,1,0:T(8,128)(2,1)S(1)}, bf16[16,96,128]{2,1,0:T(8,128)(2,1)S(1)}, u32[]{:S(2)}, u32[]{:S(2)}) collective-permute-start(bf16[16,96,128]{2,1,0:T(8,128)(2,1)S(1)} %all_to_all.21.own_ref), channel_id=1, source_target_pairs={{0,8},{8,0},{1,9},{9,1},{2,10},{10,2},{3,11},{11,3},{4,12},{12,4},... | collective-permute-start | bytes 1179656 | tf_op jit(solution)/shard_map/ppermute | solution.py:373
  71.9 1.3 %collective-permute-done.6.other_ref = bf16[16,96,128]{2,1,0:T(8,128)(2,1)S(1)} collective-permute-done((bf16[16,96,128]{2,1,0:T(8,128)(2,1)S(1)}, bf16[16,96,128]{2,1,0:T(8,128)(2,1)S(1)}, u32[]{:S(2)}, u32[]{:S(2)}) %collective-permute-start.6) | collective-permute-done | bytes 393248 | tf_op jit(solution)/shard_map/ppermute | solution.py:373
  73.3 0.0 copy-done
  73.3 0.8 project.1
  74.0 9.9 %all_to_all.22.parts_ref = bf16[8,3,8,512]{3,2,1,0:T(8,128)(2,1)S(1)} all-to-all(bf16[8,3,8,512]{3,2,1,0:T(8,128)(2,1)S(1)} %project.1), channel_id=1, replica_groups=mesh['xh'=2,'z'=8,'core'=2,'xl'=2,'y'=4] {'xl','y'}, dimensions={0} | all-to-all | bytes 393216 | tf_op jit(solution)/shard_map/all_to_all | solution.py:385
  84.0 0.6 total.1
Async XLA Ops:
  0.0 22.5 %collective-permute-start = (bf16[2048,128]{1,0:T(8,128)(2,1)}, bf16[2048,128]{1,0:T(8,128)(2,1)S(1)}, u32[]{:S(2)}, u32[]{:S(2)}) collective-permute-start(bf16[2048,128]{1,0:T(8,128)(2,1)} %bitcast.7), channel_id=1, source_target_pairs={{0,8},{8,0},{1,9},{9,1},{2,10},{10,2},{3,11},{11,3},{4,12},{12,4},... | collective-permute-start | bytes 1572872 | tf_op jit(solution)/shard_map/ppermute | solution.py:294
  3.2 19.3 %collective-permute-start.1 = (bf16[2048,128]{1,0:T(8,128)(2,1)}, bf16[2048,128]{1,0:T(8,128)(2,1)S(1)}, u32[]{:S(2)}, u32[]{:S(2)}) collective-permute-start(bf16[2048,128]{1,0:T(8,128)(2,1)} %bitcast.10), channel_id=1, source_target_pairs={{0,8},{8,0},{1,9},{9,1},{2,10},{10,2},{3,11},{11,3},{4,12},{12,4},... | collective-permute-start | bytes 1572872 | tf_op jit(solution)/shard_map/ppermute | solution.py:295
  3.2 24.0 %collective-permute-start.2 = (bf16[2048,128]{1,0:T(8,128)(2,1)}, bf16[2048,128]{1,0:T(8,128)(2,1)S(1)}, u32[]{:S(2)}, u32[]{:S(2)}) collective-permute-start(bf16[2048,128]{1,0:T(8,128)(2,1)} %bitcast.8), channel_id=1, source_target_pairs={{0,128},{128,0},{1,129},{129,1},{2,130},{130,2},{3,131},{131,3},{4... | collective-permute-start | bytes 1572872 | tf_op jit(solution)/shard_map/ppermute | solution.py:292
  4.2 24.9 %collective-permute-start.3 = (bf16[2048,128]{1,0:T(8,128)(2,1)}, bf16[2048,128]{1,0:T(8,128)(2,1)S(1)}, u32[]{:S(2)}, u32[]{:S(2)}) collective-permute-start(bf16[2048,128]{1,0:T(8,128)(2,1)} %bitcast.11), channel_id=1, source_target_pairs={{0,128},{128,0},{1,129},{129,1},{2,130},{130,2},{3,131},{131,3},{4... | collective-permute-start | bytes 1572872 | tf_op jit(solution)/shard_map/ppermute | solution.py:293
  7.6 14.9 %all-to-all-start = ((bf16[8,96,128]{2,1,0:T(8,128)(2,1)}), bf16[8,96,128]{2,1,0:T(8,128)(2,1)S(1)}, u32[]{:S(2)}, u32[]{:S(2)}) async-start(bf16[8,96,128]{2,1,0:T(8,128)(2,1)} %broadcast_in_dim.8), calls=%async_computation | async-start | bytes 393216 | tf_op jit(solution)/shard_map/all_to_all | solution.py:298
  14.1 1.0 %copy-start.1 = (bf16[2048,1,128]{2,0,1:T(8,128)(2,1)S(1)}, bf16[2048,1,128]{2,0,1:T(8,128)(2,1)}, u32[]{:S(2)}) copy-start(bf16[2048,1,128]{2,0,1:T(8,128)(2,1)} %param.8) | copy-start | bytes 1572868
  15.1 1.0 %copy-start.2 = (bf16[2048,1,128]{2,0,1:T(8,128)(2,1)S(1)}, bf16[2048,1,128]{2,0,1:T(8,128)(2,1)}, u32[]{:S(2)}) copy-start(bf16[2048,1,128]{2,0,1:T(8,128)(2,1)} %param.9) | copy-start | bytes 1572868
  16.2 0.9 %copy-start.3 = (bf16[2,512,1,128]{3,1,2,0:T(8,128)(2,1)S(1)}, bf16[2,512,1,128]{3,1,2,0:T(8,128)(2,1)}, u32[]{:S(2)}) copy-start(bf16[2,512,1,128]{3,1,2,0:T(8,128)(2,1)} %param.10) | copy-start | bytes 786436
  17.1 0.9 %copy-start.4 = (bf16[2,512,1,128]{3,1,2,0:T(8,128)(2,1)S(1)}, bf16[2,512,1,128]{3,1,2,0:T(8,128)(2,1)}, u32[]{:S(2)}) copy-start(bf16[2,512,1,128]{3,1,2,0:T(8,128)(2,1)} %param.11) | copy-start | bytes 786436
  18.1 0.7 copy-start.5
  18.8 0.7 copy-start.6
  29.1 3.6 %collective-permute-start.4 = (bf16[2048,128]{1,0:T(8,128)(2,1)S(1)}, bf16[2048,128]{1,0:T(8,128)(2,1)S(1)}, u32[]{:S(2)}, u32[]{:S(2)}) collective-permute-start(bf16[2048,128]{1,0:T(8,128)(2,1)S(1)} %collective-permute-done.2.k_ref), channel_id=1, source_target_pairs={{0,8},{8,0},{1,9},{9,1},{2,10},{10,2},{3,11},{11,3},{4,12},{12,4},... | collective-permute-start | bytes 1572872 | tf_op jit(solution)/shard_map/ppermute | solution.py:355
  30.5 2.3 %collective-permute-start.5 = (bf16[2048,128]{1,0:T(8,128)(2,1)S(1)}, bf16[2048,128]{1,0:T(8,128)(2,1)S(1)}, u32[]{:S(2)}, u32[]{:S(2)}) collective-permute-start(bf16[2048,128]{1,0:T(8,128)(2,1)S(1)} %collective-permute-done.3.v_ref), channel_id=1, source_target_pairs={{0,8},{8,0},{1,9},{9,1},{2,10},{10,2},{3,11},{11,3},{4,12},{12,4},... | collective-permute-start | bytes 1572872 | tf_op jit(solution)/shard_map/ppermute | solution.py:356
  32.8 40.5 %copy-start = (bf16[2048,512]{1,0:T(8,128)(2,1)S(1)}, bf16[2048,512]{1,0:T(8,128)(2,1)}, u32[]{:S(2)}) copy-start(bf16[2048,512]{1,0:T(8,128)(2,1)} %w_ref.1) | copy-start | bytes 6291460
  69.1 4.2 %collective-permute-start.6 = (bf16[16,96,128]{2,1,0:T(8,128)(2,1)S(1)}, bf16[16,96,128]{2,1,0:T(8,128)(2,1)S(1)}, u32[]{:S(2)}, u32[]{:S(2)}) collective-permute-start(bf16[16,96,128]{2,1,0:T(8,128)(2,1)S(1)} %all_to_all.21.own_ref), channel_id=1, source_target_pairs={{0,8},{8,0},{1,9},{9,1},{2,10},{10,2},{3,11},{11,3},{4,12},{12,4},... | collective-permute-start | bytes 1179656 | tf_op jit(solution)/shard_map/ppermute | solution.py:373

commit v5 on v4

--- a/solution.py
+++ b/solution.py
@@ -184,13 +184,16 @@
         out_ref[i, rows:, :] = turned[STATS * i : STATS * (i + 1)].astype(bf)
 
 
-def suffix_kernel(
-    c, heads, len_ref, q_ref, k_ref, v_ref, pk_ref, pv_ref, out_ref, k_out, v_out, sems
-):
-    get_k = pltpu.make_async_copy(pk_ref, k_out, sems.at[0])
-    get_v = pltpu.make_async_copy(pv_ref, v_out, sems.at[1])
+def hold_kernel(k_ref, v_ref, k_out, v_out, sems):
+    get_k = pltpu.make_async_copy(k_ref, k_out, sems.at[0])
+    get_v = pltpu.make_async_copy(v_ref, v_out, sems.at[1])
     get_k.start()
     get_v.start()
+    get_k.wait()
+    get_v.wait()
+
+
+def suffix_kernel(c, heads, len_ref, q_ref, k_ref, v_ref, out_ref):
     forks, slots, _ = k_ref.shape
     rows = q_ref.shape[0] // forks
     his, los, tots = [], [], []
@@ -210,8 +213,6 @@
         tots.append(jnp.sum(p, axis=1, keepdims=True))
     cat = functools.partial(jnp.concatenate, axis=0)
     out_ref[forks * rows :, :] = stat_rows(cat(his), cat(los), cat(tots))
-    get_k.wait()
-    get_v.wait()
 
 
 def combine_kernel(got_ref, own_ref, out_ref):
@@ -298,32 +299,18 @@
     every = lax.all_to_all(
         jnp.broadcast_to(q[None], (ring, rows, hd)), "z", 0, 0, tiled=True
     )
-    hbm = pl.BlockSpec(memory_space=pltpu.HBM)
-    own, k_held, v_held = pl.pallas_call(
-        functools.partial(suffix_kernel, c, heads),
-        out_shape=[
-            jax.ShapeDtypeStruct((rows + STATS, hd), bf),
-            jax.ShapeDtypeStruct((keys, hd), bf),
-            jax.ShapeDtypeStruct((keys, hd), bf),
-        ],
-        in_specs=[pl.BlockSpec(memory_space=pltpu.SMEM)] + whole(3) + [hbm, hbm],
-        out_specs=whole(3),
+    k_held, v_held = pl.pallas_call(
+        hold_kernel,
+        out_shape=[jax.ShapeDtypeStruct((keys, hd), bf)] * 2,
+        in_specs=[pl.BlockSpec(memory_space=pltpu.HBM)] * 2,
+        out_specs=whole(2),
         scratch_shapes=[pltpu.SemaphoreType.DMA((2,))],
         cost_estimate=pl.CostEstimate(
-            flops=4 * rows * slots * hd,
-            bytes_accessed=4 * forks * slots * hd,
-            transcendentals=rows * slots,
+            flops=0, bytes_accessed=8 * keys * hd, transcendentals=0
         ),
-        compiler_params=pltpu.CompilerParams(vmem_limit_bytes=6 * 2**20),
-        name="suffix",
-    )(
-        lengths,
-        q,
-        sk.reshape(forks, slots, hd),
-        sv.reshape(forks, slots, hd),
-        k_own,
-        v_own,
-    )
+        compiler_params=pltpu.CompilerParams(vmem_limit_bytes=2 * 2**20),
+        name="hold",
+    )(k_own, v_own)
 
     total = ring * rows
     f = jnp.float32
@@ -351,7 +338,21 @@
     o1, m1 = attend(near_kernel, 5, 2 * keys, False, 20)(
         every, k_held, k_pair, v_held, v_pair
     )
-    o1, m1, k_far, v_far = lax.optimization_barrier((o1, m1, k_far, v_far))
+    o1, m1, q_late = lax.optimization_barrier((o1, m1, q))
+    own = pl.pallas_call(
+        functools.partial(suffix_kernel, c, heads),
+        out_shape=jax.ShapeDtypeStruct((rows + STATS, hd), bf),
+        in_specs=[pl.BlockSpec(memory_space=pltpu.SMEM)] + whole(3),
+        out_specs=pl.BlockSpec(memory_space=VMEM),
+        cost_estimate=pl.CostEstimate(
+            flops=4 * rows * slots * hd,
+            bytes_accessed=4 * forks * slots * hd,
+            transcendentals=rows * slots,
+        ),
+        compiler_params=pltpu.CompilerParams(vmem_limit_bytes=4 * 2**20),
+        name="suffix",
+    )(lengths, q_late, sk.reshape(forks, slots, hd), sv.reshape(forks, slots, hd))
+    own, o1, m1, k_far, v_far = lax.optimization_barrier((own, o1, m1, k_far, v_far))
     k_far_pair = lax.ppermute(k_far, "core", swap)
     v_far_pair = lax.ppermute(v_far, "core", swap)
     o2, m2 = attend(next_kernel, 5, keys, False, 14)(every, k_far, v_far, o1, m1)

time: 85.2 us -> 84.6 us (level)
  local copies, waits for them, and re-layouts: 6.82 us -> 3.56 us
  waiting for transfers between devices: 4.9 us -> 8.06 us
  blocking collectives: 43.5 us -> 41.8 us
  starting transfers between devices: 16.8 us -> 18.1 us
    all_to_all x1, waiting for transfers between devices: 1.56 us -> 6.24 us  [body(): lax.all_to_all(jnp.broadcast_to(q[None], (ring, rows, hd)), 'z', 0, 0, ti...]
    unnamed x14, local copies, waits for them, and re-layouts: 5.37 us -> 2.11 us
    ppermute x1, waiting for transfers between devices: 1.92 us -> 0.45 us  [body(): v_far = lax.ppermute(v_own, 'xh', swap)]
    all_to_all x1, blocking collectives: 15.9 us -> 14.4 us  [body(): got = lax.all_to_all(states, 'z', 0, 0, tiled=True)]
    ppermute x1, starting transfers between devices: 1.37 us -> 2.61 us  [body(): k_far_pair = lax.ppermute(k_far, 'core', swap)]
where the time goes in v5:
time: 84.6 us; the launch traced here: 84.2 us
  blocking collectives  41.8 us (49%)
  starting transfers between devices  18.1 us (21%)
  Pallas kernels  12.5 us (15%)
  waiting for transfers between devices  8.06 us (10%)
  local copies, waits for them, and re-layouts  3.56 us (4%)
    all_to_all x1, blocking collectives, body(): att = lax.all_to_all(att, CHIPS, 0, 0, tiled=True)  17.6 us
    all_to_all x1, blocking collectives, body(): got = lax.all_to_all(states, 'z', 0, 0, tiled=True)  14.4 us
    all_to_all x1, blocking collectives, body(): parts = lax.all_to_all(product, TP, 0, 0, tiled=True)  9.8 us
    all_to_all x1, starting transfers between devices, body(): lax.all_to_all(jnp.broadcast_to(q[None], (ring, rows, hd)), 'z', 0, 0, ti...  6.48 us
    all_to_all x1, waiting for transfers between devices, body(): lax.all_to_all(jnp.broadcast_to(q[None], (ring, rows, hd)), 'z', 0, 0, ti...  6.24 us
    pallas_call x1, Pallas kernels, body(): attend(near_kernel, 5, 2 * keys, False, 20)  4.67 us
    ppermute x1, starting transfers between devices, body(): k_pair = lax.ppermute(k_own, 'core', swap)  3.2 us
    ppermute x1, starting transfers between devices, body(): other = lax.ppermute(att, 'core', swap)  2.75 us
  transfers between devices with their start and end apart: 8, of which 3 were waited for; matrix products, arithmetic and copies ran while one was open for 2% of the time, Pallas kernels for 10%

profile of v5, /device:TPU:1, one launch (start us, length us, event | category | flops | bytes accessed | tf_op | source)
XLA Modules:
  0.0 84.2 jit_solution(2842244278897453562)
XLA Ops:
  0.0 3.2 %collective-permute-start = (bf16[2048,128]{1,0:T(8,128)(2,1)}, bf16[2048,128]{1,0:T(8,128)(2,1)S(1)}, u32[]{:S(2)}, u32[]{:S(2)}) collective-permute-start(bf16[2048,128]{1,0:T(8,128)(2,1)} %bitcast.7), channel_id=1, source_target_pairs={{0,8},{8,0},{1,9},{9,1},{2,10},{10,2},{3,11},{11,3},{4,12},{12,4},... | collective-permute-start | bytes 1572872 | tf_op jit(solution)/shard_map/ppermute | solution.py:295
  3.2 0.0 collective-permute-start.1
  3.2 1.0 %collective-permute-start.2 = (bf16[2048,128]{1,0:T(8,128)(2,1)}, bf16[2048,128]{1,0:T(8,128)(2,1)S(1)}, u32[]{:S(2)}, u32[]{:S(2)}) collective-permute-start(bf16[2048,128]{1,0:T(8,128)(2,1)} %bitcast.8), channel_id=1, source_target_pairs={{0,128},{128,0},{1,129},{129,1},{2,130},{130,2},{3,131},{131,3},{4... | collective-permute-start | bytes 1572872 | tf_op jit(solution)/shard_map/ppermute | solution.py:293
  4.2 1.9 %collective-permute-start.3 = (bf16[2048,128]{1,0:T(8,128)(2,1)}, bf16[2048,128]{1,0:T(8,128)(2,1)S(1)}, u32[]{:S(2)}, u32[]{:S(2)}) collective-permute-start(bf16[2048,128]{1,0:T(8,128)(2,1)} %bitcast.11), channel_id=1, source_target_pairs={{0,128},{128,0},{1,129},{129,1},{2,130},{130,2},{3,131},{131,3},{4... | collective-permute-start | bytes 1572872 | tf_op jit(solution)/shard_map/ppermute | solution.py:294
  6.2 1.5 %broadcast_in_dim.8 = bf16[8,96,128]{2,1,0:T(8,128)(2,1)} broadcast(bf16[96,128]{1,0:T(8,128)(2,1)} %bitcast.15), dimensions={1,2} | broadcast | bytes 221184 | tf_op jit(solution)/shard_map/broadcast_in_dim | solution.py:300
  7.6 6.5 %all-to-all-start = ((bf16[8,96,128]{2,1,0:T(8,128)(2,1)}), bf16[8,96,128]{2,1,0:T(8,128)(2,1)S(1)}, u32[]{:S(2)}, u32[]{:S(2)}) async-start(bf16[8,96,128]{2,1,0:T(8,128)(2,1)} %broadcast_in_dim.8), calls=%async_computation | async-start | bytes 393216 | tf_op jit(solution)/shard_map/all_to_all | solution.py:299
  14.1 0.0 copy-start.1
  14.1 1.0 %copy-done.1 = bf16[2048,1,128]{2,0,1:T(8,128)(2,1)S(1)} copy-done((bf16[2048,1,128]{2,0,1:T(8,128)(2,1)S(1)}, bf16[2048,1,128]{2,0,1:T(8,128)(2,1)}, u32[]{:S(2)}) %copy-start.1) | copy-done | bytes 524312
  15.1 0.0 copy-start.2
  15.1 1.0 %copy-done.2 = bf16[2048,1,128]{2,0,1:T(8,128)(2,1)S(1)} copy-done((bf16[2048,1,128]{2,0,1:T(8,128)(2,1)S(1)}, bf16[2048,1,128]{2,0,1:T(8,128)(2,1)}, u32[]{:S(2)}) %copy-start.2) | copy-done | bytes 524312
  16.2 0.1 hold.1
  16.3 6.2 %all-to-all-done.q_ref = bf16[8,96,128]{2,1,0:T(8,128)(2,1)S(1)} async-done(((bf16[8,96,128]{2,1,0:T(8,128)(2,1)}), bf16[8,96,128]{2,1,0:T(8,128)(2,1)S(1)}, u32[]{:S(2)}, u32[]{:S(2)}) %all-to-all-start) | async-done | bytes 196640 | tf_op jit(solution)/shard_map/all_to_all | solution.py:299
  22.5 0.0 collective-permute-done.kp_ref
  22.5 0.0 collective-permute-done.1.vp_ref
  22.5 0.0 copy-start.3
  22.5 0.0 copy-start.4
  22.6 0.0 copy-start.5
  22.6 0.0 copy-start.6
  22.6 4.7 %shard_map.73 = (f32[768,256]{1,0:T(8,128)S(1)}, f32[768,128]{1,0:T(8,128)S(1)}) custom-call(bf16[8,96,128]{2,1,0:T(8,128)(2,1)S(1)} %all-to-all-done.q_ref, bf16[2048,128]{1,0:T(8,128)(2,1)S(1)} %get-tuple-element.19.ko_ref, bf16[2048,128]{1,0:T(8,128)(2,1)S(1)} %collective-permute-done.kp_ref, bf16[2048,128]{1,0:T(8,128)(2,1)S(1)} %get-tuple-element.20.vo_ref, ...), custom_call_target="tpu_custom_call" | custom-call | flops 1610612736 | bytes 2097152 | tf_op jit(solution)/shard_map/pallas_call | solution.py:338
  27.3 0.0 copy-done.3
  27.3 0.0 copy-done.4
  27.3 0.0 copy-done.5
  27.3 0.0 copy-done.6
  27.3 1.4 %suffix.1.own_ref = bf16[104,128]{1,0:T(8,128)(2,1)S(1)} custom-call(s32[2]{0:T(128)S(1)} %copy-done.6, bf16[96,128]{1,0:T(8,128)(2,1)S(1)} %bitcast.16, bf16[2,512,128]{2,1,0:T(8,128)(2,1)S(1)} %bitcast.13, bf16[2,512,128]{2,1,0:T(8,128)(2,1)S(1)} %bitcast.14), custom_call_target="tpu_custom_call" | custom-call | flops 25165824 | bytes 524288 | tf_op jit(solution)/shard_map/suffix/pallas_call | solution.py:342
  28.7 0.0 collective-permute-done.2.k_ref
  28.7 0.5 collective-permute-done.3.v_ref
  29.1 2.6 %collective-permute-start.4 = (bf16[2048,128]{1,0:T(8,128)(2,1)S(1)}, bf16[2048,128]{1,0:T(8,128)(2,1)S(1)}, u32[]{:S(2)}, u32[]{:S(2)}) collective-permute-start(bf16[2048,128]{1,0:T(8,128)(2,1)S(1)} %collective-permute-done.2.k_ref), channel_id=1, source_target_pairs={{0,8},{8,0},{1,9},{9,1},{2,10},{10,2},{3,11},{11,3},{4,12},{12,4},... | collective-permute-start | bytes 1572872 | tf_op jit(solution)/shard_map/ppermute | solution.py:356
  31.7 0.1 collective-permute-start.5
  31.8 2.2 %shard_map.74 = (f32[768,256]{1,0:T(8,128)S(1)}, f32[768,128]{1,0:T(8,128)S(1)}) custom-call(bf16[8,96,128]{2,1,0:T(8,128)(2,1)S(1)} %all-to-all-done.q_ref, bf16[2048,128]{1,0:T(8,128)(2,1)S(1)} %collective-permute-done.2.k_ref, bf16[2048,128]{1,0:T(8,128)(2,1)S(1)} %collective-permute-done.3.v_ref, f32[768,256]{1,0:T(8,128)S(1)} %get-tuple-element.28.o1_ref, ...), custom_call_target="tpu_custom_call" | custom-call | flops 805306368 | bytes 1048576 | tf_op jit(solution)/shard_map/pallas_call | solution.py:358
  34.1 0.0 collective-permute-done.4.k_ref
  34.1 0.0 collective-permute-done.5.v_ref
  34.1 0.0 copy-start
  34.1 2.4 %shard_map.75 = bf16[8,104,128]{2,1,0:T(8,128)(2,1)S(1)} custom-call(bf16[8,96,128]{2,1,0:T(8,128)(2,1)S(1)} %all-to-all-done.q_ref, bf16[2048,128]{1,0:T(8,128)(2,1)S(1)} %collective-permute-done.4.k_ref, bf16[2048,128]{1,0:T(8,128)(2,1)S(1)} %collective-permute-done.5.v_ref, f32[768,256]{1,0:T(8,128)S(1)} %get-tuple-element.30.o1_ref, ...), custom_call_target="tpu_custom_call" | custom-call | flops 805306368 | bytes 1048576 | tf_op jit(solution)/shard_map/pallas_call | solution.py:359
  36.5 14.4 %all_to_all.20.got_ref = bf16[8,104,128]{2,1,0:T(8,128)(2,1)S(1)} all-to-all(bf16[8,104,128]{2,1,0:T(8,128)(2,1)S(1)} %shard_map.75), channel_id=1, replica_groups=mesh['xh'=2,'z'=8,'core'=2,'xl'=2,'y'=4] {'z'}, dimensions={0} | all-to-all | bytes 425984 | tf_op jit(solution)/shard_map/all_to_all | solution.py:363
  50.9 0.4 combine.1
  51.3 17.6 %all_to_all.21.own_ref = bf16[16,96,128]{2,1,0:T(8,128)(2,1)S(1)} all-to-all(bf16[16,96,128]{2,1,0:T(8,128)(2,1)S(1)} %combine.1), channel_id=1, replica_groups=mesh['xh'=2,'z'=8,'core'=2,'xl'=2,'y'=4] {'xh','z'}, dimensions={0} | all-to-all | bytes 786432 | tf_op jit(solution)/shard_map/all_to_all | solution.py:373
  68.9 2.8 %collective-permute-start.6 = (bf16[16,96,128]{2,1,0:T(8,128)(2,1)S(1)}, bf16[16,96,128]{2,1,0:T(8,128)(2,1)S(1)}, u32[]{:S(2)}, u32[]{:S(2)}) collective-permute-start(bf16[16,96,128]{2,1,0:T(8,128)(2,1)S(1)} %all_to_all.21.own_ref), channel_id=1, source_target_pairs={{0,8},{8,0},{1,9},{9,1},{2,10},{10,2},{3,11},{11,3},{4,12},{12,4},... | collective-permute-start | bytes 1179656 | tf_op jit(solution)/shard_map/ppermute | solution.py:374
  71.6 1.3 %collective-permute-done.6.other_ref = bf16[16,96,128]{2,1,0:T(8,128)(2,1)S(1)} collective-permute-done((bf16[16,96,128]{2,1,0:T(8,128)(2,1)S(1)}, bf16[16,96,128]{2,1,0:T(8,128)(2,1)S(1)}, u32[]{:S(2)}, u32[]{:S(2)}) %collective-permute-start.6) | collective-permute-done | bytes 393248 | tf_op jit(solution)/shard_map/ppermute | solution.py:374
  73.0 0.0 copy-done
  73.0 0.8 project.1
  73.7 9.8 %all_to_all.22.parts_ref = bf16[8,3,8,512]{3,2,1,0:T(8,128)(2,1)S(1)} all-to-all(bf16[8,3,8,512]{3,2,1,0:T(8,128)(2,1)S(1)} %project.1), channel_id=1, replica_groups=mesh['xh'=2,'z'=8,'core'=2,'xl'=2,'y'=4] {'xl','y'}, dimensions={0} | all-to-all | bytes 393216 | tf_op jit(solution)/shard_map/all_to_all | solution.py:386
  83.5 0.6 total.1
Async XLA Ops:
  0.0 22.5 %collective-permute-start = (bf16[2048,128]{1,0:T(8,128)(2,1)}, bf16[2048,128]{1,0:T(8,128)(2,1)S(1)}, u32[]{:S(2)}, u32[]{:S(2)}) collective-permute-start(bf16[2048,128]{1,0:T(8,128)(2,1)} %bitcast.7), channel_id=1, source_target_pairs={{0,8},{8,0},{1,9},{9,1},{2,10},{10,2},{3,11},{11,3},{4,12},{12,4},... | collective-permute-start | bytes 1572872 | tf_op jit(solution)/shard_map/ppermute | solution.py:295
  3.2 19.3 %collective-permute-start.1 = (bf16[2048,128]{1,0:T(8,128)(2,1)}, bf16[2048,128]{1,0:T(8,128)(2,1)S(1)}, u32[]{:S(2)}, u32[]{:S(2)}) collective-permute-start(bf16[2048,128]{1,0:T(8,128)(2,1)} %bitcast.10), channel_id=1, source_target_pairs={{0,8},{8,0},{1,9},{9,1},{2,10},{10,2},{3,11},{11,3},{4,12},{12,4},... | collective-permute-start | bytes 1572872 | tf_op jit(solution)/shard_map/ppermute | solution.py:296
  3.2 25.5 %collective-permute-start.2 = (bf16[2048,128]{1,0:T(8,128)(2,1)}, bf16[2048,128]{1,0:T(8,128)(2,1)S(1)}, u32[]{:S(2)}, u32[]{:S(2)}) collective-permute-start(bf16[2048,128]{1,0:T(8,128)(2,1)} %bitcast.8), channel_id=1, source_target_pairs={{0,128},{128,0},{1,129},{129,1},{2,130},{130,2},{3,131},{131,3},{4... | collective-permute-start | bytes 1572872 | tf_op jit(solution)/shard_map/ppermute | solution.py:293
  4.2 24.9 %collective-permute-start.3 = (bf16[2048,128]{1,0:T(8,128)(2,1)}, bf16[2048,128]{1,0:T(8,128)(2,1)S(1)}, u32[]{:S(2)}, u32[]{:S(2)}) collective-permute-start(bf16[2048,128]{1,0:T(8,128)(2,1)} %bitcast.11), channel_id=1, source_target_pairs={{0,128},{128,0},{1,129},{129,1},{2,130},{130,2},{3,131},{131,3},{4... | collective-permute-start | bytes 1572872 | tf_op jit(solution)/shard_map/ppermute | solution.py:294
  7.6 14.9 %all-to-all-start = ((bf16[8,96,128]{2,1,0:T(8,128)(2,1)}), bf16[8,96,128]{2,1,0:T(8,128)(2,1)S(1)}, u32[]{:S(2)}, u32[]{:S(2)}) async-start(bf16[8,96,128]{2,1,0:T(8,128)(2,1)} %broadcast_in_dim.8), calls=%async_computation | async-start | bytes 393216 | tf_op jit(solution)/shard_map/all_to_all | solution.py:299
  14.1 1.0 %copy-start.1 = (bf16[2048,1,128]{2,0,1:T(8,128)(2,1)S(1)}, bf16[2048,1,128]{2,0,1:T(8,128)(2,1)}, u32[]{:S(2)}) copy-start(bf16[2048,1,128]{2,0,1:T(8,128)(2,1)} %param.8) | copy-start | bytes 1572868
  15.1 1.0 %copy-start.2 = (bf16[2048,1,128]{2,0,1:T(8,128)(2,1)S(1)}, bf16[2048,1,128]{2,0,1:T(8,128)(2,1)}, u32[]{:S(2)}) copy-start(bf16[2048,1,128]{2,0,1:T(8,128)(2,1)} %param.9) | copy-start | bytes 1572868
  22.5 4.7 %copy-start.3 = (bf16[2,512,1,128]{3,1,2,0:T(8,128)(2,1)S(1)}, bf16[2,512,1,128]{3,1,2,0:T(8,128)(2,1)}, u32[]{:S(2)}) copy-start(bf16[2,512,1,128]{3,1,2,0:T(8,128)(2,1)} %param.10) | copy-start | bytes 786436
  22.5 4.7 %copy-start.4 = (bf16[2,512,1,128]{3,1,2,0:T(8,128)(2,1)S(1)}, bf16[2,512,1,128]{3,1,2,0:T(8,128)(2,1)}, u32[]{:S(2)}) copy-start(bf16[2,512,1,128]{3,1,2,0:T(8,128)(2,1)} %param.11) | copy-start | bytes 786436
  22.6 4.7 %copy-start.5 = (bf16[2,3,16,128]{3,2,1,0:T(8,128)(2,1)S(1)}, bf16[2,3,16,128]{3,2,1,0:T(8,128)(2,1)}, u32[]{:S(2)}) copy-start(bf16[2,3,16,128]{3,2,1,0:T(8,128)(2,1)} %param.7) | copy-start | bytes 73732
  22.6 4.7 %copy-start.6 = (s32[2]{0:T(128)S(1)}, s32[2]{0:T(128)}, u32[]{:S(2)}) copy-start(s32[2]{0:T(128)} %len_ref.1) | copy-start | bytes 28
  29.1 5.0 %collective-permute-start.4 = (bf16[2048,128]{1,0:T(8,128)(2,1)S(1)}, bf16[2048,128]{1,0:T(8,128)(2,1)S(1)}, u32[]{:S(2)}, u32[]{:S(2)}) collective-permute-start(bf16[2048,128]{1,0:T(8,128)(2,1)S(1)} %collective-permute-done.2.k_ref), channel_id=1, source_target_pairs={{0,8},{8,0},{1,9},{9,1},{2,10},{10,2},{3,11},{11,3},{4,12},{12,4},... | collective-permute-start | bytes 1572872 | tf_op jit(solution)/shard_map/ppermute | solution.py:356
  31.7 2.4 %collective-permute-start.5 = (bf16[2048,128]{1,0:T(8,128)(2,1)S(1)}, bf16[2048,128]{1,0:T(8,128)(2,1)S(1)}, u32[]{:S(2)}, u32[]{:S(2)}) collective-permute-start(bf16[2048,128]{1,0:T(8,128)(2,1)S(1)} %collective-permute-done.3.v_ref), channel_id=1, source_target_pairs={{0,8},{8,0},{1,9},{9,1},{2,10},{10,2},{3,11},{11,3},{4,12},{12,4},... | collective-permute-start | bytes 1572872 | tf_op jit(solution)/shard_map/ppermute | solution.py:357
  34.1 38.9 %copy-start = (bf16[2048,512]{1,0:T(8,128)(2,1)S(1)}, bf16[2048,512]{1,0:T(8,128)(2,1)}, u32[]{:S(2)}) copy-start(bf16[2048,512]{1,0:T(8,128)(2,1)} %w_ref.1) | copy-start | bytes 6291460
  68.9 4.1 %collective-permute-start.6 = (bf16[16,96,128]{2,1,0:T(8,128)(2,1)S(1)}, bf16[16,96,128]{2,1,0:T(8,128)(2,1)S(1)}, u32[]{:S(2)}, u32[]{:S(2)}) collective-permute-start(bf16[16,96,128]{2,1,0:T(8,128)(2,1)S(1)} %all_to_all.21.own_ref), channel_id=1, source_target_pairs={{0,8},{8,0},{1,9},{9,1},{2,10},{10,2},{3,11},{11,3},{4,12},{12,4},... | collective-permute-start | bytes 1179656 | tf_op jit(solution)/shard_map/ppermute | solution.py:374

commit v6 on v5

--- a/solution.py
+++ b/solution.py
@@ -149,8 +149,7 @@
     return ref.at[:half], ref.at[half:]
 
 
-def next_kernel(c, q_ref, k_ref, v_ref, o1_ref, m1_ref, o_ref, m_ref, q2, s_o, s_p):
-    scaled_queries(c, q_ref, q2)
+def next_kernel(q2, k_ref, v_ref, o1_ref, m1_ref, o_ref, m_ref, s_o, s_p):
     m_ref[...] = m1_ref[...]
     score_pass(q2, halves(k_ref), (s_o, s_p), m_ref)
     mix_pass(halves(v_ref), (s_o, s_p), m_ref, o_ref)
@@ -159,11 +158,10 @@
 
 
 def far_kernel(
-    c, q_ref, k_ref, v_ref, o1_ref, m1_ref, out_ref, q2, s_o, s_p, m_ref, o_ref
+    q2, k_ref, v_ref, o1_ref, m1_ref, out_ref, s_o, s_p, m_ref, o_ref
 ):
-    n, rows, hd = q_ref.shape
+    n, rows, hd = out_ref.shape[0], out_ref.shape[1] - STATS, v_ref.shape[1]
     f, bf = jnp.float32, jnp.bfloat16
-    scaled_queries(c, q_ref, q2)
     m_ref[...] = m1_ref[...]
     score_pass(q2, halves(k_ref), (s_o, s_p), m_ref)
     mix_pass(halves(v_ref), (s_o, s_p), m_ref, o_ref)
@@ -315,14 +313,16 @@
     total = ring * rows
     f = jnp.float32
 
-    def attend(kernel, n_in, key_count, packed, limit):
+    def attend(kernel, n_in, key_count, kind, limit):
         state = [((total, TILE), f), ((total, 128), f)]
-        outs = [((ring, rows + STATS, hd), bf)] if packed else state
-        scratch = [((total, TILE), bf)] + [((total, key_count // 2), f)] * 2
-        if packed:
-            scratch += [state[1], state[0]]
+        scores = [((total, key_count // 2), f)] * 2
+        outs, scratch = {
+            "first": (state + [((total, TILE), bf)], scores),
+            "next": (state, scores),
+            "last": ([((ring, rows + STATS, hd), bf)], scores + state[::-1]),
+        }[kind]
         return pl.pallas_call(
-            functools.partial(kernel, c),
+            kernel,
             out_shape=[jax.ShapeDtypeStruct(*o) for o in outs],
             in_specs=whole(n_in),
             out_specs=whole(len(outs)),
@@ -335,7 +335,7 @@
             ),
         )
 
-    o1, m1 = attend(near_kernel, 5, 2 * keys, False, 20)(
+    o1, m1, q2 = attend(functools.partial(near_kernel, c), 5, 2 * keys, "first", 20)(
         every, k_held, k_pair, v_held, v_pair
     )
     o1, m1, q_late = lax.optimization_barrier((o1, m1, q))
@@ -355,9 +355,9 @@
     own, o1, m1, k_far, v_far = lax.optimization_barrier((own, o1, m1, k_far, v_far))
     k_far_pair = lax.ppermute(k_far, "core", swap)
     v_far_pair = lax.ppermute(v_far, "core", swap)
-    o2, m2 = attend(next_kernel, 5, keys, False, 14)(every, k_far, v_far, o1, m1)
-    (states,) = attend(far_kernel, 5, keys, True, 16)(
-        every, k_far_pair, v_far_pair, o2, m2
+    o2, m2 = attend(next_kernel, 5, keys, "next", 14)(q2, k_far, v_far, o1, m1)
+    (states,) = attend(far_kernel, 5, keys, "last", 16)(
+        q2, k_far_pair, v_far_pair, o2, m2
     )
 
     got = lax.all_to_all(states, "z", 0, 0, tiled=True)

time: 84.6 us -> 84.7 us (level)
  no operation moved by 1% of the time
where the time goes in v6:
time: 84.7 us; the launch traced here: 84.3 us
  blocking collectives  41.9 us (49%)
  starting transfers between devices  18.1 us (21%)
  Pallas kernels  12.5 us (15%)
  waiting for transfers between devices  8.06 us (10%)
  local copies, waits for them, and re-layouts  3.56 us (4%)
    all_to_all x1, blocking collectives, body(): att = lax.all_to_all(att, CHIPS, 0, 0, tiled=True)  17.5 us
    all_to_all x1, blocking collectives, body(): got = lax.all_to_all(states, 'z', 0, 0, tiled=True)  14.5 us
    all_to_all x1, blocking collectives, body(): parts = lax.all_to_all(product, TP, 0, 0, tiled=True)  9.91 us
    all_to_all x1, starting transfers between devices, body(): lax.all_to_all(jnp.broadcast_to(q[None], (ring, rows, hd)), 'z', 0, 0, ti...  6.48 us
    all_to_all x1, waiting for transfers between devices, body(): lax.all_to_all(jnp.broadcast_to(q[None], (ring, rows, hd)), 'z', 0, 0, ti...  6.24 us
    pallas_call x1, Pallas kernels, body(): attend(functools.partial(near_kernel, c), 5, 2 * keys, 'first', 20)  4.67 us
    ppermute x1, starting transfers between devices, body(): k_pair = lax.ppermute(k_own, 'core', swap)  3.2 us
    ppermute x1, starting transfers between devices, body(): other = lax.ppermute(att, 'core', swap)  2.75 us
  transfers between devices with their start and end apart: 8, of which 3 were waited for; matrix products, arithmetic and copies ran while one was open for 2% of the time, Pallas kernels for 10%

profile of v6, /device:TPU:1, one launch (start us, length us, event | category | flops | bytes accessed | tf_op | source)
XLA Modules:
  0.0 84.3 jit_solution(312814043298825806)
XLA Ops:
  0.0 3.2 %collective-permute-start = (bf16[2048,128]{1,0:T(8,128)(2,1)}, bf16[2048,128]{1,0:T(8,128)(2,1)S(1)}, u32[]{:S(2)}, u32[]{:S(2)}) collective-permute-start(bf16[2048,128]{1,0:T(8,128)(2,1)} %bitcast.7), channel_id=1, source_target_pairs={{0,8},{8,0},{1,9},{9,1},{2,10},{10,2},{3,11},{11,3},{4,12},{12,4},... | collective-permute-start | bytes 1572872 | tf_op jit(solution)/shard_map/ppermute | solution.py:293
  3.2 0.0 collective-permute-start.1
  3.2 1.0 %collective-permute-start.2 = (bf16[2048,128]{1,0:T(8,128)(2,1)}, bf16[2048,128]{1,0:T(8,128)(2,1)S(1)}, u32[]{:S(2)}, u32[]{:S(2)}) collective-permute-start(bf16[2048,128]{1,0:T(8,128)(2,1)} %bitcast.8), channel_id=1, source_target_pairs={{0,128},{128,0},{1,129},{129,1},{2,130},{130,2},{3,131},{131,3},{4... | collective-permute-start | bytes 1572872 | tf_op jit(solution)/shard_map/ppermute | solution.py:291
  4.2 1.9 %collective-permute-start.3 = (bf16[2048,128]{1,0:T(8,128)(2,1)}, bf16[2048,128]{1,0:T(8,128)(2,1)S(1)}, u32[]{:S(2)}, u32[]{:S(2)}) collective-permute-start(bf16[2048,128]{1,0:T(8,128)(2,1)} %bitcast.11), channel_id=1, source_target_pairs={{0,128},{128,0},{1,129},{129,1},{2,130},{130,2},{3,131},{131,3},{4... | collective-permute-start | bytes 1572872 | tf_op jit(solution)/shard_map/ppermute | solution.py:292
  6.2 1.5 %broadcast_in_dim.8 = bf16[8,96,128]{2,1,0:T(8,128)(2,1)} broadcast(bf16[96,128]{1,0:T(8,128)(2,1)} %bitcast.15), dimensions={1,2} | broadcast | bytes 221184 | tf_op jit(solution)/shard_map/broadcast_in_dim | solution.py:298
  7.6 6.5 %all-to-all-start = ((bf16[8,96,128]{2,1,0:T(8,128)(2,1)}), bf16[8,96,128]{2,1,0:T(8,128)(2,1)S(1)}, u32[]{:S(2)}, u32[]{:S(2)}) async-start(bf16[8,96,128]{2,1,0:T(8,128)(2,1)} %broadcast_in_dim.8), calls=%async_computation | async-start | bytes 393216 | tf_op jit(solution)/shard_map/all_to_all | solution.py:297
  14.1 0.0 copy-start.1
  14.1 1.0 %copy-done.1 = bf16[2048,1,128]{2,0,1:T(8,128)(2,1)S(1)} copy-done((bf16[2048,1,128]{2,0,1:T(8,128)(2,1)S(1)}, bf16[2048,1,128]{2,0,1:T(8,128)(2,1)}, u32[]{:S(2)}) %copy-start.1) | copy-done | bytes 524312
  15.1 0.0 copy-start.2
  15.1 1.0 %copy-done.2 = bf16[2048,1,128]{2,0,1:T(8,128)(2,1)S(1)} copy-done((bf16[2048,1,128]{2,0,1:T(8,128)(2,1)S(1)}, bf16[2048,1,128]{2,0,1:T(8,128)(2,1)}, u32[]{:S(2)}) %copy-start.2) | copy-done | bytes 524312
  16.2 0.1 hold.1
  16.3 6.2 %all-to-all-done.q_ref = bf16[8,96,128]{2,1,0:T(8,128)(2,1)S(1)} async-done(((bf16[8,96,128]{2,1,0:T(8,128)(2,1)}), bf16[8,96,128]{2,1,0:T(8,128)(2,1)S(1)}, u32[]{:S(2)}, u32[]{:S(2)}) %all-to-all-start) | async-done | bytes 196640 | tf_op jit(solution)/shard_map/all_to_all | solution.py:297
  22.5 0.0 collective-permute-done.kp_ref
  22.5 0.0 collective-permute-done.1.vp_ref
  22.5 0.0 copy-start.3
  22.5 0.0 copy-start.4
  22.6 0.0 copy-start.5
  22.6 0.0 copy-start.6
  22.6 4.7 %shard_map.73 = (f32[768,256]{1,0:T(8,128)S(1)}, f32[768,128]{1,0:T(8,128)S(1)}, bf16[768,256]{1,0:T(8,128)(2,1)S(1)}) custom-call(bf16[8,96,128]{2,1,0:T(8,128)(2,1)S(1)} %all-to-all-done.q_ref, bf16[2048,128]{1,0:T(8,128)(2,1)S(1)} %get-tuple-element.20.ko_ref, bf16[2048,128]{1,0:T(8,128)(2,1)S(1)} %collective-permute-done.kp_ref, ...), custom_call_target="tpu_custom_call" | custom-call | flops 1610612736 | bytes 2097152 | tf_op jit(solution)/shard_map/pallas_call | solution.py:338
  27.3 0.0 copy-done.3
  27.3 0.0 copy-done.4
  27.3 0.0 copy-done.5
  27.3 0.0 copy-done.6
  27.3 1.4 %suffix.1.own_ref = bf16[104,128]{1,0:T(8,128)(2,1)S(1)} custom-call(s32[2]{0:T(128)S(1)} %copy-done.6, bf16[96,128]{1,0:T(8,128)(2,1)S(1)} %bitcast.16, bf16[2,512,128]{2,1,0:T(8,128)(2,1)S(1)} %bitcast.13, bf16[2,512,128]{2,1,0:T(8,128)(2,1)S(1)} %bitcast.14), custom_call_target="tpu_custom_call" | custom-call | flops 25165824 | bytes 524288 | tf_op jit(solution)/shard_map/suffix/pallas_call | solution.py:342
  28.7 0.0 collective-permute-done.2.k_ref
  28.7 0.5 collective-permute-done.3.v_ref
  29.1 2.6 %collective-permute-start.4 = (bf16[2048,128]{1,0:T(8,128)(2,1)S(1)}, bf16[2048,128]{1,0:T(8,128)(2,1)S(1)}, u32[]{:S(2)}, u32[]{:S(2)}) collective-permute-start(bf16[2048,128]{1,0:T(8,128)(2,1)S(1)} %collective-permute-done.2.k_ref), channel_id=1, source_target_pairs={{0,8},{8,0},{1,9},{9,1},{2,10},{10,2},{3,11},{11,3},{4,12},{12,4},... | collective-permute-start | bytes 1572872 | tf_op jit(solution)/shard_map/ppermute | solution.py:356
  31.7 0.1 collective-permute-start.5
  31.8 2.2 %shard_map.74 = (f32[768,256]{1,0:T(8,128)S(1)}, f32[768,128]{1,0:T(8,128)S(1)}) custom-call(bf16[768,256]{1,0:T(8,128)(2,1)S(1)} %get-tuple-element.22.q2, bf16[2048,128]{1,0:T(8,128)(2,1)S(1)} %collective-permute-done.2.k_ref, bf16[2048,128]{1,0:T(8,128)(2,1)S(1)} %collective-permute-done.3.v_ref, f32[768,256]{1,0:T(8,128)S(1)} %get-tuple-element.30.o1_ref, ...), custom_call_target="tpu_custom_call" | custom-call | flops 805306368 | bytes 1048576 | tf_op jit(solution)/shard_map/pallas_call | solution.py:358
  34.1 0.0 collective-permute-done.4.k_ref
  34.1 0.0 collective-permute-done.5.v_ref
  34.1 0.0 copy-start
  34.1 2.4 %shard_map.75 = bf16[8,104,128]{2,1,0:T(8,128)(2,1)S(1)} custom-call(bf16[768,256]{1,0:T(8,128)(2,1)S(1)} %get-tuple-element.22.q2, bf16[2048,128]{1,0:T(8,128)(2,1)S(1)} %collective-permute-done.4.k_ref, bf16[2048,128]{1,0:T(8,128)(2,1)S(1)} %collective-permute-done.5.v_ref, f32[768,256]{1,0:T(8,128)S(1)} %get-tuple-element.32.o1_ref, ...), custom_call_target="tpu_custom_call" | custom-call | flops 805306368 | bytes 1048576 | tf_op jit(solution)/shard_map/pallas_call | solution.py:359
  36.5 14.5 %all_to_all.20.got_ref = bf16[8,104,128]{2,1,0:T(8,128)(2,1)S(1)} all-to-all(bf16[8,104,128]{2,1,0:T(8,128)(2,1)S(1)} %shard_map.75), channel_id=1, replica_groups=mesh['xh'=2,'z'=8,'core'=2,'xl'=2,'y'=4] {'z'}, dimensions={0} | all-to-all | bytes 425984 | tf_op jit(solution)/shard_map/all_to_all | solution.py:363
  51.0 0.4 combine.1
  51.4 17.5 %all_to_all.21.own_ref = bf16[16,96,128]{2,1,0:T(8,128)(2,1)S(1)} all-to-all(bf16[16,96,128]{2,1,0:T(8,128)(2,1)S(1)} %combine.1), channel_id=1, replica_groups=mesh['xh'=2,'z'=8,'core'=2,'xl'=2,'y'=4] {'xh','z'}, dimensions={0} | all-to-all | bytes 786432 | tf_op jit(solution)/shard_map/all_to_all | solution.py:373
  68.8 2.8 %collective-permute-start.6 = (bf16[16,96,128]{2,1,0:T(8,128)(2,1)S(1)}, bf16[16,96,128]{2,1,0:T(8,128)(2,1)S(1)}, u32[]{:S(2)}, u32[]{:S(2)}) collective-permute-start(bf16[16,96,128]{2,1,0:T(8,128)(2,1)S(1)} %all_to_all.21.own_ref), channel_id=1, source_target_pairs={{0,8},{8,0},{1,9},{9,1},{2,10},{10,2},{3,11},{11,3},{4,12},{12,4},... | collective-permute-start | bytes 1179656 | tf_op jit(solution)/shard_map/ppermute | solution.py:374
  71.6 1.3 %collective-permute-done.6.other_ref = bf16[16,96,128]{2,1,0:T(8,128)(2,1)S(1)} collective-permute-done((bf16[16,96,128]{2,1,0:T(8,128)(2,1)S(1)}, bf16[16,96,128]{2,1,0:T(8,128)(2,1)S(1)}, u32[]{:S(2)}, u32[]{:S(2)}) %collective-permute-start.6) | collective-permute-done | bytes 393248 | tf_op jit(solution)/shard_map/ppermute | solution.py:374
  73.0 0.0 copy-done
  73.0 0.8 project.1
  73.7 9.9 %all_to_all.22.parts_ref = bf16[8,3,8,512]{3,2,1,0:T(8,128)(2,1)S(1)} all-to-all(bf16[8,3,8,512]{3,2,1,0:T(8,128)(2,1)S(1)} %project.1), channel_id=1, replica_groups=mesh['xh'=2,'z'=8,'core'=2,'xl'=2,'y'=4] {'xl','y'}, dimensions={0} | all-to-all | bytes 393216 | tf_op jit(solution)/shard_map/all_to_all | solution.py:386
  83.6 0.6 total.1
Async XLA Ops:
  0.0 22.5 %collective-permute-start = (bf16[2048,128]{1,0:T(8,128)(2,1)}, bf16[2048,128]{1,0:T(8,128)(2,1)S(1)}, u32[]{:S(2)}, u32[]{:S(2)}) collective-permute-start(bf16[2048,128]{1,0:T(8,128)(2,1)} %bitcast.7), channel_id=1, source_target_pairs={{0,8},{8,0},{1,9},{9,1},{2,10},{10,2},{3,11},{11,3},{4,12},{12,4},... | collective-permute-start | bytes 1572872 | tf_op jit(solution)/shard_map/ppermute | solution.py:293
  3.2 19.3 %collective-permute-start.1 = (bf16[2048,128]{1,0:T(8,128)(2,1)}, bf16[2048,128]{1,0:T(8,128)(2,1)S(1)}, u32[]{:S(2)}, u32[]{:S(2)}) collective-permute-start(bf16[2048,128]{1,0:T(8,128)(2,1)} %bitcast.10), channel_id=1, source_target_pairs={{0,8},{8,0},{1,9},{9,1},{2,10},{10,2},{3,11},{11,3},{4,12},{12,4},... | collective-permute-start | bytes 1572872 | tf_op jit(solution)/shard_map/ppermute | solution.py:294
  3.2 25.5 %collective-permute-start.2 = (bf16[2048,128]{1,0:T(8,128)(2,1)}, bf16[2048,128]{1,0:T(8,128)(2,1)S(1)}, u32[]{:S(2)}, u32[]{:S(2)}) collective-permute-start(bf16[2048,128]{1,0:T(8,128)(2,1)} %bitcast.8), channel_id=1, source_target_pairs={{0,128},{128,0},{1,129},{129,1},{2,130},{130,2},{3,131},{131,3},{4... | collective-permute-start | bytes 1572872 | tf_op jit(solution)/shard_map/ppermute | solution.py:291
  4.2 24.9 %collective-permute-start.3 = (bf16[2048,128]{1,0:T(8,128)(2,1)}, bf16[2048,128]{1,0:T(8,128)(2,1)S(1)}, u32[]{:S(2)}, u32[]{:S(2)}) collective-permute-start(bf16[2048,128]{1,0:T(8,128)(2,1)} %bitcast.11), channel_id=1, source_target_pairs={{0,128},{128,0},{1,129},{129,1},{2,130},{130,2},{3,131},{131,3},{4... | collective-permute-start | bytes 1572872 | tf_op jit(solution)/shard_map/ppermute | solution.py:292
  7.6 14.9 %all-to-all-start = ((bf16[8,96,128]{2,1,0:T(8,128)(2,1)}), bf16[8,96,128]{2,1,0:T(8,128)(2,1)S(1)}, u32[]{:S(2)}, u32[]{:S(2)}) async-start(bf16[8,96,128]{2,1,0:T(8,128)(2,1)} %broadcast_in_dim.8), calls=%async_computation | async-start | bytes 393216 | tf_op jit(solution)/shard_map/all_to_all | solution.py:297
  14.1 1.0 %copy-start.1 = (bf16[2048,1,128]{2,0,1:T(8,128)(2,1)S(1)}, bf16[2048,1,128]{2,0,1:T(8,128)(2,1)}, u32[]{:S(2)}) copy-start(bf16[2048,1,128]{2,0,1:T(8,128)(2,1)} %param.8) | copy-start | bytes 1572868
  15.1 1.0 %copy-start.2 = (bf16[2048,1,128]{2,0,1:T(8,128)(2,1)S(1)}, bf16[2048,1,128]{2,0,1:T(8,128)(2,1)}, u32[]{:S(2)}) copy-start(bf16[2048,1,128]{2,0,1:T(8,128)(2,1)} %param.9) | copy-start | bytes 1572868
  22.5 4.7 %copy-start.3 = (bf16[2,512,1,128]{3,1,2,0:T(8,128)(2,1)S(1)}, bf16[2,512,1,128]{3,1,2,0:T(8,128)(2,1)}, u32[]{:S(2)}) copy-start(bf16[2,512,1,128]{3,1,2,0:T(8,128)(2,1)} %param.10) | copy-start | bytes 786436
  22.5 4.7 %copy-start.4 = (bf16[2,512,1,128]{3,1,2,0:T(8,128)(2,1)S(1)}, bf16[2,512,1,128]{3,1,2,0:T(8,128)(2,1)}, u32[]{:S(2)}) copy-start(bf16[2,512,1,128]{3,1,2,0:T(8,128)(2,1)} %param.11) | copy-start | bytes 786436
  22.6 4.7 %copy-start.5 = (bf16[2,3,16,128]{3,2,1,0:T(8,128)(2,1)S(1)}, bf16[2,3,16,128]{3,2,1,0:T(8,128)(2,1)}, u32[]{:S(2)}) copy-start(bf16[2,3,16,128]{3,2,1,0:T(8,128)(2,1)} %param.7) | copy-start | bytes 73732
  22.6 4.7 %copy-start.6 = (s32[2]{0:T(128)S(1)}, s32[2]{0:T(128)}, u32[]{:S(2)}) copy-start(s32[2]{0:T(128)} %len_ref.1) | copy-start | bytes 28
  29.1 5.0 %collective-permute-start.4 = (bf16[2048,128]{1,0:T(8,128)(2,1)S(1)}, bf16[2048,128]{1,0:T(8,128)(2,1)S(1)}, u32[]{:S(2)}, u32[]{:S(2)}) collective-permute-start(bf16[2048,128]{1,0:T(8,128)(2,1)S(1)} %collective-permute-done.2.k_ref), channel_id=1, source_target_pairs={{0,8},{8,0},{1,9},{9,1},{2,10},{10,2},{3,11},{11,3},{4,12},{12,4},... | collective-permute-start | bytes 1572872 | tf_op jit(solution)/shard_map/ppermute | solution.py:356
  31.7 2.3 %collective-permute-start.5 = (bf16[2048,128]{1,0:T(8,128)(2,1)S(1)}, bf16[2048,128]{1,0:T(8,128)(2,1)S(1)}, u32[]{:S(2)}, u32[]{:S(2)}) collective-permute-start(bf16[2048,128]{1,0:T(8,128)(2,1)S(1)} %collective-permute-done.3.v_ref), channel_id=1, source_target_pairs={{0,8},{8,0},{1,9},{9,1},{2,10},{10,2},{3,11},{11,3},{4,12},{12,4},... | collective-permute-start | bytes 1572872 | tf_op jit(solution)/shard_map/ppermute | solution.py:357
  34.1 38.9 %copy-start = (bf16[2048,512]{1,0:T(8,128)(2,1)S(1)}, bf16[2048,512]{1,0:T(8,128)(2,1)}, u32[]{:S(2)}) copy-start(bf16[2048,512]{1,0:T(8,128)(2,1)} %w_ref.1) | copy-start | bytes 6291460
  68.8 4.1 %collective-permute-start.6 = (bf16[16,96,128]{2,1,0:T(8,128)(2,1)S(1)}, bf16[16,96,128]{2,1,0:T(8,128)(2,1)S(1)}, u32[]{:S(2)}, u32[]{:S(2)}) collective-permute-start(bf16[16,96,128]{2,1,0:T(8,128)(2,1)S(1)} %all_to_all.21.own_ref), channel_id=1, source_target_pairs={{0,8},{8,0},{1,9},{9,1},{2,10},{10,2},{3,11},{11,3},{4,12},{12,4},... | collective-permute-start | bytes 1179656 | tf_op jit(solution)/shard_map/ppermute | solution.py:374

commit v7 on v6

--- a/solution.py
+++ b/solution.py
@@ -246,20 +246,17 @@
     x4[:, core] = own_ref[...].astype(jnp.float32)
     x4[:, 1 - core] = other_ref[...].astype(jnp.float32)
     forks = n * 2 * rows // heads // steps
-    acc = jnp.zeros((steps * forks, w_ref.shape[1]), jnp.float32)
-    for h in range(0, heads, 2):
-        pair = [
-            jnp.concatenate(
-                [
-                    x_ref[pl.ds(s * heads + h + j, forks, stride=steps * heads), :]
-                    for s in range(steps)
-                ],
-                axis=0,
-            ).astype(jnp.bfloat16)
-            for j in range(2)
-        ]
-        lhs = jnp.concatenate(pair, axis=1)
-        acc = acc + dot(lhs, w_ref[h * hd : (h + 2) * hd, :], 1, 0)
+    lhs = [
+        jnp.concatenate(
+            [
+                x_ref[pl.ds(s * heads + h, forks, stride=steps * heads), :]
+                for s in range(steps)
+            ],
+            axis=0,
+        ).astype(jnp.bfloat16)
+        for h in range(heads)
+    ]
+    acc = dot(jnp.concatenate(lhs, axis=1), w_ref[...], 1, 0)
     tps = out_ref.shape[0]
     mine = forks // tps
     for s in range(steps):

time: 84.7 us -> 84.7 us (level)
  no operation moved by 1% of the time
where the time goes in v7:
time: 84.7 us; the launch traced here: 84.3 us
  blocking collectives  41.9 us (49%)
  starting transfers between devices  18.1 us (21%)
  Pallas kernels  12.5 us (15%)
  waiting for transfers between devices  8.06 us (10%)
  local copies, waits for them, and re-layouts  3.56 us (4%)
    all_to_all x1, blocking collectives, body(): att = lax.all_to_all(att, CHIPS, 0, 0, tiled=True)  17.5 us
    all_to_all x1, blocking collectives, body(): got = lax.all_to_all(states, 'z', 0, 0, tiled=True)  14.5 us
    all_to_all x1, blocking collectives, body(): parts = lax.all_to_all(product, TP, 0, 0, tiled=True)  9.91 us
    all_to_all x1, starting transfers between devices, body(): lax.all_to_all(jnp.broadcast_to(q[None], (ring, rows, hd)), 'z', 0, 0, ti...  6.48 us
    all_to_all x1, waiting for transfers between devices, body(): lax.all_to_all(jnp.broadcast_to(q[None], (ring, rows, hd)), 'z', 0, 0, ti...  6.24 us
    pallas_call x1, Pallas kernels, body(): attend(functools.partial(near_kernel, c), 5, 2 * keys, 'first', 20)  4.67 us
    ppermute x1, starting transfers between devices, body(): k_pair = lax.ppermute(k_own, 'core', swap)  3.2 us
    ppermute x1, starting transfers between devices, body(): other = lax.ppermute(att, 'core', swap)  2.75 us
  transfers between devices with their start and end apart: 8, of which 3 were waited for; matrix products, arithmetic and copies ran while one was open for 2% of the time, Pallas kernels for 10%

profile of v7, /device:TPU:1, one launch (start us, length us, event | category | flops | bytes accessed | tf_op | source)
XLA Modules:
  0.0 84.3 jit_solution(5927562360736365678)
XLA Ops:
  0.0 3.2 %collective-permute-start = (bf16[2048,128]{1,0:T(8,128)(2,1)}, bf16[2048,128]{1,0:T(8,128)(2,1)S(1)}, u32[]{:S(2)}, u32[]{:S(2)}) collective-permute-start(bf16[2048,128]{1,0:T(8,128)(2,1)} %bitcast.7), channel_id=1, source_target_pairs={{0,8},{8,0},{1,9},{9,1},{2,10},{10,2},{3,11},{11,3},{4,12},{12,4},... | collective-permute-start | bytes 1572872 | tf_op jit(solution)/shard_map/ppermute | solution.py:290
  3.2 0.0 collective-permute-start.1
  3.2 1.0 %collective-permute-start.2 = (bf16[2048,128]{1,0:T(8,128)(2,1)}, bf16[2048,128]{1,0:T(8,128)(2,1)S(1)}, u32[]{:S(2)}, u32[]{:S(2)}) collective-permute-start(bf16[2048,128]{1,0:T(8,128)(2,1)} %bitcast.8), channel_id=1, source_target_pairs={{0,128},{128,0},{1,129},{129,1},{2,130},{130,2},{3,131},{131,3},{4... | collective-permute-start | bytes 1572872 | tf_op jit(solution)/shard_map/ppermute | solution.py:288
  4.2 1.9 %collective-permute-start.3 = (bf16[2048,128]{1,0:T(8,128)(2,1)}, bf16[2048,128]{1,0:T(8,128)(2,1)S(1)}, u32[]{:S(2)}, u32[]{:S(2)}) collective-permute-start(bf16[2048,128]{1,0:T(8,128)(2,1)} %bitcast.11), channel_id=1, source_target_pairs={{0,128},{128,0},{1,129},{129,1},{2,130},{130,2},{3,131},{131,3},{4... | collective-permute-start | bytes 1572872 | tf_op jit(solution)/shard_map/ppermute | solution.py:289
  6.2 1.5 %broadcast_in_dim.8 = bf16[8,96,128]{2,1,0:T(8,128)(2,1)} broadcast(bf16[96,128]{1,0:T(8,128)(2,1)} %bitcast.15), dimensions={1,2} | broadcast | bytes 221184 | tf_op jit(solution)/shard_map/broadcast_in_dim | solution.py:295
  7.6 6.5 %all-to-all-start = ((bf16[8,96,128]{2,1,0:T(8,128)(2,1)}), bf16[8,96,128]{2,1,0:T(8,128)(2,1)S(1)}, u32[]{:S(2)}, u32[]{:S(2)}) async-start(bf16[8,96,128]{2,1,0:T(8,128)(2,1)} %broadcast_in_dim.8), calls=%async_computation | async-start | bytes 393216 | tf_op jit(solution)/shard_map/all_to_all | solution.py:294
  14.1 0.0 copy-start.1
  14.1 1.0 %copy-done.1 = bf16[2048,1,128]{2,0,1:T(8,128)(2,1)S(1)} copy-done((bf16[2048,1,128]{2,0,1:T(8,128)(2,1)S(1)}, bf16[2048,1,128]{2,0,1:T(8,128)(2,1)}, u32[]{:S(2)}) %copy-start.1) | copy-done | bytes 524312
  15.1 0.0 copy-start.2
  15.1 1.0 %copy-done.2 = bf16[2048,1,128]{2,0,1:T(8,128)(2,1)S(1)} copy-done((bf16[2048,1,128]{2,0,1:T(8,128)(2,1)S(1)}, bf16[2048,1,128]{2,0,1:T(8,128)(2,1)}, u32[]{:S(2)}) %copy-start.2) | copy-done | bytes 524312
  16.2 0.1 hold.1
  16.3 6.2 %all-to-all-done.q_ref = bf16[8,96,128]{2,1,0:T(8,128)(2,1)S(1)} async-done(((bf16[8,96,128]{2,1,0:T(8,128)(2,1)}), bf16[8,96,128]{2,1,0:T(8,128)(2,1)S(1)}, u32[]{:S(2)}, u32[]{:S(2)}) %all-to-all-start) | async-done | bytes 196640 | tf_op jit(solution)/shard_map/all_to_all | solution.py:294
  22.5 0.0 collective-permute-done.kp_ref
  22.5 0.0 collective-permute-done.1.vp_ref
  22.5 0.0 copy-start.3
  22.5 0.0 copy-start.4
  22.6 0.0 copy-start.5
  22.6 0.0 copy-start.6
  22.6 4.7 %shard_map.73 = (f32[768,256]{1,0:T(8,128)S(1)}, f32[768,128]{1,0:T(8,128)S(1)}, bf16[768,256]{1,0:T(8,128)(2,1)S(1)}) custom-call(bf16[8,96,128]{2,1,0:T(8,128)(2,1)S(1)} %all-to-all-done.q_ref, bf16[2048,128]{1,0:T(8,128)(2,1)S(1)} %get-tuple-element.20.ko_ref, bf16[2048,128]{1,0:T(8,128)(2,1)S(1)} %collective-permute-done.kp_ref, ...), custom_call_target="tpu_custom_call" | custom-call | flops 1610612736 | bytes 2097152 | tf_op jit(solution)/shard_map/pallas_call | solution.py:335
  27.3 0.0 copy-done.3
  27.3 0.0 copy-done.4
  27.3 0.0 copy-done.5
  27.3 0.0 copy-done.6
  27.3 1.4 %suffix.1.own_ref = bf16[104,128]{1,0:T(8,128)(2,1)S(1)} custom-call(s32[2]{0:T(128)S(1)} %copy-done.6, bf16[96,128]{1,0:T(8,128)(2,1)S(1)} %bitcast.16, bf16[2,512,128]{2,1,0:T(8,128)(2,1)S(1)} %bitcast.13, bf16[2,512,128]{2,1,0:T(8,128)(2,1)S(1)} %bitcast.14), custom_call_target="tpu_custom_call" | custom-call | flops 25165824 | bytes 524288 | tf_op jit(solution)/shard_map/suffix/pallas_call | solution.py:339
  28.7 0.0 collective-permute-done.2.k_ref
  28.7 0.5 collective-permute-done.3.v_ref
  29.1 2.6 %collective-permute-start.4 = (bf16[2048,128]{1,0:T(8,128)(2,1)S(1)}, bf16[2048,128]{1,0:T(8,128)(2,1)S(1)}, u32[]{:S(2)}, u32[]{:S(2)}) collective-permute-start(bf16[2048,128]{1,0:T(8,128)(2,1)S(1)} %collective-permute-done.2.k_ref), channel_id=1, source_target_pairs={{0,8},{8,0},{1,9},{9,1},{2,10},{10,2},{3,11},{11,3},{4,12},{12,4},... | collective-permute-start | bytes 1572872 | tf_op jit(solution)/shard_map/ppermute | solution.py:353
  31.7 0.1 collective-permute-start.5
  31.8 2.2 %shard_map.74 = (f32[768,256]{1,0:T(8,128)S(1)}, f32[768,128]{1,0:T(8,128)S(1)}) custom-call(bf16[768,256]{1,0:T(8,128)(2,1)S(1)} %get-tuple-element.22.q2, bf16[2048,128]{1,0:T(8,128)(2,1)S(1)} %collective-permute-done.2.k_ref, bf16[2048,128]{1,0:T(8,128)(2,1)S(1)} %collective-permute-done.3.v_ref, f32[768,256]{1,0:T(8,128)S(1)} %get-tuple-element.30.o1_ref, ...), custom_call_target="tpu_custom_call" | custom-call | flops 805306368 | bytes 1048576 | tf_op jit(solution)/shard_map/pallas_call | solution.py:355
  34.1 0.0 collective-permute-done.4.k_ref
  34.1 0.0 collective-permute-done.5.v_ref
  34.1 0.0 copy-start
  34.1 2.4 %shard_map.75 = bf16[8,104,128]{2,1,0:T(8,128)(2,1)S(1)} custom-call(bf16[768,256]{1,0:T(8,128)(2,1)S(1)} %get-tuple-element.22.q2, bf16[2048,128]{1,0:T(8,128)(2,1)S(1)} %collective-permute-done.4.k_ref, bf16[2048,128]{1,0:T(8,128)(2,1)S(1)} %collective-permute-done.5.v_ref, f32[768,256]{1,0:T(8,128)S(1)} %get-tuple-element.32.o1_ref, ...), custom_call_target="tpu_custom_call" | custom-call | flops 805306368 | bytes 1048576 | tf_op jit(solution)/shard_map/pallas_call | solution.py:356
  36.5 14.5 %all_to_all.20.got_ref = bf16[8,104,128]{2,1,0:T(8,128)(2,1)S(1)} all-to-all(bf16[8,104,128]{2,1,0:T(8,128)(2,1)S(1)} %shard_map.75), channel_id=1, replica_groups=mesh['xh'=2,'z'=8,'core'=2,'xl'=2,'y'=4] {'z'}, dimensions={0} | all-to-all | bytes 425984 | tf_op jit(solution)/shard_map/all_to_all | solution.py:360
  51.0 0.4 combine.1
  51.4 17.5 %all_to_all.21.own_ref = bf16[16,96,128]{2,1,0:T(8,128)(2,1)S(1)} all-to-all(bf16[16,96,128]{2,1,0:T(8,128)(2,1)S(1)} %combine.1), channel_id=1, replica_groups=mesh['xh'=2,'z'=8,'core'=2,'xl'=2,'y'=4] {'xh','z'}, dimensions={0} | all-to-all | bytes 786432 | tf_op jit(solution)/shard_map/all_to_all | solution.py:370
  68.8 2.8 %collective-permute-start.6 = (bf16[16,96,128]{2,1,0:T(8,128)(2,1)S(1)}, bf16[16,96,128]{2,1,0:T(8,128)(2,1)S(1)}, u32[]{:S(2)}, u32[]{:S(2)}) collective-permute-start(bf16[16,96,128]{2,1,0:T(8,128)(2,1)S(1)} %all_to_all.21.own_ref), channel_id=1, source_target_pairs={{0,8},{8,0},{1,9},{9,1},{2,10},{10,2},{3,11},{11,3},{4,12},{12,4},... | collective-permute-start | bytes 1179656 | tf_op jit(solution)/shard_map/ppermute | solution.py:371
  71.6 1.3 %collective-permute-done.6.other_ref = bf16[16,96,128]{2,1,0:T(8,128)(2,1)S(1)} collective-permute-done((bf16[16,96,128]{2,1,0:T(8,128)(2,1)S(1)}, bf16[16,96,128]{2,1,0:T(8,128)(2,1)S(1)}, u32[]{:S(2)}, u32[]{:S(2)}) %collective-permute-start.6) | collective-permute-done | bytes 393248 | tf_op jit(solution)/shard_map/ppermute | solution.py:371
  73.0 0.0 copy-done
  73.0 0.8 project.1
  73.7 9.9 %all_to_all.22.parts_ref = bf16[8,3,8,512]{3,2,1,0:T(8,128)(2,1)S(1)} all-to-all(bf16[8,3,8,512]{3,2,1,0:T(8,128)(2,1)S(1)} %project.1), channel_id=1, replica_groups=mesh['xh'=2,'z'=8,'core'=2,'xl'=2,'y'=4] {'xl','y'}, dimensions={0} | all-to-all | bytes 393216 | tf_op jit(solution)/shard_map/all_to_all | solution.py:383
  83.6 0.6 total.1
Async XLA Ops:
  0.0 22.5 %collective-permute-start = (bf16[2048,128]{1,0:T(8,128)(2,1)}, bf16[2048,128]{1,0:T(8,128)(2,1)S(1)}, u32[]{:S(2)}, u32[]{:S(2)}) collective-permute-start(bf16[2048,128]{1,0:T(8,128)(2,1)} %bitcast.7), channel_id=1, source_target_pairs={{0,8},{8,0},{1,9},{9,1},{2,10},{10,2},{3,11},{11,3},{4,12},{12,4},... | collective-permute-start | bytes 1572872 | tf_op jit(solution)/shard_map/ppermute | solution.py:290
  3.2 19.3 %collective-permute-start.1 = (bf16[2048,128]{1,0:T(8,128)(2,1)}, bf16[2048,128]{1,0:T(8,128)(2,1)S(1)}, u32[]{:S(2)}, u32[]{:S(2)}) collective-permute-start(bf16[2048,128]{1,0:T(8,128)(2,1)} %bitcast.10), channel_id=1, source_target_pairs={{0,8},{8,0},{1,9},{9,1},{2,10},{10,2},{3,11},{11,3},{4,12},{12,4},... | collective-permute-start | bytes 1572872 | tf_op jit(solution)/shard_map/ppermute | solution.py:291
  3.2 25.5 %collective-permute-start.2 = (bf16[2048,128]{1,0:T(8,128)(2,1)}, bf16[2048,128]{1,0:T(8,128)(2,1)S(1)}, u32[]{:S(2)}, u32[]{:S(2)}) collective-permute-start(bf16[2048,128]{1,0:T(8,128)(2,1)} %bitcast.8), channel_id=1, source_target_pairs={{0,128},{128,0},{1,129},{129,1},{2,130},{130,2},{3,131},{131,3},{4... | collective-permute-start | bytes 1572872 | tf_op jit(solution)/shard_map/ppermute | solution.py:288
  4.2 24.9 %collective-permute-start.3 = (bf16[2048,128]{1,0:T(8,128)(2,1)}, bf16[2048,128]{1,0:T(8,128)(2,1)S(1)}, u32[]{:S(2)}, u32[]{:S(2)}) collective-permute-start(bf16[2048,128]{1,0:T(8,128)(2,1)} %bitcast.11), channel_id=1, source_target_pairs={{0,128},{128,0},{1,129},{129,1},{2,130},{130,2},{3,131},{131,3},{4... | collective-permute-start | bytes 1572872 | tf_op jit(solution)/shard_map/ppermute | solution.py:289
  7.6 14.9 %all-to-all-start = ((bf16[8,96,128]{2,1,0:T(8,128)(2,1)}), bf16[8,96,128]{2,1,0:T(8,128)(2,1)S(1)}, u32[]{:S(2)}, u32[]{:S(2)}) async-start(bf16[8,96,128]{2,1,0:T(8,128)(2,1)} %broadcast_in_dim.8), calls=%async_computation | async-start | bytes 393216 | tf_op jit(solution)/shard_map/all_to_all | solution.py:294
  14.1 1.0 %copy-start.1 = (bf16[2048,1,128]{2,0,1:T(8,128)(2,1)S(1)}, bf16[2048,1,128]{2,0,1:T(8,128)(2,1)}, u32[]{:S(2)}) copy-start(bf16[2048,1,128]{2,0,1:T(8,128)(2,1)} %param.8) | copy-start | bytes 1572868
  15.1 1.0 %copy-start.2 = (bf16[2048,1,128]{2,0,1:T(8,128)(2,1)S(1)}, bf16[2048,1,128]{2,0,1:T(8,128)(2,1)}, u32[]{:S(2)}) copy-start(bf16[2048,1,128]{2,0,1:T(8,128)(2,1)} %param.9) | copy-start | bytes 1572868
  22.5 4.7 %copy-start.3 = (bf16[2,512,1,128]{3,1,2,0:T(8,128)(2,1)S(1)}, bf16[2,512,1,128]{3,1,2,0:T(8,128)(2,1)}, u32[]{:S(2)}) copy-start(bf16[2,512,1,128]{3,1,2,0:T(8,128)(2,1)} %param.10) | copy-start | bytes 786436
  22.5 4.7 %copy-start.4 = (bf16[2,512,1,128]{3,1,2,0:T(8,128)(2,1)S(1)}, bf16[2,512,1,128]{3,1,2,0:T(8,128)(2,1)}, u32[]{:S(2)}) copy-start(bf16[2,512,1,128]{3,1,2,0:T(8,128)(2,1)} %param.11) | copy-start | bytes 786436
  22.6 4.7 %copy-start.5 = (bf16[2,3,16,128]{3,2,1,0:T(8,128)(2,1)S(1)}, bf16[2,3,16,128]{3,2,1,0:T(8,128)(2,1)}, u32[]{:S(2)}) copy-start(bf16[2,3,16,128]{3,2,1,0:T(8,128)(2,1)} %param.7) | copy-start | bytes 73732
  22.6 4.7 %copy-start.6 = (s32[2]{0:T(128)S(1)}, s32[2]{0:T(128)}, u32[]{:S(2)}) copy-start(s32[2]{0:T(128)} %len_ref.1) | copy-start | bytes 28
  29.1 5.0 %collective-permute-start.4 = (bf16[2048,128]{1,0:T(8,128)(2,1)S(1)}, bf16[2048,128]{1,0:T(8,128)(2,1)S(1)}, u32[]{:S(2)}, u32[]{:S(2)}) collective-permute-start(bf16[2048,128]{1,0:T(8,128)(2,1)S(1)} %collective-permute-done.2.k_ref), channel_id=1, source_target_pairs={{0,8},{8,0},{1,9},{9,1},{2,10},{10,2},{3,11},{11,3},{4,12},{12,4},... | collective-permute-start | bytes 1572872 | tf_op jit(solution)/shard_map/ppermute | solution.py:353
  31.7 2.3 %collective-permute-start.5 = (bf16[2048,128]{1,0:T(8,128)(2,1)S(1)}, bf16[2048,128]{1,0:T(8,128)(2,1)S(1)}, u32[]{:S(2)}, u32[]{:S(2)}) collective-permute-start(bf16[2048,128]{1,0:T(8,128)(2,1)S(1)} %collective-permute-done.3.v_ref), channel_id=1, source_target_pairs={{0,8},{8,0},{1,9},{9,1},{2,10},{10,2},{3,11},{11,3},{4,12},{12,4},... | collective-permute-start | bytes 1572872 | tf_op jit(solution)/shard_map/ppermute | solution.py:354
  34.1 38.9 %copy-start = (bf16[2048,512]{1,0:T(8,128)(2,1)S(1)}, bf16[2048,512]{1,0:T(8,128)(2,1)}, u32[]{:S(2)}) copy-start(bf16[2048,512]{1,0:T(8,128)(2,1)} %w_ref.1) | copy-start | bytes 6291460
  68.8 4.1 %collective-permute-start.6 = (bf16[16,96,128]{2,1,0:T(8,128)(2,1)S(1)}, bf16[16,96,128]{2,1,0:T(8,128)(2,1)S(1)}, u32[]{:S(2)}, u32[]{:S(2)}) collective-permute-start(bf16[16,96,128]{2,1,0:T(8,128)(2,1)S(1)} %all_to_all.21.own_ref), channel_id=1, source_target_pairs={{0,8},{8,0},{1,9},{9,1},{2,10},{10,2},{3,11},{11,3},{4,12},{12,4},... | collective-permute-start | bytes 1179656 | tf_op jit(solution)/shard_map/ppermute | solution.py:371
